TPU v7x, 32 devices: a whole 2x2x4 slice. The times are simulated.
32 devices in a mesh: dp: 8 (over y, x, core), tensor: 4 (over z).
Axes of the slice: x: 2, y: 2, z: 4, core: 2. Of those that a mesh axis runs over, the one named last changes fastest.
Arguments:
- tokens: bfloat16 [2, 8192, 1024], P(None, ('dp', 'tensor')), may hold values from -6 to 6
- attn_gain: float32 [1024], replicated, may hold values from 0.25 to 1.75
- ffn_gain: float32 [1024], replicated, may hold values from 0.25 to 1.75
- query_weight: bfloat16 [1024, 1024], P(None, 'tensor'), may hold values from -0.1875 to 0.1875
- key_weight: bfloat16 [1024, 1024], P(None, 'tensor'), may hold values from -0.1875 to 0.1875
- value_weight: bfloat16 [1024, 1024], P(None, 'tensor'), may hold values from -0.1875 to 0.1875
- out_weight: bfloat16 [1024, 1024], P('tensor'), may hold values from -1 to 1
- gate_weight: bfloat16 [1024, 2816], P(None, 'tensor'), may hold values from -0.1875 to 0.1875
- up_weight: bfloat16 [1024, 2816], P(None, 'tensor'), may hold values from -0.1875 to 0.1875
- down_weight: bfloat16 [2816, 1024], P('tensor'), may hold values from -0.109375 to 0.109375
- cache_keys: bfloat16 [2, 2048, 1024], P(None, 'dp', 'tensor'), may hold values from -6 to 6
- cache_values: bfloat16 [2, 2048, 1024], P(None, 'dp', 'tensor'), may hold values from -6 to 6
- knn_index: int32 [2, 32, 8, 128], P(None, 'dp', 'tensor'), may hold values from 0 to 511, all different within a row
- cotangent: bfloat16 [2, 8192, 1024], P(None, ('dp', 'tensor')), may hold values from -6 to 6
Outputs:
- output: bfloat16 [2, 8192, 1024], P(None, ('dp', 'tensor'))
- grad_tokens: bfloat16 [2, 8192, 1024], P(None, ('dp', 'tensor'))
- grad_query: float32 [1024, 1024], P(None, 'tensor')
- grad_key: float32 [1024, 1024], P(None, 'tensor')
- grad_value: float32 [1024, 1024], P(None, 'tensor')
- grad_outproj: float32 [1024, 1024], P('tensor')
- grad_gate: float32 [1024, 2816], P(None, 'tensor')
- grad_up: float32 [1024, 2816], P(None, 'tensor')
- grad_down: float32 [2816, 1024], P('tensor')
- grad_attn_gain: float32 [1024], replicated
- grad_ffn_gain: float32 [1024], replicated
Inputs may be any that keep to these rules, and one draw needn't show every extreme that they name: knn_index[m, s * 4 + b, h] lists 128 distinct candidate rows read in head h by the queries of block b of sequence s of micro-batch m; an entry e < 256 is row e of the sequence's own cache, an entry e >= 256 is row e - 256 of the cache of sequence s - 1 of the same micro-batch, sequence 0 taking sequence 8 - 1.
All inputs are finite; a program needn't handle non-finite values.
Results may differ from a plain program's by a relative error of at most 0.02.
Values may be sent and summed in bfloat16 or wider, within the bound.
A program may use at most 192 MiB of HBM per device.

v0:
```python
import jax
import jax.numpy as jnp
from jax import lax
from jax.sharding import PartitionSpec as P

HEADS = 8
HD = 128
MICRO = 2
BLK = 256
TOPK = 128
CACHE = 256
QB = 512


EPS = 1e-06
NEG = -1e30


def from_behind(value, axis, steps):
    count = lax.axis_size(axis)
    pairs = [(source, (source + steps) % count) for source in range(count)]
    return lax.ppermute(value, axis, pairs)


def product(first_arg, second_arg):
    return jnp.dot(first_arg, second_arg, preferred_element_type=jnp.float32)


def product_back(first_arg, second_arg):
    return lax.dot_general(
        first_arg, second_arg, (((1,), (1,)), ((), ())), preferred_element_type=jnp.float32
    )


def across_rows(first_arg, second_arg):
    return lax.dot_general(
        first_arg, second_arg, (((0,), (0,)), ((), ())), preferred_element_type=jnp.float32
    )


def row_scale(values):
    return lax.rsqrt(jnp.mean(values * values, axis=-1, keepdims=True) + EPS)


def norm_back(grad_normed, values, scales, gain):
    scaled = grad_normed * gain
    return scales * scaled - values * scales**3 * jnp.mean(scaled * values, axis=-1, keepdims=True)


def whole_rows(normed):
    return lax.all_gather(normed, "tensor", axis=0, tiled=True)


def whole_grads(grads):
    return lax.all_gather(grads, "tensor", axis=0, tiled=True)


def sum_rows(factor, weight):
    return lax.psum_scatter(
        product(factor, weight).astype(jnp.bfloat16), "tensor", scatter_dimension=0, tiled=True
    ).astype(jnp.float32)


def back_rows(pairs):
    summed = product_back(pairs[0][0], pairs[0][1])
    for factor, weight in pairs[1:]:
        summed = summed + product_back(factor, weight)
    return lax.psum_scatter(
        summed.astype(jnp.bfloat16), "tensor", scatter_dimension=0, tiled=True
    ).astype(jnp.float32)


def block_scores(query_block, key_heads, mem_keys, first_row, local_heads):
    near_scores = jnp.einsum(
        "qhd,khd->hqk", query_block, key_heads, preferred_element_type=jnp.float32
    )
    row_ids = first_row + jnp.arange(QB)
    col_ids = jnp.arange(key_heads.shape[0])
    near_scores = jnp.where(col_ids[None, None, :] <= row_ids[None, :, None], near_scores, NEG)
    query_sub = query_block.reshape(QB // BLK, BLK, local_heads, HD)
    memory = jnp.einsum("sbhd,shtd->hsbt", query_sub, mem_keys, preferred_element_type=jnp.float32)
    return (near_scores, memory.reshape(local_heads, QB, TOPK))


def attention_forward(queries, keys_all, values_all, mem_keys, mem_values, local_heads):
    length = queries.shape[0]
    sub_blocks = QB // BLK
    query_heads = queries.reshape(length, local_heads, HD)
    key_heads = keys_all.reshape(length, local_heads, HD)
    value_heads = values_all.reshape(length, local_heads, HD)
    block_outs = []
    block_lses = []
    for block_index in range(length // QB):
        first_row = block_index * QB
        query_block = query_heads[first_row : first_row + QB]
        mem_kb = mem_keys[block_index * sub_blocks : (block_index + 1) * sub_blocks]
        mem_vb = mem_values[block_index * sub_blocks : (block_index + 1) * sub_blocks]
        near_scores, memory = block_scores(query_block, key_heads, mem_kb, first_row, local_heads)
        top_score = jnp.maximum(
            jnp.max(near_scores, axis=2, keepdims=True), jnp.max(memory, axis=2, keepdims=True)
        )
        near_exp = jnp.exp(near_scores - top_score)
        memory_exp = jnp.exp(memory - top_score)
        totals = jnp.sum(near_exp, axis=2, keepdims=True) + jnp.sum(
            memory_exp, axis=2, keepdims=True
        )
        near_prob = (near_exp / totals).astype(jnp.bfloat16)
        memory_prob = (memory_exp / totals).astype(jnp.bfloat16)
        result = jnp.einsum(
            "hqk,khd->qhd", near_prob, value_heads, preferred_element_type=jnp.float32
        )
        memory_part = jnp.einsum(
            "hsbt,shtd->sbhd",
            memory_prob.reshape(local_heads, sub_blocks, BLK, TOPK),
            mem_vb,
            preferred_element_type=jnp.float32,
        )
        block_outs.append(result + memory_part.reshape(QB, local_heads, HD))
        block_lses.append(top_score + jnp.log(totals))
    attended = (
        jnp.concatenate(block_outs, axis=0).reshape(length, local_heads * HD).astype(jnp.bfloat16)
    )
    return (attended, block_lses)


def attention_backward(
    queries, keys_all, values_all, mem_keys, mem_values, block_lses, grad_attended, local_heads
):
    length = queries.shape[0]
    sub_blocks = QB // BLK
    score_scale = HD ** (-0.5)
    query_heads = queries.reshape(length, local_heads, HD)
    key_heads = keys_all.reshape(length, local_heads, HD)
    value_heads = values_all.reshape(length, local_heads, HD)
    grad_heads = grad_attended.reshape(length, local_heads, HD)
    grad_keys = jnp.zeros((length, local_heads, HD), jnp.float32)
    grad_values = jnp.zeros((length, local_heads, HD), jnp.float32)
    grad_query_blocks = []
    for block_index in range(length // QB):
        first_row = block_index * QB
        query_block = query_heads[first_row : first_row + QB]
        grad_block = grad_heads[first_row : first_row + QB]
        mem_kb = mem_keys[block_index * sub_blocks : (block_index + 1) * sub_blocks]
        mem_vb = mem_values[block_index * sub_blocks : (block_index + 1) * sub_blocks]
        near_scores, memory = block_scores(query_block, key_heads, mem_kb, first_row, local_heads)
        near_prob = jnp.exp(near_scores - block_lses[block_index])
        memory_prob = jnp.exp(memory - block_lses[block_index])
        grad_near = jnp.einsum(
            "qhd,khd->hqk", grad_block, value_heads, preferred_element_type=jnp.float32
        )
        grad_sub = grad_block.reshape(sub_blocks, BLK, local_heads, HD)
        grad_memory = jnp.einsum(
            "sbhd,shtd->hsbt", grad_sub, mem_vb, preferred_element_type=jnp.float32
        ).reshape(local_heads, QB, TOPK)
        row_delta = jnp.sum(near_prob * grad_near, axis=2, keepdims=True) + jnp.sum(
            memory_prob * grad_memory, axis=2, keepdims=True
        )
        near_grad_scores = (near_prob * (grad_near - row_delta)).astype(jnp.bfloat16)
        memory_grad_scores = (memory_prob * (grad_memory - row_delta)).astype(jnp.bfloat16)
        grad_query_block = jnp.einsum(
            "hqk,khd->qhd", near_grad_scores, key_heads, preferred_element_type=jnp.float32
        )
        memory_part = jnp.einsum(
            "hsbt,shtd->sbhd",
            memory_grad_scores.reshape(local_heads, sub_blocks, BLK, TOPK),
            mem_kb,
            preferred_element_type=jnp.float32,
        )
        grad_query_block = grad_query_block + memory_part.reshape(QB, local_heads, HD)
        grad_query_blocks.append((grad_query_block * score_scale).astype(jnp.bfloat16))
        grad_keys = grad_keys + jnp.einsum(
            "hqk,qhd->khd", near_grad_scores, query_block, preferred_element_type=jnp.float32
        )
        grad_values = grad_values + jnp.einsum(
            "hqk,qhd->khd",
            near_prob.astype(jnp.bfloat16),
            grad_block,
            preferred_element_type=jnp.float32,
        )
    width = local_heads * HD
    grad_queries = jnp.concatenate(grad_query_blocks, axis=0).reshape(length, width)
    return (
        grad_queries,
        grad_keys.reshape(length, width).astype(jnp.bfloat16),
        grad_values.reshape(length, width).astype(jnp.bfloat16),
    )


def per_device(
    tokens,
    attn_gain,
    ffn_gain,
    query_weight,
    key_weight,
    value_weight,
    out_weight,
    gate_weight,
    up_weight,
    down_weight,
    cache_keys,
    cache_values,
    knn_index,
    cotangent,
):
    local_heads = HEADS // lax.axis_size("tensor")
    score_scale = HD ** (-0.5)
    head_pick = jnp.arange(local_heads)[None, :, None]
    grad_q_total = jnp.zeros(query_weight.shape, jnp.float32)
    grad_k_total = jnp.zeros(key_weight.shape, jnp.float32)
    grad_v_total = jnp.zeros(value_weight.shape, jnp.float32)
    grad_o_total = jnp.zeros(out_weight.shape, jnp.float32)
    grad_gate_total = jnp.zeros(gate_weight.shape, jnp.float32)
    grad_up_total = jnp.zeros(up_weight.shape, jnp.float32)
    grad_down_total = jnp.zeros(down_weight.shape, jnp.float32)
    gain_one_total = jnp.zeros(attn_gain.shape, jnp.float32)
    gain_two_total = jnp.zeros(ffn_gain.shape, jnp.float32)
    outputs = []
    input_grads = []
    for micro_index in range(MICRO):
        inputs = tokens[micro_index].astype(jnp.float32)
        scale_one = row_scale(inputs)
        normed_one = whole_rows((inputs * scale_one * attn_gain).astype(jnp.bfloat16))
        queries = (product(normed_one, query_weight) * score_scale).astype(jnp.bfloat16)
        keys_all = product(normed_one, key_weight).astype(jnp.bfloat16)
        values_all = product(normed_one, value_weight).astype(jnp.bfloat16)
        own_cache = jnp.stack((cache_keys[micro_index], cache_values[micro_index]))
        prev_cache = from_behind(own_cache, "dp", 1)
        cand_cache = jnp.concatenate((own_cache, prev_cache), axis=1)
        key_table = jnp.transpose(cand_cache[0].reshape(2 * CACHE, local_heads, HD), (1, 0, 2))
        value_table = jnp.transpose(cand_cache[1].reshape(2 * CACHE, local_heads, HD), (1, 0, 2))
        mem_keys = key_table[head_pick, knn_index[micro_index]]
        mem_values = value_table[head_pick, knn_index[micro_index]]
        attended, block_lses = attention_forward(
            queries, keys_all, values_all, mem_keys, mem_values, local_heads
        )
        hidden = inputs + sum_rows(attended, out_weight)
        scale_two = row_scale(hidden)
        normed_two = whole_rows((hidden * scale_two * ffn_gain).astype(jnp.bfloat16))
        gate_value = product(normed_two, gate_weight)
        up_value = product(normed_two, up_weight)
        sigmoid_gate = jax.nn.sigmoid(gate_value)
        silu_gate = gate_value * sigmoid_gate
        activated = (silu_gate * up_value).astype(jnp.bfloat16)
        outputs.append((hidden + sum_rows(activated, down_weight)).astype(jnp.bfloat16))
        grad_rows = cotangent[micro_index].astype(jnp.float32)
        grad_ffn = whole_grads(cotangent[micro_index])
        grad_down_total = grad_down_total + across_rows(activated, grad_ffn)
        grad_act = product_back(grad_ffn, down_weight)
        grad_gate_value = (
            grad_act * up_value * sigmoid_gate * (1.0 + gate_value * (1.0 - sigmoid_gate))
        ).astype(jnp.bfloat16)
        grad_up_value = (grad_act * silu_gate).astype(jnp.bfloat16)
        grad_gate_total = grad_gate_total + across_rows(normed_two, grad_gate_value)
        grad_up_total = grad_up_total + across_rows(normed_two, grad_up_value)
        grad_normed_two = back_rows(((grad_gate_value, gate_weight), (grad_up_value, up_weight)))
        gain_two_total = gain_two_total + jnp.sum(grad_normed_two * hidden * scale_two, axis=0)
        grad_hidden = grad_rows + norm_back(grad_normed_two, hidden, scale_two, ffn_gain)
        grad_attn_out = whole_grads(grad_hidden.astype(jnp.bfloat16))
        grad_o_total = grad_o_total + across_rows(attended, grad_attn_out)
        grad_attended = product_back(grad_attn_out, out_weight).astype(jnp.bfloat16)
        grad_queries, grad_keys, grad_values = attention_backward(
            queries,
            keys_all,
            values_all,
            mem_keys,
            mem_values,
            block_lses,
            grad_attended,
            local_heads,
        )
        grad_q_total = grad_q_total + across_rows(normed_one, grad_queries)
        grad_k_total = grad_k_total + across_rows(normed_one, grad_keys)
        grad_v_total = grad_v_total + across_rows(normed_one, grad_values)
        grad_normed_one = back_rows(
            ((grad_queries, query_weight), (grad_keys, key_weight), (grad_values, value_weight))
        )
        gain_one_total = gain_one_total + jnp.sum(grad_normed_one * inputs * scale_one, axis=0)
        input_grads.append(
            (grad_hidden + norm_back(grad_normed_one, inputs, scale_one, attn_gain)).astype(
                jnp.bfloat16
            )
        )
    summed = lax.psum(
        (
            grad_q_total,
            grad_k_total,
            grad_v_total,
            grad_o_total,
            grad_gate_total,
            grad_up_total,
            grad_down_total,
            gain_one_total,
            gain_two_total,
        ),
        "dp",
    )
    gain_sums = lax.psum((summed[7], summed[8]), "tensor")
    return (
        jnp.stack(outputs),
        jnp.stack(input_grads),
        summed[0],
        summed[1],
        summed[2],
        summed[3],
        summed[4],
        summed[5],
        summed[6],
        gain_sums[0],
        gain_sums[1],
    )


def solution(mesh):
    placed = (
        P(None, ("dp", "tensor"), None),
        P(),
        P(),
        P(None, "tensor"),
        P(None, "tensor"),
        P(None, "tensor"),
        P("tensor", None),
        P(None, "tensor"),
        P(None, "tensor"),
        P("tensor", None),
        P(None, "dp", "tensor"),
        P(None, "dp", "tensor"),
        P(None, "dp", "tensor", None),
        P(None, ("dp", "tensor"), None),
    )
    return jax.shard_map(
        per_device,
        mesh=mesh,
        in_specs=placed,
        out_specs=(
            P(None, ("dp", "tensor"), None),
            P(None, ("dp", "tensor"), None),
            P(None, "tensor"),
            P(None, "tensor"),
            P(None, "tensor"),
            P("tensor", None),
            P(None, "tensor"),
            P(None, "tensor"),
            P("tensor", None),
            P(),
            P(),
        ),
        check_vma=False,
    )
```

profile of v0, /device:TPU:0, one launch (start us, length us, event | category | flops | bytes accessed | tf_op | source)
XLA Modules:
  0.0 1089.9 jit_solution(3771710543735005826)
XLA Ops:
  20.9 5.8 gather_fusion.1
  26.7 5.8 gather_fusion
  33.0 5.8 gather_fusion.2
  38.8 6.4 gather_fusion.3
  47.4 13.7 %all-gather.15.cloned.1.call-done = bf16[1024,1024]{1,0:T(8,128)(2,1)} async-done(((bf16[256,1024]{1,0:T(8,128)(2,1)}), bf16[1024,1024]{1,0:T(8,128)(2,1)}) %all-gather.15.cloned.1.call-update) | async-done | bytes 2097168 | tf_op jit(solution)/shard_map/all_gather | solution.py:51
  67.0 40.8 %all-gather.11.cloned.1.call-done = bf16[1024,1024]{1,0:T(8,128)(2,1)} async-done(((bf16[256,1024]{1,0:T(8,128)(2,1)}), bf16[1024,1024]{1,0:T(8,128)(2,1)}) %all-gather.11.cloned.1.call-update) | async-done | bytes 2097168 | tf_op jit(solution)/shard_map/all_gather | solution.py:51
  121.8 3.0 select_reduce_fusion.2
  129.7 4.2 select_reduce_fusion.3
  140.8 6.2 fusion
  149.6 3.4 fusion.2
  159.1 6.6 fusion.1
  181.1 4.2 fusion.3
  199.7 20.8 %reduce-scatter.9.cloned.1.call-done = bf16[256,1024]{1,0:T(8,128)(2,1)} async-done(((bf16[1024,1024]{1,0:T(8,128)(2,1)}), bf16[256,1024]{1,0:T(8,128)(2,1)}) %reduce-scatter.9.cloned.1.call-update) | async-done | bytes 524304 | tf_op jit(solution)/shard_map/reduce_scatter | solution.py:59
  220.5 45.6 %reduce-scatter.13.cloned.1.call-done = bf16[256,1024]{1,0:T(8,128)(2,1)} async-done(((bf16[1024,1024]{1,0:T(8,128)(2,1)}), bf16[256,1024]{1,0:T(8,128)(2,1)}) %reduce-scatter.13.cloned.1.call-update) | async-done | bytes 524304 | tf_op jit(solution)/shard_map/reduce_scatter | solution.py:59
  275.4 41.1 %all-gather.17.cloned.1.call-done = bf16[1024,1024]{1,0:T(8,128)(2,1)} async-done(((bf16[256,1024]{1,0:T(8,128)(2,1)}), bf16[1024,1024]{1,0:T(8,128)(2,1)}) %all-gather.17.cloned.1.call-update) | async-done | bytes 2097168 | tf_op jit(solution)/shard_map/all_gather | solution.py:51
  316.5 5.4 fusion.197
  321.9 3.3 fusion.196
  325.2 37.8 %all-gather.25.cloned.1.call-done = bf16[1,1024,1024]{2,1,0:T(8,128)(2,1)} async-done(((bf16[1,256,1024]{2,1,0:T(8,128)(2,1)}), bf16[1,1024,1024]{2,1,0:T(8,128)(2,1)}) %all-gather.25.cloned.1.call-update) | async-done | bytes 2097168 | tf_op jit(solution)/shard_map/all_gather | solution.py:55
  363.0 6.5 multiply_convert_fusion.4
  372.0 3.2 add_convert_fusion.1
  375.2 34.4 %all-gather.13.cloned.1.call-done = bf16[1024,1024]{1,0:T(8,128)(2,1)} async-done(((bf16[256,1024]{1,0:T(8,128)(2,1)}), bf16[1024,1024]{1,0:T(8,128)(2,1)}) %all-gather.13.cloned.1.call-update) | async-done | bytes 2097168 | tf_op jit(solution)/shard_map/all_gather | solution.py:51
  409.6 5.4 fusion.195
  415.0 3.3 fusion.194
  418.3 37.4 %all-gather.23.cloned.1.call-done = bf16[1,1024,1024]{2,1,0:T(8,128)(2,1)} async-done(((bf16[1,256,1024]{2,1,0:T(8,128)(2,1)}), bf16[1,1024,1024]{2,1,0:T(8,128)(2,1)}) %all-gather.23.cloned.1.call-update) | async-done | bytes 2097168 | tf_op jit(solution)/shard_map/all_gather | solution.py:55
  455.7 6.6 multiply_convert_fusion.6
  464.8 3.2 add_convert_fusion.3
  468.1 4.6 convolution_convert_fusion.2
  472.7 28.3 %reduce-scatter.21.cloned.1.call-done = bf16[256,1024]{1,0:T(8,128)(2,1)} async-done(((bf16[1024,1024]{1,0:T(8,128)(2,1)}), bf16[256,1024]{1,0:T(8,128)(2,1)}) %reduce-scatter.21.cloned.1.call-update) | async-done | bytes 524304 | tf_op jit(solution)/shard_map/reduce_scatter | solution.py:68
  501.0 45.6 %reduce-scatter.17.cloned.1.call-done = bf16[256,1024]{1,0:T(8,128)(2,1)} async-done(((bf16[1024,1024]{1,0:T(8,128)(2,1)}), bf16[256,1024]{1,0:T(8,128)(2,1)}) %reduce-scatter.17.cloned.1.call-update) | async-done | bytes 524304 | tf_op jit(solution)/shard_map/reduce_scatter | solution.py:68
  550.5 41.8 %reduce-scatter.15.cloned.1.call-done = bf16[256,1024]{1,0:T(8,128)(2,1)} async-done(((bf16[1024,1024]{1,0:T(8,128)(2,1)}), bf16[256,1024]{1,0:T(8,128)(2,1)}) %reduce-scatter.15.cloned.1.call-update) | async-done | bytes 524304 | tf_op jit(solution)/shard_map/reduce_scatter | solution.py:59
  592.3 3.8 fusion.175
  597.0 44.2 %all-gather.21.cloned.1.call-done = bf16[1024,1024]{1,0:T(8,128)(2,1)} async-done(((bf16[256,1024]{1,0:T(8,128)(2,1)}), bf16[1024,1024]{1,0:T(8,128)(2,1)}) %all-gather.21.cloned.1.call-update) | async-done | bytes 2097168 | tf_op jit(solution)/shard_map/all_gather | solution.py:55
  653.1 34.7 %all-gather.19.cloned.1.call-done = bf16[1024,1024]{1,0:T(8,128)(2,1)} async-done(((bf16[256,1024]{1,0:T(8,128)(2,1)}), bf16[1024,1024]{1,0:T(8,128)(2,1)}) %all-gather.19.cloned.1.call-update) | async-done | bytes 2097168 | tf_op jit(solution)/shard_map/all_gather | solution.py:55
  707.4 5.0 multiply_reduce_fusion.2
  718.3 4.8 fusion.51
  723.1 6.5 multiply_reduce_fusion.3
  734.6 8.4 multiply_convert_fusion.3
  746.5 3.1 multiply_convert_fusion.2
  775.6 4.6 convolution_convert_fusion.3
  780.7 3.9 fusion.18
  784.6 3.2 fusion.42
  791.6 3.3 convolution_add_fusion
  794.8 3.3 convolution_add_fusion.1
  812.2 31.1 %reduce-scatter.19.cloned.1.call-done = bf16[256,1024]{1,0:T(8,128)(2,1)} async-done(((bf16[1024,1024]{1,0:T(8,128)(2,1)}), bf16[256,1024]{1,0:T(8,128)(2,1)}) %reduce-scatter.19.cloned.1.call-update) | async-done | bytes 524304 | tf_op jit(solution)/shard_map/reduce_scatter | solution.py:68
  846.5 14.2 %all-reduce = (f32[1024]{0:T(1024)}, f32[1024]{0:T(1024)}) all-reduce(f32[1024]{0:T(1024)} %add.457, f32[1024]{0:T(1024)} %add.458), channel_id=1, replica_groups=mesh['dp'=8,'tensor'=4] {'dp'}, use_global_device_ids=true, to_apply=%region_49.50 | all-reduce | flops 2048 | bytes 16384 | tf_op jit(solution)/shard_map/psum | solution.py:283
  860.7 11.9 %all-reduce.2 = (f32[1024]{0:T(1024)}, f32[1024]{0:T(1024)}) all-reduce(f32[1024]{0:T(1024)} %get-tuple-element.35, f32[1024]{0:T(1024)} %get-tuple-element.36), channel_id=1, replica_groups=mesh['dp'=8,'tensor'=4] {'tensor'}, use_global_device_ids=true, to_apply=%region_50.51 | all-reduce | flops 2048 | bytes 16384 | tf_op jit(solution)/shard_map/psum | solution.py:297
  877.5 11.4 %reduce-scatter.11.cloned.1.call-done = bf16[256,1024]{1,0:T(8,128)(2,1)} async-done(((bf16[1024,1024]{1,0:T(8,128)(2,1)}), bf16[256,1024]{1,0:T(8,128)(2,1)}) %reduce-scatter.11.cloned.1.call-update) | async-done | bytes 524304 | tf_op jit(solution)/shard_map/reduce_scatter | solution.py:59
  893.4 175.8 %all-reduce.5.cloned.1.call-done = (f32[1024,256]{1,0:T(8,128)}, f32[1024,256]{1,0:T(8,128)}, f32[1024,256]{1,0:T(8,128)}, f32[256,1024]{1,0:T(8,128)}, f32[1024...) async-done(((f32[1024,256]{1,0:T(8,128)}, f32[1024,256]{1,0:T(8,128)}, f32[1024,256]{1,0:T(8,128)}, f32[256,1024]{1,0:T(8,128)}, f32[1024,704]{0,1:T(8,128)}, ...) | async-done | bytes 12845072 | tf_op jit(solution)/shard_map/psum | solution.py:283
  (549 shorter events, 221.0 us)
Async XLA Ops:
  7.2 355.8 %copy-start = (bf16[704,1024]{1,0:T(8,128)(2,1)S(1)}, bf16[704,1024]{1,0:T(8,128)(2,1)}, u32[]{:S(2)}) copy-start(bf16[704,1024]{1,0:T(8,128)(2,1)} %param.23) | copy-start | bytes 4325380
  7.2 53.9 %all-gather.15.cloned.1.call-start = ((), (), s32[]{:S(2)}) async-start(), calls=%async_computation.12 | async-start | bytes 2621440 | tf_op jit(solution)/shard_map/all_gather | solution.py:51
  10.1 6.4 copy-start.139
  12.6 95.2 %all-gather.11.cloned.1.call-start = ((), (), s32[]{:S(2)}) async-start(), calls=%async_computation.8 | async-start | bytes 2621440 | tf_op jit(solution)/shard_map/all_gather | solution.py:51
  12.9 7.5 collective-permute-start
  13.7 18.8 %collective-permute-start.1 = (bf16[2,256,256]{1,2,0:T(8,128)(2,1)S(1)}, bf16[2,256,256]{1,2,0:T(8,128)(2,1)S(1)}, u32[]{:S(2)}, u32[]{:S(2)}) collective-permute-start(bf16[2,256,256]{1,2,0:T(8,128)(2,1)S(1)} %pad_maximum_fusion.9), channel_id=1, source_target_pairs={{0,4},{4,8},{8,12},{12,16},{16,20},{20,24},{24,28},{28,0},{1,5},{5... | collective-permute-start | bytes 786440 | tf_op jit(solution)/shard_map/ppermute | solution.py:22
  16.4 204.1 %reduce-scatter.9.cloned.1.call-start = ((), (), s32[]{:S(2)}) async-start(), calls=%async_computation.9 | async-start | bytes 2621440 | tf_op jit(solution)/shard_map/reduce_scatter | solution.py:59
  38.8 22.3 %copy-start.76 = (bf16[1024,256]{1,0:T(8,128)(2,1)S(1)}, bf16[1024,256]{1,0:T(8,128)(2,1)}, u32[]{:S(2)}) copy-start(bf16[1024,256]{1,0:T(8,128)(2,1)} %param.17) | copy-start | bytes 1572868
  47.4 17.3 %copy-start.95 = (bf16[512,128]{1,0:T(8,128)(2,1)}, bf16[512,128]{1,0:T(8,128)(2,1)S(1)}, u32[]{:S(2)}) copy-start(bf16[512,128]{1,0:T(8,128)(2,1)S(1)} %get-tuple-element.100) | copy-start | bytes 393220
  47.4 17.9 %copy-start.94 = (bf16[512,128]{1,0:T(8,128)(2,1)}, bf16[512,128]{1,0:T(8,128)(2,1)S(1)}, u32[]{:S(2)}) copy-start(bf16[512,128]{1,0:T(8,128)(2,1)S(1)} %get-tuple-element.99) | copy-start | bytes 393220
  107.8 12.2 %copy-start.14 = (bf16[1024,1024]{1,0:T(8,128)(2,1)S(1)}, bf16[1024,1024]{1,0:T(8,128)(2,1)}, u32[]{:S(2)}) copy-start(bf16[1024,1024]{1,0:T(8,128)(2,1)} %all-gather.11.cloned.1.call-done) | copy-start | bytes 6291460
  114.6 7.1 copy-start.20
  114.6 7.2 copy-start.66
  134.5 6.2 copy-start.24
  134.5 6.3 copy-start.64
  140.7 6.3 copy-start.39
  178.0 88.2 %reduce-scatter.13.cloned.1.call-start = ((), (), s32[]{:S(2)}) async-start(), calls=%async_computation.13 | async-start | bytes 2621440 | tf_op jit(solution)/shard_map/reduce_scatter | solution.py:59
  196.8 69.3 %copy-start.13 = (bf16[2,256,1024]{2,1,0:T(8,128)(2,1)S(1)}, bf16[2,256,1024]{2,1,0:T(8,128)(2,1)}, u32[]{:S(2)}) copy-start(bf16[2,256,1024]{2,1,0:T(8,128)(2,1)} %param.14) | copy-start | bytes 3145732
  199.7 69.3 %copy-start.102 = (f32[1024]{0:T(1024)S(1)}, f32[1024]{0:T(1024)}, u32[]{:S(2)}) copy-start(f32[1024]{0:T(1024)} %param.16) | copy-start | bytes 12292
  199.7 116.8 %all-gather.17.cloned.1.call-start = ((), (), s32[]{:S(2)}) async-start(), calls=%async_computation.14 | async-start | bytes 2621440 | tf_op jit(solution)/shard_map/all_gather | solution.py:51
  271.5 91.5 %all-gather.25.cloned.1.call-start = ((), (), s32[]{:S(2)}) async-start(), calls=%async_computation.23 | async-start | bytes 2621440 | tf_op jit(solution)/shard_map/all_gather | solution.py:55
  273.8 135.8 %all-gather.13.cloned.1.call-start = ((), (), s32[]{:S(2)}) async-start(), calls=%async_computation.10 | async-start | bytes 2621440 | tf_op jit(solution)/shard_map/all_gather | solution.py:51
  274.6 181.1 %all-gather.23.cloned.1.call-start = ((), (), s32[]{:S(2)}) async-start(), calls=%async_computation.22 | async-start | bytes 2621440 | tf_op jit(solution)/shard_map/all_gather | solution.py:55
  275.3 225.7 %reduce-scatter.21.cloned.1.call-start = ((), (), s32[]{:S(2)}) async-start(), calls=%async_computation.19 | async-start | bytes 2621440 | tf_op jit(solution)/shard_map/reduce_scatter | solution.py:68
  363.0 6.5 copy-start.147
  375.2 171.4 %reduce-scatter.17.cloned.1.call-start = ((), (), s32[]{:S(2)}) async-start(), calls=%async_computation.16 | async-start | bytes 2621440 | tf_op jit(solution)/shard_map/reduce_scatter | solution.py:68
  455.7 6.6 copy-start.149
  468.0 124.3 %reduce-scatter.15.cloned.1.call-start = ((), (), s32[]{:S(2)}) async-start(), calls=%async_computation.15 | async-start | bytes 2621440 | tf_op jit(solution)/shard_map/reduce_scatter | solution.py:59
  468.0 78.5 %copy-start.31 = (bf16[256,1024]{1,0:T(8,128)(2,1)S(1)}, bf16[256,1024]{1,0:T(8,128)(2,1)}, u32[]{:S(2)}) copy-start(bf16[256,1024]{1,0:T(8,128)(2,1)} %reduce-scatter.9.cloned.1.call-done) | copy-start | bytes 1572868
  472.7 168.5 %all-gather.21.cloned.1.call-start = ((), (), s32[]{:S(2)}) async-start(), calls=%async_computation.20 | async-start | bytes 2621440 | tf_op jit(solution)/shard_map/all_gather | solution.py:55
  596.2 91.6 %all-gather.19.cloned.1.call-start = ((), (), s32[]{:S(2)}) async-start(), calls=%async_computation.17 | async-start | bytes 2621440 | tf_op jit(solution)/shard_map/all_gather | solution.py:55
  596.9 49.2 %copy-start.38 = (f32[2,2,256,128]{2,3,1,0:T(8,128)S(1)}, f32[2,2,256,128]{2,3,1,0:T(8,128)}, u32[]{:S(2)}) copy-start(f32[2,2,256,128]{2,3,1,0:T(8,128)} %get-tuple-element.130) | copy-start | bytes 1572868
  596.9 215.3 %reduce-scatter.23.cloned.1.call-start = ((), (), s32[]{:S(2)}) async-start(), calls=%async_computation.21 | async-start | bytes 2621440 | tf_op jit(solution)/shard_map/reduce_scatter | solution.py:68
  653.1 39.7 %copy-start.36 = (f32[2,2,256,128]{2,3,1,0:T(8,128)S(1)}, f32[2,2,256,128]{2,3,1,0:T(8,128)}, u32[]{:S(2)}) copy-start(f32[2,2,256,128]{2,3,1,0:T(8,128)} %get-tuple-element.125) | copy-start | bytes 1572868
  715.7 7.5 copy-start.9
  734.6 8.4 copy-start.65
  734.6 11.1 %copy-start.12 = (f32[2,512,1024]{2,1,0:T(8,128)S(1)}, f32[2,512,1024]{2,1,0:T(8,128)}, u32[]{:S(2)}) copy-start(f32[2,512,1024]{2,1,0:T(8,128)} %get-tuple-element.121) | copy-start | bytes 12582916
  734.6 11.1 %copy-start.19 = (f32[2,512,1024]{2,1,0:T(8,128)S(1)}, f32[2,512,1024]{2,1,0:T(8,128)}, u32[]{:S(2)}) copy-start(f32[2,512,1024]{2,1,0:T(8,128)} %copy-done.18) | copy-start | bytes 12582916
  734.6 11.1 %copy-start.30 = (f32[2,512,1024]{2,1,0:T(8,128)S(1)}, f32[2,512,1024]{2,1,0:T(8,128)}, u32[]{:S(2)}) copy-start(f32[2,512,1024]{2,1,0:T(8,128)} %get-tuple-element.131) | copy-start | bytes 12582916
  755.7 87.6 %reduce-scatter.19.cloned.1.call-start = ((), (), s32[]{:S(2)}) async-start(), calls=%async_computation.18 | async-start | bytes 2621440 | tf_op jit(solution)/shard_map/reduce_scatter | solution.py:68
  775.6 113.3 %reduce-scatter.11.cloned.1.call-start = ((), (), s32[]{:S(2)}) async-start(), calls=%async_computation.11 | async-start | bytes 2621440 | tf_op jit(solution)/shard_map/reduce_scatter | solution.py:59
  780.2 289.0 %all-reduce.5.cloned.1.call-start = ((), (), s32[]{:S(2)}) async-start(), calls=%async_computation.24 | async-start | bytes 25690112 | tf_op jit(solution)/shard_map/psum | solution.py:283
  810.8 32.5 %copy-start.103 = (f32[1024]{0:T(1024)S(1)}, f32[1024]{0:T(1024)}, u32[]{:S(2)}) copy-start(f32[1024]{0:T(1024)} %param.15) | copy-start | bytes 12292
  810.8 63.8 %copy-start.33 = (bf16[256,1024]{1,0:T(8,128)(2,1)S(1)}, bf16[256,1024]{1,0:T(8,128)(2,1)}, u32[]{:S(2)}) copy-start(bf16[256,1024]{1,0:T(8,128)(2,1)} %reduce-scatter.13.cloned.1.call-done) | copy-start | bytes 1572868
  810.8 63.8 %copy-start.131 = (f32[256]{0:T(256)S(1)}, f32[256]{0:T(256)}, u32[]{:S(2)}) copy-start(f32[256]{0:T(256)} %copy-done.130) | copy-start | bytes 3076
  810.8 78.0 %copy-start.32 = (bf16[256,1024]{1,0:T(8,128)(2,1)S(1)}, bf16[256,1024]{1,0:T(8,128)(2,1)}, u32[]{:S(2)}) copy-start(bf16[256,1024]{1,0:T(8,128)(2,1)} %reduce-scatter.9.cloned.1.call-done) | copy-start | bytes 1572868
  810.8 78.0 %copy-start.129 = (f32[256]{0:T(256)S(1)}, f32[256]{0:T(256)}, u32[]{:S(2)}) copy-start(f32[256]{0:T(256)} %copy-done.128) | copy-start | bytes 3076
  877.5 13.8 %copy-start.93 = (bf16[1,256,1024]{2,1,0:T(8,128)(2,1)S(1)}, bf16[1,256,1024]{2,1,0:T(8,128)(2,1)}, u32[]{:S(2)}) copy-start(bf16[1,256,1024]{2,1,0:T(8,128)(2,1)} %fusion.124) | copy-start | bytes 1572868
  (132 other events, 380.2 us)
Sparse Core Ops, SparseCore 0:
  12.7 48.3 all-gather.14
  63.3 44.4 all-gather.10
  178.1 42.4 reduce-scatter.8
  223.3 42.8 reduce-scatter.12
  271.6 44.8 all-gather.16
  318.5 44.4 all-gather.24
  365.1 44.4 all-gather.12
  411.2 44.4 all-gather.22
  458.6 42.4 reduce-scatter.20
  503.7 42.8 reduce-scatter.16
  549.5 42.8 reduce-scatter.14
  596.3 44.8 all-gather.20
  643.3 44.4 all-gather.18
  755.8 42.4 reduce-scatter.22
  800.4 42.8 reduce-scatter.18
  845.4 43.3 reduce-scatter.10
  894.8 174.3 all-reduce.4
where the time goes:
time: 1100 us; the launch traced here: 1090 us
  waiting for transfers between devices  689 us (63%)
  matrix products  188 us (17%)
  local copies, waits for them, and re-layouts  92.3 us (8%)
  other arithmetic  74.5 us (7%)
  blocking collectives  26.1 us (2%)
  between operations  15.9 us (1%)
    psum x1, waiting for transfers between devices, per_device(): lax.psum((grad_q_total, grad_k_total, grad_v_total, grad_o_total, grad_ga...  176 us
    all_gather x4, waiting for transfers between devices, whole_grads(): return lax.all_gather(grads, 'tensor', axis=0, tiled=True)  154 us
    all_gather x4, waiting for transfers between devices, whole_rows(): return lax.all_gather(normed, 'tensor', axis=0, tiled=True)  130 us
    reduce_scatter x4, waiting for transfers between devices, sum_rows(): lax.psum_scatter(product(factor, weight).astype(jnp.bfloat16), 'tensor',...  120 us
    reduce_scatter x4, waiting for transfers between devices, back_rows(): lax.psum_scatter(summed.astype(jnp.bfloat16), 'tensor', scatter_dimension...  105 us
    dot_general x14, matrix products, product(): return jnp.dot(first_arg, second_arg, preferred_element_type=jnp.float32)  41.5 us
    unnamed x345, local copies, waits for them, and re-layouts  38.4 us
    dot_general x14, matrix products, product_back(): lax.dot_general(first_arg, second_arg, (((1,), (1,)), ((), ())), preferre...  35.3 us
  transfers between devices with their start and end apart: 19, of which 17 were waited for; matrix products, arithmetic and copies ran while one was open for 17% of the time, Pallas kernels for 0%

commit v1 on v0

v1 whole, which is shorter than its diff:
```python
import functools

import jax
import jax.numpy as jnp
from jax import lax
from jax.experimental import pallas as pl
from jax.experimental.pallas import tpu as pltpu
from jax.sharding import Mesh
from jax.sharding import PartitionSpec as P

HEADS = 8
HD = 128
MICRO = 2
BLK = 256
TOPK = 128
CACHE = 256
D = 1024
NQ = 4
DP = D // NQ
HALF = 512
LEN = 1024
HID = 352
RA = 4 * HD
RB = 3 * HID

EPS = 1e-06
NEG = -1e30
BF = jnp.bfloat16
F32 = jnp.float32


def nn(a, b):
    return lax.dot_general(a, b, (((1,), (0,)), ((), ())), preferred_element_type=F32)


def nt(a, b):
    return lax.dot_general(a, b, (((1,), (1,)), ((), ())), preferred_element_type=F32)


def tn(a, b):
    return lax.dot_general(a, b, (((0,), (0,)), ((), ())), preferred_element_type=F32)


VM = pl.BlockSpec(memory_space=pltpu.VMEM)
SM = pl.BlockSpec(memory_space=pltpu.SMEM)


def call(body, outs, args, flops=0, trans=0, scratch=(), name=None, vmem=None):
    nbytes = sum(a.size * a.dtype.itemsize for a in args) + sum(
        jnp.dtype(t).itemsize * functools.reduce(lambda x, y: x * y, s, 1) for s, t in outs
    )
    return pl.pallas_call(
        body,
        out_shape=[jax.ShapeDtypeStruct(s, t) for s, t in outs],
        in_specs=[SM if i == 0 else VM for i in range(len(args))],
        out_specs=[VM for _ in outs],
        scratch_shapes=list(scratch),
        name=name,
        compiler_params=pltpu.CompilerParams(vmem_limit_bytes=vmem),
        cost_estimate=pl.CostEstimate(flops=int(flops), bytes_accessed=int(nbytes), transcendentals=int(trans)),
    )(*args)


def block(index, size):
    return pl.ds(pl.multiple_of(index * size, size), size)


def lanes(k):
    return slice(k * DP, (k + 1) * DP)


def prep_rows_body(ids, x, gains, s0, s1, rel_gains):
    q, t = ids[0], ids[2]
    for k in range(NQ):
        cols = block(q ^ k, DP)
        rel_gains[:, lanes(k)] = gains[:, cols]
        for r, out in ((0, s0), (1, s1)):
            out[:, lanes(k)] = x[(r + t) & 1, :, cols]


def unprep_rows_body(ids, b0, b1, out):
    q, t = ids[0], ids[2]
    for k in range(NQ):
        cols = block(q ^ k, DP)
        for r, src in ((0, b0), (1, b1)):
            out[(r + t) & 1, :, cols] = src[:, lanes(k)]


def prep_a_body(ids, wq, wk, wv, wo, out):
    q, c = ids[0], ids[1]
    for k in range(NQ):
        rows = block(q ^ k, DP)
        for i, w in enumerate((wq, wk, wv)):
            out[k, i * HD : (i + 1) * HD, :] = w[rows, block(c, HD)].T
        out[k, 3 * HD : 4 * HD, :] = wo[block(c, HD), rows]


def prep_b_body(ids, wg, wu, wd, out, turned):
    q, c = ids[0], ids[1]
    for k in range(NQ):
        rows = block(q ^ k, DP)
        for i, w in enumerate((wg, wu)):
            turned[...] = w[rows, :].T
            out[k, i * HID : (i + 1) * HID, :] = turned[pl.ds(pl.multiple_of(c * HID, 32), HID), :]
        out[k, 2 * HID : 3 * HID, :] = wd[pl.ds(pl.multiple_of(c * HID, 32), HID), rows]


def memory_body(ids, own, prev, knn, out):
    for m in range(MICRO):
        for h in range(2):
            cols = slice(h * HD, (h + 1) * HD)
            for b in range(LEN // BLK):
                picks = knn[m, b, h : h + 1, :]
                rows = lax.broadcasted_iota(jnp.int32, (CACHE, TOPK), 0)
                hot_own = jnp.where(rows == picks, 1.0, 0.0).astype(BF)
                hot_prev = jnp.where(rows + CACHE == picks, 1.0, 0.0).astype(BF)
                for kv in range(2):
                    got = tn(hot_own, own[kv, m, :, cols]) + tn(hot_prev, prev[kv, m, :, cols])
                    out[m, h, kv * 512 + b * TOPK : kv * 512 + (b + 1) * TOPK, :] = got.astype(BF)


def scale_of(x):
    return lax.rsqrt(jnp.mean(x * x, axis=-1, keepdims=True) + EPS)


def norm_one_body(ids, r0, r1, gains, x_own, n_own):
    t = ids[2]
    for r, src in ((0, r0), (1, r1)):
        rows = block((t & 1) ^ r, 256)
        raw = src[...]
        x = raw.astype(F32)
        x_own[rows, :] = raw
        n_own[rows, :] = (x * scale_of(x) * gains[0:1, :]).astype(BF)


def arrange_body(ids, r0, r1, own):
    t = ids[2]
    for r, src in ((0, r0), (1, r1)):
        own[block((t & 1) ^ r, 256), :] = src[...]


def norm_two_body(ids, x, o_own, o_got, gains, hidden, n_own):
    for i in range(2):
        rows = slice(i * 256, (i + 1) * 256)
        h = x[rows, :].astype(F32) + (o_own[rows, :] + o_got[rows, :].astype(F32))
        hidden[rows, :] = h
        n_own[rows, :] = (h * scale_of(h) * gains[1:2, :]).astype(BF)


def output_body(ids, hidden, y_own, y_got, s0, s1):
    t = ids[2]
    for r, out in ((0, s0), (1, s1)):
        rows = block((t & 1) ^ r, 256)
        out[...] = (hidden[rows, :] + (y_own[rows, :] + y_got[rows, :].astype(F32))).astype(BF)


def norm_back(grad, x, gain):
    scale = scale_of(x)
    scaled = grad * gain
    gain_part = jnp.sum(grad * x * scale, axis=0, keepdims=True)
    back = scale * scaled - x * (scale * scale * scale) * jnp.mean(scaled * x, axis=-1, keepdims=True)
    return back, gain_part


def put_gain(ids, out, total):
    q = ids[0]
    for k in range(NQ):
        out[:, block(q ^ k, DP)] = total[:, lanes(k)]


def norm_two_back_body(ids, d_own, d_got, cot, hidden, gains, grad_hidden, low, gain_out):
    total = jnp.zeros((1, D), F32)
    for i in range(2):
        rows = slice(i * 256, (i + 1) * 256)
        grad = d_own[rows, :] + d_got[rows, :].astype(F32)
        back, part = norm_back(grad, hidden[rows, :], gains[1:2, :])
        total = total + part
        g = cot[rows, :].astype(F32) + back
        grad_hidden[rows, :] = g
        low[rows, :] = g.astype(BF)
    put_gain(ids, gain_out, total)


def norm_one_back_body(ids, d_own, d_got, grad_hidden, x, gains, s0, s1, gain_out):
    t = ids[2]
    total = jnp.zeros((1, D), F32)
    for r, out in ((0, s0), (1, s1)):
        rows = block((t & 1) ^ r, 256)
        grad = d_own[rows, :] + d_got[rows, :].astype(F32)
        back, part = norm_back(grad, x[rows, :].astype(F32), gains[0:1, :])
        total = total + part
        out[...] = (grad_hidden[rows, :] + back).astype(BF)
    put_gain(ids, gain_out, total)


def causal():
    return lax.broadcasted_iota(jnp.int32, (BLK, BLK), 1) <= lax.broadcasted_iota(jnp.int32, (BLK, BLK), 0)


def attention_body(ids, n_own, n_oth, w0, w1, w2, w3, mem, qkv, att, lse):
    c = ids[1]
    w = jnp.concatenate([p[0 : 3 * HD, :] for p in (w0, w1, w2, w3)], axis=1)
    for who, n in ((c, n_own), (1 - c, n_oth)):
        acc = nt(n[...], w)
        rows = block(who, HALF)
        qkv[rows, 0:HD] = (acc[:, 0:HD] * (HD**-0.5)).astype(BF)
        qkv[rows, HD : 3 * HD] = acc[:, HD : 3 * HD].astype(BF)
    keep = causal()
    for b in range(LEN // BLK):
        rows = slice(b * BLK, (b + 1) * BLK)
        query = qkv[rows, 0:HD]
        diag = jnp.where(keep, nt(query, qkv[rows, HD : 2 * HD]), NEG)
        far = nt(query, mem[b * TOPK : (b + 1) * TOPK, :])
        top = jnp.maximum(jnp.max(diag, axis=1, keepdims=True), jnp.max(far, axis=1, keepdims=True))
        if b:
            past = nt(query, qkv[0 : b * BLK, HD : 2 * HD])
            top = jnp.maximum(top, jnp.max(past, axis=1, keepdims=True))
        diag = jnp.exp(diag - top)
        far = jnp.exp(far - top)
        total = jnp.sum(diag, axis=1, keepdims=True) + jnp.sum(far, axis=1, keepdims=True)
        if b:
            past = jnp.exp(past - top)
            total = total + jnp.sum(past, axis=1, keepdims=True)
        inverse = 1.0 / total
        out = nn((diag * inverse).astype(BF), qkv[rows, 2 * HD : 3 * HD])
        out = out + nn((far * inverse).astype(BF), mem[512 + b * TOPK : 512 + (b + 1) * TOPK, :])
        if b:
            out = out + nn((past * inverse).astype(BF), qkv[0 : b * BLK, 2 * HD : 3 * HD])
        att[rows, :] = out.astype(BF)
        lse[rows, :] = jnp.broadcast_to(top + jnp.log(total), (BLK, HD))


def out_proj_body(ids, a0, a1, a2, a3, *refs):
    c = ids[1]
    w, (o_own, o_oth) = refs[:16], refs[16:]
    weights = jnp.concatenate(
        [jnp.concatenate([w[4 * j + k][3 * HD : 4 * HD, :] for k in range(NQ)], axis=1) for j in range(4)], axis=0
    )
    for who, out in ((1 - c, o_oth), (c, o_own)):
        rows = block(who, HALF)
        a = jnp.concatenate([a[rows, :] for a in (a0, a1, a2, a3)], axis=1)
        out[...] = nn(a, weights).astype(out.dtype)


def attention_back_body(pieces, ids, g_own, g_oth, n_own, n_oth, w0, w1, w2, w3, qkv, att, lse, mem,
                        keep_out, send_out, dq_own, dq_oth, da, dk, dv, dall):
    c = ids[1]
    wo = jnp.concatenate([p[3 * HD : 4 * HD, :] for p in (w0, w1, w2, w3)], axis=1)
    grad_o = jnp.zeros((HD, D), F32)
    for who, g in ((c, g_own), (1 - c, g_oth)):
        rows = block(who, HALF)
        grads = g[...]
        da[rows, :] = nt(grads, wo).astype(BF)
        grad_o = grad_o + tn(att[rows, :], grads)
    keep = causal()
    for b in range(LEN // BLK):
        rows = slice(b * BLK, (b + 1) * BLK)
        query = qkv[rows, 0:HD]
        grad = da[rows, :]
        level = lse[rows, 0:1]
        mem_k = mem[b * TOPK : (b + 1) * TOPK, :]
        mem_v = mem[512 + b * TOPK : 512 + (b + 1) * TOPK, :]
        p_d = jnp.exp(jnp.where(keep, nt(query, qkv[rows, HD : 2 * HD]), NEG) - level)
        p_f = jnp.exp(nt(query, mem_k) - level)
        g_d = nt(grad, qkv[rows, 2 * HD : 3 * HD])
        g_f = nt(grad, mem_v)
        delta = jnp.sum(p_d * g_d, axis=1, keepdims=True) + jnp.sum(p_f * g_f, axis=1, keepdims=True)
        if b:
            past = slice(0, b * BLK)
            p_p = jnp.exp(nt(query, qkv[past, HD : 2 * HD]) - level)
            g_p = nt(grad, qkv[past, 2 * HD : 3 * HD])
            delta = delta + jnp.sum(p_p * g_p, axis=1, keepdims=True)
        s_d = (p_d * (g_d - delta)).astype(BF)
        s_f = (p_f * (g_f - delta)).astype(BF)
        dq = nn(s_d, qkv[rows, HD : 2 * HD]) + nn(s_f, mem_k)
        if b:
            s_p = (p_p * (g_p - delta)).astype(BF)
            dq = dq + nn(s_p, qkv[past, HD : 2 * HD])
            dk[past, :] = dk[past, :] + tn(s_p, query)
            dv[past, :] = dv[past, :] + tn(p_p.astype(BF), grad)
        dk[rows, :] = tn(s_d, query)
        dv[rows, :] = tn(p_d.astype(BF), grad)
        dall[rows, 0:HD] = (dq * (HD**-0.5)).astype(BF)
    dall[:, HD : 2 * HD] = dk[...].astype(BF)
    dall[:, 2 * HD : 3 * HD] = dv[...].astype(BF)
    grad_w = jnp.zeros((3 * HD, D), F32)
    for who, n, out in ((c, n_own, dq_own), (1 - c, n_oth, dq_oth)):
        part = dall[block(who, HALF), :]
        out[...] = part
        grad_w = grad_w + tn(part, n[...])
    for out, which in ((keep_out, pieces[:2]), (send_out, pieces[2:])):
        for slot, k in enumerate(which):
            out[slot, 0 : 3 * HD, :] = grad_w[:, lanes(k)].astype(BF)
            out[slot, 3 * HD : 4 * HD, :] = grad_o[:, lanes(k)].astype(BF)


def in_proj_back_body(ids, *refs):
    parts, w, (d_own, d_oth) = refs[:8], refs[8:24], refs[24:]
    weights = jnp.concatenate(
        [jnp.concatenate([w[4 * j + k][0 : 3 * HD, :] for k in range(NQ)], axis=1) for j in range(4)], axis=0
    )
    for side, out in ((1, d_oth), (0, d_own)):
        d = jnp.concatenate([parts[2 * j + side][...] for j in range(4)], axis=1)
        out[...] = nn(d, weights).astype(out.dtype)


def ffn_body(pieces, ids, n_own, n_oth, c_own, c_oth, w0, w1, w2, w3, keep_out, send_out, act, dgu, w):
    for k, p in enumerate((w0, w1, w2, w3)):
        w[:, lanes(k)] = p[...]
    for side, n, cot in ((0, n_own, c_own), (1, n_oth, c_oth)):
        for i in range(2):
            rows = slice(i * 256, (i + 1) * 256)
            cols = slice(side * HALF + i * 256, side * HALF + (i + 1) * 256)
            normed = n[rows, :]
            gate = nt(w[0:HID, :], normed)
            up = nt(w[HID : 2 * HID, :], normed)
            grad = nt(w[2 * HID : 3 * HID, :], cot[rows, :])
            sig = 1.0 / (1.0 + jnp.exp(-gate))
            silu = gate * sig
            act[:, cols] = (silu * up).astype(BF)
            dgu[0:HID, cols] = (grad * up * sig * (1.0 + gate * (1.0 - sig))).astype(BF)
            dgu[HID : 2 * HID, cols] = (grad * silu).astype(BF)
    for out, which in ((keep_out, pieces[:2]), (send_out, pieces[2:])):
        for slot, k in enumerate(which):
            g = nn(dgu[:, 0:HALF], n_own[:, lanes(k)]) + nn(dgu[:, HALF:LEN], n_oth[:, lanes(k)])
            out[slot, 0 : 2 * HID, :] = g.astype(BF)
            g = nn(act[:, 0:HALF], c_own[:, lanes(k)]) + nn(act[:, HALF:LEN], c_oth[:, lanes(k)])
            out[slot, 2 * HID : 3 * HID, :] = g.astype(BF)


def ffn_sum_body(lo, hi, ids, *refs):
    parts, w, (own, oth, acc) = refs[:4], refs[4:20], refs[20:]
    for side, out in ((1, oth), (0, own)):
        cols = slice(side * HALF, (side + 1) * HALF)
        for j in range(4):
            weights = jnp.concatenate([w[4 * j + k][lo:hi, :] for k in range(NQ)], axis=1)
            got = tn(parts[j][:, cols], weights)
            if j == 0:
                acc[...] = got
            elif j < 3:
                acc[...] = acc[...] + got
            else:
                out[...] = (acc[...] + got).astype(out.dtype)


def place_a_body(ids, *refs):
    q, c = ids[0], ids[1]
    own, oth, (gq, gk, gv, go) = refs[:4], refs[4:8], refs[8:]
    for k in range(NQ):
        rows = block(q ^ k, DP)
        for half, src in ((c, own[k]), (1 - c, oth[k])):
            for i, out in enumerate((gq, gk, gv)):
                out[rows, block(half, HD)] = src[i * HD : (i + 1) * HD, :].astype(F32).T
            go[block(half, HD), rows] = src[3 * HD : 4 * HD, :].astype(F32)


def place_b_body(ids, *refs):
    q, c = ids[0], ids[1]
    own, oth, (gg, gu, gd, joined) = refs[:4], refs[4:8], refs[8:]
    for k in range(NQ):
        rows = block(q ^ k, DP)
        for i, out in enumerate((gg, gu)):
            for half, src in ((c, own[k]), (1 - c, oth[k])):
                joined[pl.ds(pl.multiple_of(half * HID, 32), HID), :] = src[i * HID : (i + 1) * HID, :].astype(F32)
            out[rows, :] = joined[...].T
        for half, src in ((c, own[k]), (1 - c, oth[k])):
            gd[pl.ds(pl.multiple_of(half * HID, 32), HID), rows] = src[2 * HID : 3 * HID, :].astype(F32)


def send(value, axis, pairs):
    return lax.ppermute(value, axis, pairs)


def flip(value, axis, bits):
    count = lax.axis_size(axis)
    return send(value, axis, [(i, i ^ bits) for i in range(count)])


def row_pairs(r):
    return [
        (c * 4 + t, (t // 2) * 4 + 2 * c + (r + t) % 2)
        for c in range(2)
        for t in range(4)
    ]


def rows_to_sequences(s0, s1):
    return [send(s, ("c", "t"), row_pairs(r)) for r, s in ((0, s0), (1, s1))]


def rows_back(s0, s1):
    return [send(s, ("c", "t"), [(b, a) for a, b in row_pairs(r)]) for r, s in ((0, s0), (1, s1))]


def memory_pairs(k, i):
    pairs = []
    for c in range(2):
        for t in range(4):
            kind = k + 2 * (c ^ (t >> 1))
            pairs.append((c * 4 + t, (i ^ (kind >> 1)) * 4 + (t ^ kind)))
    return pairs


def gather_weights(own):
    table = [[own[k] for k in range(NQ)]]
    for j in range(1, 4):
        mine = flip(own[0], "t", j)
        by_x = flip(mine, "q", 1)
        by_y = flip(mine, "q", 2)
        if j == 1:
            far = flip(by_x, "q", 2)
        elif j == 2:
            far = flip(by_y, "q", 1)
        else:
            far = flip(mine, "q", 3)
        table.append([mine, by_x, by_y, far])
    return table


PIECES = ((0, 2, 1, 3), (0, 1, 2, 3), (0, 2, 1, 3), (0, 1, 2, 3))


def plane_sum(j, keep, out):
    first, second = (1, 2) if j % 2 == 0 else (2, 1)
    kept = (keep.astype(F32) + flip(out, "q", first).astype(F32)).astype(BF)
    return (kept[0].astype(F32) + flip(kept[1], "q", second).astype(F32)).astype(BF)


def column_sum(sums):
    total = sums[0].astype(F32)
    for j in range(1, 4):
        total = total + flip(sums[j], "t", j).astype(F32)
    if lax.axis_size("r") > 1:
        total = lax.psum(total, "r")
    return total.astype(BF)


def spread(total, odd):
    by_x = flip(total, "q", 1)
    by_y = flip(total, "q", 2)
    far = flip(by_x, "q", 2) if odd else flip(by_y, "q", 1)
    own = [total, by_x, by_y, far]
    return own, [flip(p, "c", 1) for p in own]


def per_device(tokens, attn_gain, ffn_gain, query_weight, key_weight, value_weight, out_weight, gate_weight,
               up_weight, down_weight, cache_keys, cache_values, knn_index, cotangent):
    q, c, t = lax.axis_index("q"), lax.axis_index("c"), lax.axis_index("t")
    ids = jnp.stack([q, c, t]).astype(jnp.int32)
    gains = jnp.stack([attn_gain, ffn_gain])
    rows16 = ((256, D), BF)
    half16, half32 = ((HALF, D), BF), ((HALF, D), F32)

    s0, s1, rel_gains = call(prep_rows_body, [rows16, rows16, ((2, D), F32)], (ids, tokens, gains), name="prep_tokens")
    x0, x1 = rows_to_sequences(s0, s1)
    (own_a,) = call(
        prep_a_body, [((NQ, RA, DP), BF)], (ids, query_weight, key_weight, value_weight, out_weight), name="prep_a"
    )
    wa = gather_weights(own_a)
    own_cache = jnp.stack((cache_keys, cache_values))
    count = lax.axis_size(("r", "q", "c"))
    prev_cache = send(own_cache, ("r", "q", "c"), [(i, (i + 1) % count) for i in range(count)])
    (picked,) = call(
        memory_body, [((MICRO, 2, 1024, HD), BF)], (ids, own_cache, prev_cache, knn_index),
        flops=2 * 32 * 2 * 256 * 128 * 128, name="memory",
    )
    got = {}
    for k in range(2):
        for i in range(2):
            mine = picked[(t & 1) ^ k, i ^ c ^ (t >> 1)]
            got[k, i] = send(mine, ("c", "t"), memory_pairs(k, i))
    mem = [jnp.where(c == 0, got[k & 1, k >> 1], got[k & 1, (k >> 1) ^ 1]) for k in range(4)]
    cs0, cs1, _ = call(prep_rows_body, [rows16, rows16, ((2, D), F32)], (ids, cotangent, gains), name="prep_cotangent")
    cx0, cx1 = rows_to_sequences(cs0, cs1)
    (own_b,) = call(
        prep_b_body, [((NQ, RB, DP), BF)], (ids, gate_weight, up_weight, down_weight),
        scratch=[pltpu.VMEM((2 * HID, DP), BF)], name="prep_b",
    )
    wb = gather_weights(own_b)

    x_own, n1_own = call(norm_one_body, [half16, half16], (ids, x0, x1, rel_gains), name="norm_one")
    n1_oth = flip(n1_own, "c", 1)
    (cot_own,) = call(arrange_body, [half16], (ids, cx0, cx1), name="arrange")
    cot_oth = flip(cot_own, "c", 1)

    heads = [
        call(
            attention_body, [((LEN, 3 * HD), BF), ((LEN, HD), BF), ((LEN, HD), F32)],
            (ids, n1_own, n1_oth, *wa[j], mem[j]),
            flops=2 * 1024 * 1024 * 384 + 4 * 128 * 786432, trans=786432, name="attention",
        )
        for j in range(4)
    ]
    flat_a = [p for row in wa for p in row]
    flat_b = [p for row in wb for p in row]
    o_own, o_oth = call(
        out_proj_body, [half32, half16], (ids, *[h[1] for h in heads], *flat_a), flops=2 * 1024 * 512 * 1024,
        name="out_proj",
    )
    o_got = flip(o_oth, "c", 1)
    hidden, n2_own = call(norm_two_body, [half32, half16], (ids, x_own, o_own, o_got, rel_gains), name="norm_two")
    n2_oth = flip(n2_own, "c", 1)

    chunks = [
        call(
            functools.partial(ffn_body, PIECES[j]),
            [((2, RB, DP), BF), ((2, RB, DP), BF), ((HID, LEN), BF), ((2 * HID, LEN), BF)],
            (ids, n2_own, n2_oth, cot_own, cot_oth, *wb[j]),
            flops=6 * 2 * 1024 * 1024 * HID, trans=1024 * HID,
            scratch=[pltpu.VMEM((RB, D), BF)], name="ffn",
        )
        for j in range(4)
    ]
    d2_own, d2_oth = call(
        functools.partial(ffn_sum_body, 0, 2 * HID), [half32, half16], (ids, *[ch[3] for ch in chunks], *flat_b),
        flops=2 * 1024 * 1024 * 8 * HID, scratch=[pltpu.VMEM((HALF, D), F32)], name="ffn_back",
    )
    d2_got = flip(d2_oth, "c", 1)
    y_own, y_oth = call(
        functools.partial(ffn_sum_body, 2 * HID, 3 * HID), [half32, half16], (ids, *[ch[2] for ch in chunks], *flat_b),
        flops=2 * 1024 * 1024 * 4 * HID, scratch=[pltpu.VMEM((HALF, D), F32)], name="ffn_out",
    )
    y_got = flip(y_oth, "c", 1)
    grad_hidden, low_own, gain_two = call(
        norm_two_back_body, [half32, half16, ((1, D), F32)], (ids, d2_own, d2_got, cot_own, hidden, rel_gains),
        name="norm_two_back",
    )
    low_oth = flip(low_own, "c", 1)
    os0, os1 = call(output_body, [rows16, rows16], (ids, hidden, y_own, y_got), name="output")
    ob0, ob1 = rows_back(os0, os1)
    (output,) = call(unprep_rows_body, [((MICRO, 256, D), BF)], (ids, ob0, ob1), name="unprep_output")

    sums_b = [plane_sum(j, ch[0], ch[1]) for j, ch in enumerate(chunks)]
    backs = [
        call(
            functools.partial(attention_back_body, PIECES[j]),
            [((2, RA, DP), BF), ((2, RA, DP), BF), ((HALF, 3 * HD), BF), ((HALF, 3 * HD), BF)],
            (ids, low_own, low_oth, n1_own, n1_oth, *wa[j], *heads[j], mem[j]),
            flops=2 * 1024 * 1024 * 640 + 10 * 128 * 786432, trans=786432,
            scratch=[
                pltpu.VMEM((LEN, HD), BF), pltpu.VMEM((LEN, HD), F32), pltpu.VMEM((LEN, HD), F32),
                pltpu.VMEM((LEN, 3 * HD), BF),
            ],
            name="attention_back",
        )
        for j in range(4)
    ]
    total_b = column_sum(sums_b)
    b_own, b_oth = spread(total_b, True)
    sums_a = [plane_sum(j, bk[0], bk[1]) for j, bk in enumerate(backs)]
    d1_own, d1_oth = call(
        in_proj_back_body, [half32, half16], (ids, *[p for bk in backs for p in bk[2:]], *flat_a),
        flops=2 * 1024 * 1024 * 1536, name="in_proj_back",
    )
    d1_got = flip(d1_oth, "c", 1)
    gs0, gs1, gain_one = call(
        norm_one_back_body, [rows16, rows16, ((1, D), F32)], (ids, d1_own, d1_got, grad_hidden, x_own, rel_gains),
        name="norm_one_back",
    )
    gb0, gb1 = rows_back(gs0, gs1)
    (grad_tokens,) = call(unprep_rows_body, [((MICRO, 256, D), BF)], (ids, gb0, gb1), name="unprep_grad")
    total_a = column_sum(sums_a)
    a_own, a_oth = spread(total_a, False)

    wide, tall = ((D, 2 * HID), F32), ((2 * HID, D), F32)
    gg, gu, gd = call(
        place_b_body, [wide, wide, tall], (ids, *b_own, *b_oth), scratch=[pltpu.VMEM((2 * HID, DP), F32)], name="place_b"
    )
    col, row = ((D, 2 * HD), F32), ((2 * HD, D), F32)
    gq, gk, gv, go = call(place_a_body, [col, col, col, row], (ids, *a_own, *a_oth), name="place_a")
    gain_sums = lax.psum(jnp.concatenate((gain_one, gain_two)), ("r", "q", "c", "t"))
    return output, grad_tokens, gq, gk, gv, go, gg, gu, gd, gain_sums[0], gain_sums[1]


def solution(mesh):
    n_dp, n_t = mesh.shape["dp"], mesh.shape["tensor"]
    fine = Mesh(mesh.devices.reshape(n_dp // 8, NQ, 2, n_t), ("r", "q", "c", "t"))
    dp = ("r", "q", "c")
    rows = P(None, dp + ("t",), None)
    placed = (
        rows, P(), P(), P(None, "t"), P(None, "t"), P(None, "t"), P("t", None), P(None, "t"), P(None, "t"),
        P("t", None), P(None, dp, "t"), P(None, dp, "t"), P(None, dp, "t", None), rows,
    )
    return jax.shard_map(
        per_device,
        mesh=fine,
        in_specs=placed,
        out_specs=(
            rows, rows, P(None, "t"), P(None, "t"), P(None, "t"), P("t", None), P(None, "t"), P(None, "t"),
            P("t", None), P(), P(),
        ),
        check_vma=False,
    )
```

time: 1100 us -> 612 us (0.56)
  waiting for transfers between devices: 689 us -> 202 us
  Pallas kernels: 0 us -> 190 us
  matrix products: 188 us -> 0 us
  starting transfers between devices: 4.5 us -> 135 us
  local copies, waits for them, and re-layouts: 92.3 us -> 20.1 us
  other arithmetic: 74.5 us -> 13.8 us
  blocking collectives: 26.1 us -> 44.1 us
  between operations: 15.9 us -> 1.52 us
    all_gather x8 -> x0, waiting for transfers between devices: 284 us -> none  [the longest x4 154 us: whole_grads(): return lax.all_gather(grads, 'tensor', axis=0, tiled=True)]
    reduce_scatter x8 -> x0, waiting for transfers between devices: 225 us -> none  [the longest x4 120 us: sum_rows(): lax.psum_scatter(product(factor, weight).astype(jnp.bfloat16), 'tensor',...]
    ppermute x2 -> x81, waiting for transfers between devices: 1.83 us -> 202 us  [send(): return lax.ppermute(value, axis, pairs)]
    pallas_call x0 -> x31, Pallas kernels: none -> 190 us  [call(): pl.pallas_call(body, out_shape=[jax.ShapeDtypeStruct(s, t) for s, t in ou...]
    dot_general x82 -> x0, matrix products: 188 us -> none  [the longest x14 41.5 us: product(): return jnp.dot(first_arg, second_arg, preferred_element_type=jnp.float32)]
    psum x1 -> x0, waiting for transfers between devices: 176 us -> none  [per_device(): lax.psum((grad_q_total, grad_k_total, grad_v_total, grad_o_total, grad_ga...]
    ppermute x2 -> x81, starting transfers between devices: 3.19 us -> 135 us  [send(): return lax.ppermute(value, axis, pairs)]
    unnamed x345 -> x116, local copies, waits for them, and re-layouts: 38.4 us -> 14.2 us
  transfers between devices with their start and end apart: 19 -> 81, of which waited for: 17 -> 29; matrix products, arithmetic and copies ran while one was open for 17% -> 4% of each run, Pallas kernels for 0% -> 27%
where the time goes in v1:
time: 612 us; the launch traced here: 606 us
  waiting for transfers between devices  202 us (33%)
  Pallas kernels  190 us (31%)
  starting transfers between devices  135 us (22%)
  blocking collectives  44.1 us (7%)
  local copies, waits for them, and re-layouts  20.1 us (3%)
  other arithmetic  13.8 us (2%)
    ppermute x81, waiting for transfers between devices, send(): return lax.ppermute(value, axis, pairs)  202 us
    pallas_call x31, Pallas kernels, call(): pl.pallas_call(body, out_shape=[jax.ShapeDtypeStruct(s, t) for s, t in ou...  190 us
    ppermute x81, starting transfers between devices, send(): return lax.ppermute(value, axis, pairs)  135 us
    psum x1, blocking collectives, per_device(): lax.psum(jnp.concatenate((gain_one, gain_two)), ('r', 'q', 'c', 't'))  44.1 us
    unnamed x116, local copies, waits for them, and re-layouts  14.2 us
  transfers between devices with their start and end apart: 81, of which 29 were waited for; matrix products, arithmetic and copies ran while one was open for 4% of the time, Pallas kernels for 27%

profile of v1, /device:TPU:0, one launch (start us, length us, event | category | flops | bytes accessed | tf_op | source)
XLA Modules:
  0.0 606.4 jit_solution(6351938180278453246)
XLA Ops:
  15.1 7.3 %collective-permute-done.1.r1 = bf16[256,1024]{1,0:T(8,128)(2,1)S(1)} collective-permute-done((bf16[256,1024]{1,0:T(8,128)(2,1)}, bf16[256,1024]{1,0:T(8,128)(2,1)S(1)}, u32[]{:S(2)}, u32[]{:S(2)}) %collective-permute-start.1) | collective-permute-done | bytes 524320 | tf_op jit(solution)/shard_map/ppermute | solution.py:371
  25.9 7.2 %collective-permute-start.2 = (bf16[512,1024]{1,0:T(8,128)(2,1)}, bf16[512,1024]{1,0:T(8,128)(2,1)}, u32[]{:S(2)}, u32[]{:S(2)}) collective-permute-start(bf16[512,1024]{1,0:T(8,128)(2,1)} %get-tuple-element.91.n_own), channel_id=1, source_target_pairs={{0,4},{4,0},{1,5},{5,1},{2,6},{6,2},{3,7},{7,3},{8,12},{12,8},{9,1... | collective-permute-start | bytes 3145736 | tf_op jit(solution)/shard_map/ppermute | solution.py:371
  34.0 8.0 %collective-permute-start.12 = (bf16[512,256]{1,0:T(8,128)(2,1)S(1)}, bf16[512,256]{1,0:T(8,128)(2,1)S(1)}, u32[]{:S(2)}, u32[]{:S(2)}) collective-permute-start(bf16[512,256]{1,0:T(8,128)(2,1)S(1)} %get-tuple-element.185.w0.refs_0_.refs_8_), channel_id=1, source_target_pairs={{0,2},{1,3},{2,0},{3,1},{4,6},{5,7},{6,4},{7,5},{8,10},{9,11},{10,... | collective-permute-start | bytes 786440 | tf_op jit(solution)/shard_map/ppermute | solution.py:371
  42.6 17.5 %collective-permute-done.12.w0.refs_8_.refs_16_ = bf16[512,256]{1,0:T(8,128)(2,1)S(1)} collective-permute-done((bf16[512,256]{1,0:T(8,128)(2,1)S(1)}, bf16[512,256]{1,0:T(8,128)(2,1)S(1)}, u32[]{:S(2)}, u32[]{:S(2)}) %collective-permute-start.12) | collective-permute-done | bytes 262176 | tf_op jit(solution)/shard_map/ppermute | solution.py:371
  73.6 5.5 collective-permute-done.11
  87.9 4.7 prep_b.1
  100.7 6.5 %attention.6 = (bf16[1024,384]{1,0:T(8,128)(2,1)}, bf16[1024,128]{1,0:T(8,128)(2,1)}, f32[1024,128]{1,0:T(8,128)}) custom-call(s32[3]{0:T(128)} %pad_add_fusion.ids, bf16[512,1024]{1,0:T(8,128)(2,1)} %get-tuple-element.91.n_own, bf16[512,1024]{1,0:T(8,128)(2,1)} %collective-permute-done.2.n_oth, bf16[512,256]{1,0:T(8,128)(2,1)} %copy-done.45, ...), custom_call_target="tpu_custom_call" | custom-call | flops 1207959552 | bytes 4980748 | tf_op jit(solution)/shard_map/attention/pallas_call | solution.py:52
  107.2 4.7 collective-permute-done.8.w2.refs_6_.refs_14_
  111.9 5.4 collective-permute-done.9.w3.refs_7_.refs_15_
  118.0 6.5 %attention.5 = (bf16[1024,384]{1,0:T(8,128)(2,1)}, bf16[1024,128]{1,0:T(8,128)(2,1)}, f32[1024,128]{1,0:T(8,128)}) custom-call(s32[3]{0:T(128)} %pad_add_fusion.ids, bf16[512,1024]{1,0:T(8,128)(2,1)} %get-tuple-element.91.n_own, bf16[512,1024]{1,0:T(8,128)(2,1)} %collective-permute-done.2.n_oth, bf16[512,256]{1,0:T(8,128)(2,1)} %collective-permute-done.6.w0.refs_4_.refs_12_, ...), custom_call_target="tpu_custom_call" | custom-call | flops 1207959552 | bytes 4980748 | tf_op jit(solution)/shard_map/attention/pallas_call | solution.py:52
  125.4 6.5 %attention.7 = (bf16[1024,384]{1,0:T(8,128)(2,1)}, bf16[1024,128]{1,0:T(8,128)(2,1)}, f32[1024,128]{1,0:T(8,128)}) custom-call(s32[3]{0:T(128)} %pad_add_fusion.ids, bf16[512,1024]{1,0:T(8,128)(2,1)} %get-tuple-element.91.n_own, bf16[512,1024]{1,0:T(8,128)(2,1)} %collective-permute-done.2.n_oth, bf16[512,256]{1,0:T(8,128)(2,1)} %copy-done.46, ...), custom_call_target="tpu_custom_call" | custom-call | flops 1207959552 | bytes 4980748 | tf_op jit(solution)/shard_map/attention/pallas_call | solution.py:52
  131.9 6.9 %attention.4 = (bf16[1024,384]{1,0:T(8,128)(2,1)}, bf16[1024,128]{1,0:T(8,128)(2,1)}, f32[1024,128]{1,0:T(8,128)}) custom-call(s32[3]{0:T(128)} %pad_add_fusion.ids, bf16[512,1024]{1,0:T(8,128)(2,1)} %get-tuple-element.91.n_own, bf16[512,1024]{1,0:T(8,128)(2,1)} %collective-permute-done.2.n_oth, bf16[512,256]{1,0:T(8,128)(2,1)} %copy-done.15, ...), custom_call_target="tpu_custom_call" | custom-call | flops 1207959552 | bytes 4980748 | tf_op jit(solution)/shard_map/attention/pallas_call | solution.py:52
  138.8 5.2 out_proj.1
  149.8 5.4 collective-permute-start.22
  163.5 8.0 %collective-permute-done.23.r1 = bf16[256,1024]{1,0:T(8,128)(2,1)} collective-permute-done((bf16[256,1024]{1,0:T(8,128)(2,1)}, bf16[256,1024]{1,0:T(8,128)(2,1)}, u32[]{:S(2)}, u32[]{:S(2)}) %collective-permute-start.23) | collective-permute-done | bytes 524320 | tf_op jit(solution)/shard_map/ppermute | solution.py:371
  174.4 37.3 %collective-permute-start.24 = (bf16[512,1024]{1,0:T(8,128)(2,1)}, bf16[512,1024]{1,0:T(8,128)(2,1)}, u32[]{:S(2)}, u32[]{:S(2)}) collective-permute-start(bf16[512,1024]{1,0:T(8,128)(2,1)} %arrange.1.c_own.cot), channel_id=1, source_target_pairs={{0,4},{4,0},{1,5},{5,1},{2,6},{6,2},{3,7},{7,3},{8,12},{12,8},{9,1... | collective-permute-start | bytes 3145736 | tf_op jit(solution)/shard_map/ppermute | solution.py:371
  211.6 4.2 norm_two.1
  222.0 11.2 %collective-permute-done.34.w1.refs_17_ = bf16[1056,256]{1,0:T(8,128)(2,1)S(1)} collective-permute-done((bf16[1056,256]{1,0:T(8,128)(2,1)S(1)}, bf16[1056,256]{1,0:T(8,128)(2,1)S(1)}, u32[]{:S(2)}, u32[]{:S(2)}) %collective-permute-start.34) | collective-permute-done | bytes 540704 | tf_op jit(solution)/shard_map/ppermute | solution.py:371
  235.6 9.3 %collective-permute-done.26.w1.refs_9_ = bf16[1056,256]{1,0:T(8,128)(2,1)} collective-permute-done((bf16[1056,256]{1,0:T(8,128)(2,1)S(1)}, bf16[1056,256]{1,0:T(8,128)(2,1)}, u32[]{:S(2)}, u32[]{:S(2)}) %collective-permute-start.26) | collective-permute-done | bytes 540704 | tf_op jit(solution)/shard_map/ppermute | solution.py:371
  246.9 8.9 %ffn.7 = (bf16[2,1056,256]{2,1,0:T(8,128)(2,1)}, bf16[2,1056,256]{2,1,0:T(8,128)(2,1)}, bf16[352,1024]{1,0:T(8,128)(2,1)}, bf16[704,1024]{1,0:T(8,128)(2,1)}) custom-call(s32[3]{0:T(128)} %pad_add_fusion.ids, bf16[512,1024]{1,0:T(8,128)(2,1)} %get-tuple-element.99.n_own, bf16[512,1024]{1,0:T(8,128)(2,1)} %collective-permute-done.21.n_oth, ...), custom_call_target="tpu_custom_call" | custom-call | flops 4429185024 | bytes 10682380 | tf_op jit(solution)/shard_map/ffn/pallas_call | solution.py:52
  256.6 11.5 %collective-permute-done.32.w3.refs_15_ = bf16[1056,256]{1,0:T(8,128)(2,1)} collective-permute-done((bf16[1056,256]{1,0:T(8,128)(2,1)}, bf16[1056,256]{1,0:T(8,128)(2,1)}, u32[]{:S(2)}, u32[]{:S(2)}) %collective-permute-start.32) | collective-permute-done | bytes 540704 | tf_op jit(solution)/shard_map/ppermute | solution.py:371
  268.0 9.0 %ffn.6 = (bf16[2,1056,256]{2,1,0:T(8,128)(2,1)}, bf16[2,1056,256]{2,1,0:T(8,128)(2,1)}, bf16[352,1024]{1,0:T(8,128)(2,1)}, bf16[704,1024]{1,0:T(8,128)(2,1)}) custom-call(s32[3]{0:T(128)} %pad_add_fusion.ids, bf16[512,1024]{1,0:T(8,128)(2,1)} %get-tuple-element.99.n_own, bf16[512,1024]{1,0:T(8,128)(2,1)} %collective-permute-done.21.n_oth, ...), custom_call_target="tpu_custom_call" | custom-call | flops 4429185024 | bytes 10682380 | tf_op jit(solution)/shard_map/ffn/pallas_call | solution.py:52
  277.1 9.1 %ffn.5 = (bf16[2,1056,256]{2,1,0:T(8,128)(2,1)}, bf16[2,1056,256]{2,1,0:T(8,128)(2,1)}, bf16[352,1024]{1,0:T(8,128)(2,1)}, bf16[704,1024]{1,0:T(8,128)(2,1)}) custom-call(s32[3]{0:T(128)} %pad_add_fusion.ids, bf16[512,1024]{1,0:T(8,128)(2,1)} %get-tuple-element.99.n_own, bf16[512,1024]{1,0:T(8,128)(2,1)} %collective-permute-done.21.n_oth, ...), custom_call_target="tpu_custom_call" | custom-call | flops 4429185024 | bytes 10682380 | tf_op jit(solution)/shard_map/ffn/pallas_call | solution.py:52
  286.1 8.9 %ffn.4 = (bf16[2,1056,256]{2,1,0:T(8,128)(2,1)}, bf16[2,1056,256]{2,1,0:T(8,128)(2,1)}, bf16[352,1024]{1,0:T(8,128)(2,1)}, bf16[704,1024]{1,0:T(8,128)(2,1)}) custom-call(s32[3]{0:T(128)} %pad_add_fusion.ids, bf16[512,1024]{1,0:T(8,128)(2,1)} %get-tuple-element.99.n_own, bf16[512,1024]{1,0:T(8,128)(2,1)} %collective-permute-done.21.n_oth, ...), custom_call_target="tpu_custom_call" | custom-call | flops 4429185024 | bytes 10682380 | tf_op jit(solution)/shard_map/ffn/pallas_call | solution.py:52
  295.0 13.1 %ffn_back.1 = (f32[512,1024]{1,0:T(8,128)}, bf16[512,1024]{1,0:T(8,128)(2,1)}) custom-call(s32[3]{0:T(128)} %pad_add_fusion.ids, bf16[704,1024]{1,0:T(8,128)(2,1)} %get-tuple-element.110.refs_0_, bf16[704,1024]{1,0:T(8,128)(2,1)} %get-tuple-element.111.refs_1_, bf16[704,1024]{1,0:T(8,128)(2,1)} %get-tuple-element.112.refs_2_, ...), custom_call_target="tpu_custom_call" | custom-call | flops 5905580032 | bytes 17563660 | tf_op jit(solution)/shard_map/ffn_back/pallas_call | solution.py:52
  309.5 10.5 %ffn_out.1 = (f32[512,1024]{1,0:T(8,128)}, bf16[512,1024]{1,0:T(8,128)(2,1)}) custom-call(s32[3]{0:T(128)} %pad_add_fusion.ids, bf16[352,1024]{1,0:T(8,128)(2,1)} %get-tuple-element.102.refs_0_, bf16[352,1024]{1,0:T(8,128)(2,1)} %get-tuple-element.103.refs_1_, bf16[352,1024]{1,0:T(8,128)(2,1)} %get-tuple-element.104.refs_2_, ...), custom_call_target="tpu_custom_call" | custom-call | flops 2952790016 | bytes 14680076 | tf_op jit(solution)/shard_map/ffn_out/pallas_call | solution.py:52
  322.9 5.6 norm_two_back.1
  332.3 5.4 collective-permute-start.38
  338.0 9.3 %collective-permute-done.68 = bf16[2,1056,256]{2,1,0:T(8,128)(2,1)} collective-permute-done((bf16[2,1056,256]{2,1,0:T(8,128)(2,1)}, bf16[2,1056,256]{2,1,0:T(8,128)(2,1)}, u32[]{:S(2)}, u32[]{:S(2)}) %collective-permute-start.68) | collective-permute-done | bytes 1081376 | tf_op jit(solution)/shard_map/ppermute | solution.py:371
  352.6 17.8 %collective-permute-done.63 = bf16[2,1056,256]{2,1,0:T(8,128)(2,1)S(1)} collective-permute-done((bf16[2,1056,256]{2,1,0:T(8,128)(2,1)}, bf16[2,1056,256]{2,1,0:T(8,128)(2,1)S(1)}, u32[]{:S(2)}, u32[]{:S(2)}) %collective-permute-start.63) | collective-permute-done | bytes 1081376 | tf_op jit(solution)/shard_map/ppermute | solution.py:371
  372.4 9.5 %collective-permute-done.72 = bf16[1056,256]{1,0:T(8,128)(2,1)S(1)} collective-permute-done((bf16[1056,256]{1,0:T(8,128)(2,1)S(1)}, bf16[1056,256]{1,0:T(8,128)(2,1)S(1)}, u32[]{:S(2)}, u32[]{:S(2)}) %collective-permute-start.72) | collective-permute-done | bytes 540704 | tf_op jit(solution)/shard_map/ppermute | solution.py:371
  384.2 8.8 %collective-permute-done.66 = bf16[1056,256]{1,0:T(8,128)(2,1)S(1)} collective-permute-done((bf16[1056,256]{1,0:T(8,128)(2,1)S(1)}, bf16[1056,256]{1,0:T(8,128)(2,1)S(1)}, u32[]{:S(2)}, u32[]{:S(2)}) %collective-permute-start.66) | collective-permute-done | bytes 540704 | tf_op jit(solution)/shard_map/ppermute | solution.py:371
  395.2 8.8 %attention_back.7 = (bf16[2,512,256]{2,1,0:T(8,128)(2,1)}, bf16[2,512,256]{2,1,0:T(8,128)(2,1)}, bf16[512,384]{1,0:T(8,128)(2,1)}, bf16[512,384]{1,0:T(8,128)(2,1)}) custom-call(s32[3]{0:T(128)} %pad_add_fusion.ids, bf16[512,1024]{1,0:T(8,128)(2,1)} %get-tuple-element.116.g_own, bf16[512,1024]{1,0:T(8,128)(2,1)} %collective-permute-done.41.g_oth, ...), custom_call_target="tpu_custom_call" | custom-call | flops 2348810240 | bytes 8912908 | tf_op jit(solution)/shard_map/attention_back/pallas_call | solution.py:52
  404.0 9.0 %attention_back.6 = (bf16[2,512,256]{2,1,0:T(8,128)(2,1)}, bf16[2,512,256]{2,1,0:T(8,128)(2,1)}, bf16[512,384]{1,0:T(8,128)(2,1)}, bf16[512,384]{1,0:T(8,128)(2,1)}) custom-call(s32[3]{0:T(128)} %pad_add_fusion.ids, bf16[512,1024]{1,0:T(8,128)(2,1)} %get-tuple-element.116.g_own, bf16[512,1024]{1,0:T(8,128)(2,1)} %collective-permute-done.41.g_oth, ...), custom_call_target="tpu_custom_call" | custom-call | flops 2348810240 | bytes 8912908 | tf_op jit(solution)/shard_map/attention_back/pallas_call | solution.py:52
  413.0 9.0 %attention_back.5 = (bf16[2,512,256]{2,1,0:T(8,128)(2,1)}, bf16[2,512,256]{2,1,0:T(8,128)(2,1)}, bf16[512,384]{1,0:T(8,128)(2,1)}, bf16[512,384]{1,0:T(8,128)(2,1)}) custom-call(s32[3]{0:T(128)} %pad_add_fusion.ids, bf16[512,1024]{1,0:T(8,128)(2,1)} %get-tuple-element.116.g_own, bf16[512,1024]{1,0:T(8,128)(2,1)} %collective-permute-done.41.g_oth, ...), custom_call_target="tpu_custom_call" | custom-call | flops 2348810240 | bytes 8912908 | tf_op jit(solution)/shard_map/attention_back/pallas_call | solution.py:52
  421.9 8.9 %attention_back.4 = (bf16[2,512,256]{2,1,0:T(8,128)(2,1)}, bf16[2,512,256]{2,1,0:T(8,128)(2,1)}, bf16[512,384]{1,0:T(8,128)(2,1)}, bf16[512,384]{1,0:T(8,128)(2,1)}) custom-call(s32[3]{0:T(128)} %pad_add_fusion.ids, bf16[512,1024]{1,0:T(8,128)(2,1)} %get-tuple-element.116.g_own, bf16[512,1024]{1,0:T(8,128)(2,1)} %collective-permute-done.41.g_oth, ...), custom_call_target="tpu_custom_call" | custom-call | flops 2348810240 | bytes 8912908 | tf_op jit(solution)/shard_map/attention_back/pallas_call | solution.py:52
  430.9 8.0 %in_proj_back.1 = (f32[512,1024]{1,0:T(8,128)}, bf16[512,1024]{1,0:T(8,128)(2,1)}) custom-call(s32[3]{0:T(128)} %pad_add_fusion.ids, bf16[512,384]{1,0:T(8,128)(2,1)} %get-tuple-element.119.refs_0_, bf16[512,384]{1,0:T(8,128)(2,1)} %get-tuple-element.120.refs_1_, bf16[512,384]{1,0:T(8,128)(2,1)} %get-tuple-element.123.refs_2_, ...), custom_call_target="tpu_custom_call" | custom-call | flops 3221225472 | bytes 10485772 | tf_op jit(solution)/shard_map/in_proj_back/pallas_call | solution.py:52
  444.5 9.4 %collective-permute-done.47 = bf16[2,512,256]{2,1,0:T(8,128)(2,1)S(1)} collective-permute-done((bf16[2,512,256]{2,1,0:T(8,128)(2,1)}, bf16[2,512,256]{2,1,0:T(8,128)(2,1)S(1)}, u32[]{:S(2)}, u32[]{:S(2)}) %collective-permute-start.47) | collective-permute-done | bytes 524320 | tf_op jit(solution)/shard_map/ppermute | solution.py:371
  456.2 8.5 %collective-permute-done.50 = bf16[2,512,256]{2,1,0:T(8,128)(2,1)S(1)} collective-permute-done((bf16[2,512,256]{2,1,0:T(8,128)(2,1)}, bf16[2,512,256]{2,1,0:T(8,128)(2,1)S(1)}, u32[]{:S(2)}, u32[]{:S(2)}) %collective-permute-start.50) | collective-permute-done | bytes 524320 | tf_op jit(solution)/shard_map/ppermute | solution.py:371
  468.4 8.4 %collective-permute-done.75.refs_2_ = bf16[1056,256]{1,0:T(8,128)(2,1)S(1)} collective-permute-done((bf16[1056,256]{1,0:T(8,128)(2,1)S(1)}, bf16[1056,256]{1,0:T(8,128)(2,1)S(1)}, u32[]{:S(2)}, u32[]{:S(2)}) %collective-permute-start.75) | collective-permute-done | bytes 540704 | tf_op jit(solution)/shard_map/ppermute | solution.py:371
  478.6 4.1 collective-permute-done.48
  495.4 7.0 %collective-permute-done.52 = bf16[512,256]{1,0:T(8,128)(2,1)S(1)} collective-permute-done((bf16[512,256]{1,0:T(8,128)(2,1)S(1)}, bf16[512,256]{1,0:T(8,128)(2,1)S(1)}, u32[]{:S(2)}, u32[]{:S(2)}) %collective-permute-start.52) | collective-permute-done | bytes 262176 | tf_op jit(solution)/shard_map/ppermute | solution.py:371
  504.6 5.0 norm_one_back.1
  512.9 4.6 collective-permute-done.39.b1
  520.6 10.6 %collective-permute-done.57.refs_2_ = bf16[512,256]{1,0:T(8,128)(2,1)} collective-permute-done((bf16[512,256]{1,0:T(8,128)(2,1)S(1)}, bf16[512,256]{1,0:T(8,128)(2,1)}, u32[]{:S(2)}, u32[]{:S(2)}) %collective-permute-start.57) | collective-permute-done | bytes 262176 | tf_op jit(solution)/shard_map/ppermute | solution.py:371
  535.3 4.5 collective-permute-done.58.refs_3_
  541.0 44.1 %psum.7 = f32[2,1024]{1,0:T(2,128)S(1)} all-reduce(f32[2,1024]{1,0:T(2,128)S(1)} %pad_maximum_fusion.2), channel_id=1, replica_groups=mesh['r'=1,'q'=4,'c'=2,'t'=4] {'r','q','c','t'}, use_global_device_ids=true, to_apply=%region_0.1 | all-reduce | flops 2048 | bytes 16384 | tf_op jit(solution)/shard_map/psum | solution.py:571
  588.8 7.5 %place_b.1 = (f32[1024,704]{1,0:T(8,128)}, f32[1024,704]{1,0:T(8,128)}, f32[704,1024]{1,0:T(8,128)}) custom-call(s32[3]{0:T(128)} %pad_add_fusion.ids, bf16[1056,256]{1,0:T(8,128)(2,1)} %copy-done.3, bf16[1056,256]{1,0:T(8,128)(2,1)} %collective-permute-done.74.refs_1_, bf16[1056,256]{1,0:T(8,128)(2,1)} %copy-done.16, bf16[1056,256]{1,0:T(8,128)(2,1)} %copy-done.22, ...), custom_call_target="tpu_custom_call" | custom-call | bytes 12976140 | tf_op jit(solution)/shard_map/place_b/pallas_call | solution.py:52
  (296 shorter events, 152.9 us)
Async XLA Ops:
  9.8 51.9 %collective-permute-start.3 = (bf16[2,2,256,256]{3,2,1,0:T(8,128)(2,1)S(1)}, bf16[2,2,256,256]{3,2,1,0:T(8,128)(2,1)S(1)}, u32[]{:S(2)}, u32[]{:S(2)}) collective-permute-start(bf16[2,2,256,256]{3,2,1,0:T(8,128)(2,1)S(1)} %pad_maximum_fusion.own), channel_id=1, source_target_pairs={{0,4},{4,8},{8,12},{12,16},{16,20},{20,24},{24,28},{28,0},{1,5},{5... | collective-permute-start | bytes 1572872 | tf_op jit(solution)/shard_map/ppermute | solution.py:371
  25.9 71.4 %collective-permute-start.2 = (bf16[512,1024]{1,0:T(8,128)(2,1)}, bf16[512,1024]{1,0:T(8,128)(2,1)}, u32[]{:S(2)}, u32[]{:S(2)}) collective-permute-start(bf16[512,1024]{1,0:T(8,128)(2,1)} %get-tuple-element.91.n_own), channel_id=1, source_target_pairs={{0,4},{4,0},{1,5},{5,1},{2,6},{6,2},{3,7},{7,3},{8,12},{12,8},{9,1... | collective-permute-start | bytes 3145736 | tf_op jit(solution)/shard_map/ppermute | solution.py:371
  34.0 26.2 %collective-permute-start.12 = (bf16[512,256]{1,0:T(8,128)(2,1)S(1)}, bf16[512,256]{1,0:T(8,128)(2,1)S(1)}, u32[]{:S(2)}, u32[]{:S(2)}) collective-permute-start(bf16[512,256]{1,0:T(8,128)(2,1)S(1)} %get-tuple-element.185.w0.refs_0_.refs_8_), channel_id=1, source_target_pairs={{0,2},{1,3},{2,0},{3,1},{4,6},{5,7},{6,4},{7,5},{8,10},{9,11},{10,... | collective-permute-start | bytes 786440 | tf_op jit(solution)/shard_map/ppermute | solution.py:371
  42.0 26.8 %collective-permute-start.16 = (bf16[512,256]{1,0:T(8,128)(2,1)S(1)}, bf16[512,256]{1,0:T(8,128)(2,1)S(1)}, u32[]{:S(2)}, u32[]{:S(2)}) collective-permute-start(bf16[512,256]{1,0:T(8,128)(2,1)S(1)} %get-tuple-element.185.w0.refs_0_.refs_8_), channel_id=1, source_target_pairs={{0,3},{1,2},{2,1},{3,0},{4,7},{5,6},{6,5},{7,4},{8,11},{9,10},{10,... | collective-permute-start | bytes 786440 | tf_op jit(solution)/shard_map/ppermute | solution.py:371
  42.6 26.8 %collective-permute-start.6 = (bf16[512,256]{1,0:T(8,128)(2,1)S(1)}, bf16[512,256]{1,0:T(8,128)(2,1)}, u32[]{:S(2)}, u32[]{:S(2)}) collective-permute-start(bf16[512,256]{1,0:T(8,128)(2,1)S(1)} %get-tuple-element.185.w0.refs_0_.refs_8_), channel_id=1, source_target_pairs={{0,1},{1,0},{2,3},{3,2},{4,5},{5,4},{6,7},{7,6},{8,9},{9,8},{10,11... | collective-permute-start | bytes 786440 | tf_op jit(solution)/shard_map/ppermute | solution.py:371
  70.6 22.8 %collective-permute-start.7 = (bf16[512,256]{1,0:T(8,128)(2,1)}, bf16[512,256]{1,0:T(8,128)(2,1)}, u32[]{:S(2)}, u32[]{:S(2)}) collective-permute-start(bf16[512,256]{1,0:T(8,128)(2,1)} %collective-permute-done.6.w0.refs_4_.refs_12_), channel_id=1, source_target_pairs={{0,8},{8,0},{16,24},{24,16},{1,9},{9,1},{17,25},{25,17},{2,10},{10... | collective-permute-start | bytes 786440 | tf_op jit(solution)/shard_map/ppermute | solution.py:371
  71.7 22.5 %collective-permute-start.5 = (bf16[1024,128]{1,0:T(8,128)(2,1)}, bf16[1024,128]{1,0:T(8,128)(2,1)S(1)}, u32[]{:S(2)}, u32[]{:S(2)}) collective-permute-start(bf16[1024,128]{1,0:T(8,128)(2,1)} %get-tuple-element.180), channel_id=1, source_target_pairs={{0,4},{1,5},{2,0},{3,1},{4,2},{5,3},{6,6},{7,7},{8,12},{9,13},{10,... | collective-permute-start | bytes 786440 | tf_op jit(solution)/shard_map/ppermute | solution.py:371
  93.4 31.1 %collective-permute-start.19 = (bf16[512,256]{1,0:T(8,128)(2,1)S(1)}, bf16[512,256]{1,0:T(8,128)(2,1)S(1)}, u32[]{:S(2)}, u32[]{:S(2)}) collective-permute-start(bf16[512,256]{1,0:T(8,128)(2,1)S(1)} %copy-done.47), channel_id=1, source_target_pairs={{0,24},{8,16},{16,8},{24,0},{1,25},{9,17},{17,9},{25,1},{2,26},{10... | collective-permute-start | bytes 786440 | tf_op jit(solution)/shard_map/ppermute | solution.py:371
  94.2 30.3 %collective-permute-start.18 = (bf16[512,256]{1,0:T(8,128)(2,1)S(1)}, bf16[512,256]{1,0:T(8,128)(2,1)S(1)}, u32[]{:S(2)}, u32[]{:S(2)}) collective-permute-start(bf16[512,256]{1,0:T(8,128)(2,1)S(1)} %copy-done.47), channel_id=1, source_target_pairs={{0,16},{8,24},{16,0},{24,8},{1,17},{9,25},{17,1},{25,9},{2,18},{10... | collective-permute-start | bytes 786440 | tf_op jit(solution)/shard_map/ppermute | solution.py:371
  95.8 28.7 %collective-permute-start.17 = (bf16[512,256]{1,0:T(8,128)(2,1)S(1)}, bf16[512,256]{1,0:T(8,128)(2,1)S(1)}, u32[]{:S(2)}, u32[]{:S(2)}) collective-permute-start(bf16[512,256]{1,0:T(8,128)(2,1)S(1)} %copy-done.47), channel_id=1, source_target_pairs={{0,8},{8,0},{16,24},{24,16},{1,9},{9,1},{17,25},{25,17},{2,10},{10... | collective-permute-start | bytes 786440 | tf_op jit(solution)/shard_map/ppermute | solution.py:371
  144.0 30.4 %collective-permute-start.20 = (bf16[512,1024]{1,0:T(8,128)(2,1)}, bf16[512,1024]{1,0:T(8,128)(2,1)}, u32[]{:S(2)}, u32[]{:S(2)}) collective-permute-start(bf16[512,1024]{1,0:T(8,128)(2,1)} %get-tuple-element.97), channel_id=1, source_target_pairs={{0,4},{4,0},{1,5},{5,1},{2,6},{6,2},{3,7},{7,3},{8,12},{12,8},{9,1... | collective-permute-start | bytes 3145736 | tf_op jit(solution)/shard_map/ppermute | solution.py:371
  156.3 62.8 %collective-permute-start.29 = (bf16[1056,256]{1,0:T(8,128)(2,1)S(1)}, bf16[1056,256]{1,0:T(8,128)(2,1)S(1)}, u32[]{:S(2)}, u32[]{:S(2)}) collective-permute-start(bf16[1056,256]{1,0:T(8,128)(2,1)S(1)} %get-tuple-element.177.w0.refs_4_), channel_id=1, source_target_pairs={{0,2},{1,3},{2,0},{3,1},{4,6},{5,7},{6,4},{7,5},{8,10},{9,11},{10,... | collective-permute-start | bytes 1622024 | tf_op jit(solution)/shard_map/ppermute | solution.py:371
  156.3 62.8 %collective-permute-start.25 = (bf16[1056,256]{1,0:T(8,128)(2,1)S(1)}, bf16[1056,256]{1,0:T(8,128)(2,1)S(1)}, u32[]{:S(2)}, u32[]{:S(2)}) collective-permute-start(bf16[1056,256]{1,0:T(8,128)(2,1)S(1)} %get-tuple-element.177.w0.refs_4_), channel_id=1, source_target_pairs={{0,1},{1,0},{2,3},{3,2},{4,5},{5,4},{6,7},{7,6},{8,9},{9,8},{10,11... | collective-permute-start | bytes 1622024 | tf_op jit(solution)/shard_map/ppermute | solution.py:371
  162.4 57.8 %collective-permute-start.36 = (bf16[1056,256]{1,0:T(8,128)(2,1)S(1)}, bf16[1056,256]{1,0:T(8,128)(2,1)S(1)}, u32[]{:S(2)}, u32[]{:S(2)}) collective-permute-start(bf16[1056,256]{1,0:T(8,128)(2,1)S(1)} %collective-permute-done.33.w0.refs_16_), channel_id=1, source_target_pairs={{0,24},{8,16},{16,8},{24,0},{1,25},{9,17},{17,9},{25,1},{2,26},{10... | collective-permute-start | bytes 1622024 | tf_op jit(solution)/shard_map/ppermute | solution.py:371
  171.6 49.4 %collective-permute-start.35 = (bf16[1056,256]{1,0:T(8,128)(2,1)S(1)}, bf16[1056,256]{1,0:T(8,128)(2,1)S(1)}, u32[]{:S(2)}, u32[]{:S(2)}) collective-permute-start(bf16[1056,256]{1,0:T(8,128)(2,1)S(1)} %collective-permute-done.33.w0.refs_16_), channel_id=1, source_target_pairs={{0,16},{8,24},{16,0},{24,8},{1,17},{9,25},{17,1},{25,9},{2,18},{10... | collective-permute-start | bytes 1622024 | tf_op jit(solution)/shard_map/ppermute | solution.py:371
  174.4 71.1 %collective-permute-start.24 = (bf16[512,1024]{1,0:T(8,128)(2,1)}, bf16[512,1024]{1,0:T(8,128)(2,1)}, u32[]{:S(2)}, u32[]{:S(2)}) collective-permute-start(bf16[512,1024]{1,0:T(8,128)(2,1)} %arrange.1.c_own.cot), channel_id=1, source_target_pairs={{0,4},{4,0},{1,5},{5,1},{2,6},{6,2},{3,7},{7,3},{8,12},{12,8},{9,1... | collective-permute-start | bytes 3145736 | tf_op jit(solution)/shard_map/ppermute | solution.py:371
  219.2 27.7 %collective-permute-start.21 = (bf16[512,1024]{1,0:T(8,128)(2,1)}, bf16[512,1024]{1,0:T(8,128)(2,1)}, u32[]{:S(2)}, u32[]{:S(2)}) collective-permute-start(bf16[512,1024]{1,0:T(8,128)(2,1)} %get-tuple-element.99.n_own), channel_id=1, source_target_pairs={{0,4},{4,0},{1,5},{5,1},{2,6},{6,2},{3,7},{7,3},{8,12},{12,8},{9,1... | collective-permute-start | bytes 3145736 | tf_op jit(solution)/shard_map/ppermute | solution.py:371
  221.0 23.9 %collective-permute-start.26 = (bf16[1056,256]{1,0:T(8,128)(2,1)S(1)}, bf16[1056,256]{1,0:T(8,128)(2,1)}, u32[]{:S(2)}, u32[]{:S(2)}) collective-permute-start(bf16[1056,256]{1,0:T(8,128)(2,1)S(1)} %collective-permute-done.25.w0.refs_8_), channel_id=1, source_target_pairs={{0,8},{8,0},{16,24},{24,16},{1,9},{9,1},{17,25},{25,17},{2,10},{10... | collective-permute-start | bytes 1622024 | tf_op jit(solution)/shard_map/ppermute | solution.py:371
  233.2 23.4 %collective-permute-start.30 = (bf16[1056,256]{1,0:T(8,128)(2,1)S(1)}, bf16[1056,256]{1,0:T(8,128)(2,1)S(1)}, u32[]{:S(2)}, u32[]{:S(2)}) collective-permute-start(bf16[1056,256]{1,0:T(8,128)(2,1)S(1)} %collective-permute-done.29.w0.refs_12_), channel_id=1, source_target_pairs={{0,8},{8,0},{16,24},{24,16},{1,9},{9,1},{17,25},{25,17},{2,10},{10... | collective-permute-start | bytes 1622024 | tf_op jit(solution)/shard_map/ppermute | solution.py:371
  234.5 33.5 %collective-permute-start.32 = (bf16[1056,256]{1,0:T(8,128)(2,1)}, bf16[1056,256]{1,0:T(8,128)(2,1)}, u32[]{:S(2)}, u32[]{:S(2)}) collective-permute-start(bf16[1056,256]{1,0:T(8,128)(2,1)} %collective-permute-done.31.w2.refs_14_), channel_id=1, source_target_pairs={{0,8},{8,0},{16,24},{24,16},{1,9},{9,1},{17,25},{25,17},{2,10},{10... | collective-permute-start | bytes 1622024 | tf_op jit(solution)/shard_map/ppermute | solution.py:371
  244.9 32.2 %collective-permute-start.27 = (bf16[1056,256]{1,0:T(8,128)(2,1)S(1)}, bf16[1056,256]{1,0:T(8,128)(2,1)}, u32[]{:S(2)}, u32[]{:S(2)}) collective-permute-start(bf16[1056,256]{1,0:T(8,128)(2,1)S(1)} %collective-permute-done.25.w0.refs_8_), channel_id=1, source_target_pairs={{0,16},{8,24},{16,0},{24,8},{1,17},{9,25},{17,1},{25,9},{2,18},{10... | collective-permute-start | bytes 1622024 | tf_op jit(solution)/shard_map/ppermute | solution.py:371
  245.5 31.6 %collective-permute-start.28 = (bf16[1056,256]{1,0:T(8,128)(2,1)}, bf16[1056,256]{1,0:T(8,128)(2,1)}, u32[]{:S(2)}, u32[]{:S(2)}) collective-permute-start(bf16[1056,256]{1,0:T(8,128)(2,1)} %collective-permute-done.26.w1.refs_9_), channel_id=1, source_target_pairs={{0,16},{8,24},{16,0},{24,8},{1,17},{9,25},{17,1},{25,9},{2,18},{10... | collective-permute-start | bytes 1622024 | tf_op jit(solution)/shard_map/ppermute | solution.py:371
  255.9 76.4 %collective-permute-start.71 = (bf16[2,1056,256]{2,1,0:T(8,128)(2,1)}, bf16[2,1056,256]{2,1,0:T(8,128)(2,1)S(1)}, u32[]{:S(2)}, u32[]{:S(2)}) collective-permute-start(bf16[2,1056,256]{2,1,0:T(8,128)(2,1)} %get-tuple-element.157), channel_id=1, source_target_pairs={{0,16},{8,24},{16,0},{24,8},{1,17},{9,25},{17,1},{25,9},{2,18},{10... | collective-permute-start | bytes 3244040 | tf_op jit(solution)/shard_map/ppermute | solution.py:371
  320.2 27.1 %collective-permute-start.68 = (bf16[2,1056,256]{2,1,0:T(8,128)(2,1)}, bf16[2,1056,256]{2,1,0:T(8,128)(2,1)}, u32[]{:S(2)}, u32[]{:S(2)}) collective-permute-start(bf16[2,1056,256]{2,1,0:T(8,128)(2,1)} %get-tuple-element.155), channel_id=1, source_target_pairs={{0,8},{8,0},{16,24},{24,16},{1,9},{9,1},{17,25},{25,17},{2,10},{10... | collective-permute-start | bytes 3244040 | tf_op jit(solution)/shard_map/ppermute | solution.py:371
  321.2 28.6 %collective-permute-start.65 = (bf16[2,1056,256]{2,1,0:T(8,128)(2,1)}, bf16[2,1056,256]{2,1,0:T(8,128)(2,1)}, u32[]{:S(2)}, u32[]{:S(2)}) collective-permute-start(bf16[2,1056,256]{2,1,0:T(8,128)(2,1)} %get-tuple-element.153), channel_id=1, source_target_pairs={{0,16},{8,24},{16,0},{24,8},{1,17},{9,25},{17,1},{25,9},{2,18},{10... | collective-permute-start | bytes 3244040 | tf_op jit(solution)/shard_map/ppermute | solution.py:371
  322.0 48.4 %collective-permute-start.63 = (bf16[2,1056,256]{2,1,0:T(8,128)(2,1)}, bf16[2,1056,256]{2,1,0:T(8,128)(2,1)S(1)}, u32[]{:S(2)}, u32[]{:S(2)}) collective-permute-start(bf16[2,1056,256]{2,1,0:T(8,128)(2,1)} %get-tuple-element.151), channel_id=1, source_target_pairs={{0,8},{8,0},{16,24},{24,16},{1,9},{9,1},{17,25},{25,17},{2,10},{10... | collective-permute-start | bytes 3244040 | tf_op jit(solution)/shard_map/ppermute | solution.py:371
  328.5 66.7 %collective-permute-start.41 = (bf16[512,1024]{1,0:T(8,128)(2,1)}, bf16[512,1024]{1,0:T(8,128)(2,1)}, u32[]{:S(2)}, u32[]{:S(2)}) collective-permute-start(bf16[512,1024]{1,0:T(8,128)(2,1)} %get-tuple-element.116.g_own), channel_id=1, source_target_pairs={{0,4},{4,0},{1,5},{5,1},{2,6},{6,2},{3,7},{7,3},{8,12},{12,8},{9,1... | collective-permute-start | bytes 3145736 | tf_op jit(solution)/shard_map/ppermute | solution.py:371
  332.3 134.9 %collective-permute-start.38 = (bf16[256,1024]{1,0:T(8,128)(2,1)}, bf16[256,1024]{1,0:T(8,128)(2,1)}, u32[]{:S(2)}, u32[]{:S(2)}) collective-permute-start(bf16[256,1024]{1,0:T(8,128)(2,1)} %get-tuple-element.108), channel_id=1, source_target_pairs={{0,0},{1,1},{4,2},{5,3},{2,4},{3,5},{6,6},{7,7},{8,8},{9,9},{12,10... | collective-permute-start | bytes 1572872 | tf_op jit(solution)/shard_map/ppermute | solution.py:371
  347.3 34.7 %collective-permute-start.72 = (bf16[1056,256]{1,0:T(8,128)(2,1)S(1)}, bf16[1056,256]{1,0:T(8,128)(2,1)S(1)}, u32[]{:S(2)}, u32[]{:S(2)}) collective-permute-start(bf16[1056,256]{1,0:T(8,128)(2,1)S(1)} %slice_bitcast_fusion), channel_id=1, source_target_pairs={{0,8},{8,0},{16,24},{24,16},{1,9},{9,1},{17,25},{25,17},{2,10},{10... | collective-permute-start | bytes 1622024 | tf_op jit(solution)/shard_map/ppermute | solution.py:371
  349.8 32.9 %collective-permute-start.69 = (bf16[1056,256]{1,0:T(8,128)(2,1)S(1)}, bf16[1056,256]{1,0:T(8,128)(2,1)S(1)}, u32[]{:S(2)}, u32[]{:S(2)}) collective-permute-start(bf16[1056,256]{1,0:T(8,128)(2,1)S(1)} %slice_bitcast_fusion.2), channel_id=1, source_target_pairs={{0,16},{8,24},{16,0},{24,8},{1,17},{9,25},{17,1},{25,9},{2,18},{10... | collective-permute-start | bytes 1622024 | tf_op jit(solution)/shard_map/ppermute | solution.py:371
  370.3 22.6 %collective-permute-start.66 = (bf16[1056,256]{1,0:T(8,128)(2,1)S(1)}, bf16[1056,256]{1,0:T(8,128)(2,1)S(1)}, u32[]{:S(2)}, u32[]{:S(2)}) collective-permute-start(bf16[1056,256]{1,0:T(8,128)(2,1)S(1)} %slice_bitcast_fusion.4), channel_id=1, source_target_pairs={{0,8},{8,0},{16,24},{24,16},{1,9},{9,1},{17,25},{25,17},{2,10},{10... | collective-permute-start | bytes 1622024 | tf_op jit(solution)/shard_map/ppermute | solution.py:371
  381.9 57.0 %collective-permute-start.64 = (bf16[1056,256]{1,0:T(8,128)(2,1)}, bf16[1056,256]{1,0:T(8,128)(2,1)S(1)}, u32[]{:S(2)}, u32[]{:S(2)}) collective-permute-start(bf16[1056,256]{1,0:T(8,128)(2,1)} %slice_bitcast_fusion.6), channel_id=1, source_target_pairs={{0,16},{8,24},{16,0},{24,8},{1,17},{9,25},{17,1},{25,9},{2,18},{10... | collective-permute-start | bytes 1622024 | tf_op jit(solution)/shard_map/ppermute | solution.py:371
  382.7 58.1 %collective-permute-start.73 = (bf16[1056,256]{1,0:T(8,128)(2,1)S(1)}, bf16[1056,256]{1,0:T(8,128)(2,1)S(1)}, u32[]{:S(2)}, u32[]{:S(2)}) collective-permute-start(bf16[1056,256]{1,0:T(8,128)(2,1)S(1)} %fusion), channel_id=1, source_target_pairs={{0,3},{1,2},{2,1},{3,0},{4,7},{5,6},{6,5},{7,4},{8,11},{9,10},{10,... | collective-permute-start | bytes 1622024 | tf_op jit(solution)/shard_map/ppermute | solution.py:371
  393.0 48.9 %collective-permute-start.70 = (bf16[1056,256]{1,0:T(8,128)(2,1)}, bf16[1056,256]{1,0:T(8,128)(2,1)S(1)}, u32[]{:S(2)}, u32[]{:S(2)}) collective-permute-start(bf16[1056,256]{1,0:T(8,128)(2,1)} %fusion.1), channel_id=1, source_target_pairs={{0,2},{1,3},{2,0},{3,1},{4,6},{5,7},{6,4},{7,5},{8,10},{9,11},{10,... | collective-permute-start | bytes 1622024 | tf_op jit(solution)/shard_map/ppermute | solution.py:371
  395.2 47.6 %collective-permute-start.67 = (bf16[1056,256]{1,0:T(8,128)(2,1)}, bf16[1056,256]{1,0:T(8,128)(2,1)}, u32[]{:S(2)}, u32[]{:S(2)}) collective-permute-start(bf16[1056,256]{1,0:T(8,128)(2,1)} %fusion.2), channel_id=1, source_target_pairs={{0,1},{1,0},{2,3},{3,2},{4,5},{5,4},{6,7},{7,6},{8,9},{9,8},{10,11... | collective-permute-start | bytes 1622024 | tf_op jit(solution)/shard_map/ppermute | solution.py:371
  441.9 22.9 %collective-permute-start.50 = (bf16[2,512,256]{2,1,0:T(8,128)(2,1)}, bf16[2,512,256]{2,1,0:T(8,128)(2,1)S(1)}, u32[]{:S(2)}, u32[]{:S(2)}) collective-permute-start(bf16[2,512,256]{2,1,0:T(8,128)(2,1)} %get-tuple-element.143), channel_id=1, source_target_pairs={{0,8},{8,0},{16,24},{24,16},{1,9},{9,1},{17,25},{25,17},{2,10},{10... | collective-permute-start | bytes 1572872 | tf_op jit(solution)/shard_map/ppermute | solution.py:371
  442.8 23.1 %collective-permute-start.53 = (bf16[2,512,256]{2,1,0:T(8,128)(2,1)}, bf16[2,512,256]{2,1,0:T(8,128)(2,1)S(1)}, u32[]{:S(2)}, u32[]{:S(2)}) collective-permute-start(bf16[2,512,256]{2,1,0:T(8,128)(2,1)} %get-tuple-element.145), channel_id=1, source_target_pairs={{0,16},{8,24},{16,0},{24,8},{1,17},{9,25},{17,1},{25,9},{2,18},{10... | collective-permute-start | bytes 1572872 | tf_op jit(solution)/shard_map/ppermute | solution.py:371
  454.0 48.5 %collective-permute-start.42 = (bf16[512,1024]{1,0:T(8,128)(2,1)S(1)}, bf16[512,1024]{1,0:T(8,128)(2,1)S(1)}, u32[]{:S(2)}, u32[]{:S(2)}) collective-permute-start(bf16[512,1024]{1,0:T(8,128)(2,1)S(1)} %copy-done.55), channel_id=1, source_target_pairs={{0,4},{4,0},{1,5},{5,1},{2,6},{6,2},{3,7},{7,3},{8,12},{12,8},{9,1... | collective-permute-start | bytes 3145736 | tf_op jit(solution)/shard_map/ppermute | solution.py:371
  486.7 30.8 %collective-permute-start.77 = (bf16[1056,256]{1,0:T(8,128)(2,1)S(1)}, bf16[1056,256]{1,0:T(8,128)(2,1)}, u32[]{:S(2)}, u32[]{:S(2)}) collective-permute-start(bf16[1056,256]{1,0:T(8,128)(2,1)S(1)} %add_convert_fusion.4.refs_0_), channel_id=1, source_target_pairs={{0,4},{4,0},{1,5},{5,1},{2,6},{6,2},{3,7},{7,3},{8,12},{12,8},{9,1... | collective-permute-start | bytes 1622024 | tf_op jit(solution)/shard_map/ppermute | solution.py:371
  489.1 30.1 %collective-permute-start.79 = (bf16[1056,256]{1,0:T(8,128)(2,1)S(1)}, bf16[1056,256]{1,0:T(8,128)(2,1)}, u32[]{:S(2)}, u32[]{:S(2)}) collective-permute-start(bf16[1056,256]{1,0:T(8,128)(2,1)S(1)} %collective-permute-done.75.refs_2_), channel_id=1, source_target_pairs={{0,4},{4,0},{1,5},{5,1},{2,6},{6,2},{3,7},{7,3},{8,12},{12,8},{9,1... | collective-permute-start | bytes 1622024 | tf_op jit(solution)/shard_map/ppermute | solution.py:371
  510.2 22.2 %collective-permute-start.76 = (bf16[1056,256]{1,0:T(8,128)(2,1)}, bf16[1056,256]{1,0:T(8,128)(2,1)S(1)}, u32[]{:S(2)}, u32[]{:S(2)}) collective-permute-start(bf16[1056,256]{1,0:T(8,128)(2,1)} %collective-permute-done.74.refs_1_), channel_id=1, source_target_pairs={{0,16},{8,24},{16,0},{24,8},{1,17},{9,25},{17,1},{25,9},{2,18},{10... | collective-permute-start | bytes 1622024 | tf_op jit(solution)/shard_map/ppermute | solution.py:371
  517.5 22.3 %collective-permute-start.43 = (bf16[256,1024]{1,0:T(8,128)(2,1)}, bf16[256,1024]{1,0:T(8,128)(2,1)S(1)}, u32[]{:S(2)}, u32[]{:S(2)}) collective-permute-start(bf16[256,1024]{1,0:T(8,128)(2,1)} %get-tuple-element.136), channel_id=1, source_target_pairs={{0,0},{1,1},{4,2},{5,3},{2,4},{3,5},{6,6},{7,7},{8,8},{9,9},{12,10... | collective-permute-start | bytes 1572872 | tf_op jit(solution)/shard_map/ppermute | solution.py:371
  519.2 21.7 %collective-permute-start.44 = (bf16[256,1024]{1,0:T(8,128)(2,1)}, bf16[256,1024]{1,0:T(8,128)(2,1)S(1)}, u32[]{:S(2)}, u32[]{:S(2)}) collective-permute-start(bf16[256,1024]{1,0:T(8,128)(2,1)} %get-tuple-element.137), channel_id=1, source_target_pairs={{1,0},{0,1},{5,2},{4,3},{3,4},{2,5},{7,6},{6,7},{9,8},{8,9},{13,10... | collective-permute-start | bytes 1572872 | tf_op jit(solution)/shard_map/ppermute | solution.py:371
  532.5 55.5 %collective-permute-start.80 = (bf16[1056,256]{1,0:T(8,128)(2,1)S(1)}, bf16[1056,256]{1,0:T(8,128)(2,1)S(1)}, u32[]{:S(2)}, u32[]{:S(2)}) collective-permute-start(bf16[1056,256]{1,0:T(8,128)(2,1)S(1)} %collective-permute-done.76.refs_3_), channel_id=1, source_target_pairs={{0,4},{4,0},{1,5},{5,1},{2,6},{6,2},{3,7},{7,3},{8,12},{12,8},{9,1... | collective-permute-start | bytes 1622024 | tf_op jit(solution)/shard_map/ppermute | solution.py:371
  535.0 67.1 %collective-permute-start.59 = (bf16[512,256]{1,0:T(8,128)(2,1)S(1)}, bf16[512,256]{1,0:T(8,128)(2,1)}, u32[]{:S(2)}, u32[]{:S(2)}) collective-permute-start(bf16[512,256]{1,0:T(8,128)(2,1)S(1)} %add_convert_fusion.9.refs_0_), channel_id=1, source_target_pairs={{0,4},{4,0},{1,5},{5,1},{2,6},{6,2},{3,7},{7,3},{8,12},{12,8},{9,1... | collective-permute-start | bytes 786440 | tf_op jit(solution)/shard_map/ppermute | solution.py:371
  539.8 62.3 %collective-permute-start.61 = (bf16[512,256]{1,0:T(8,128)(2,1)}, bf16[512,256]{1,0:T(8,128)(2,1)}, u32[]{:S(2)}, u32[]{:S(2)}) collective-permute-start(bf16[512,256]{1,0:T(8,128)(2,1)} %collective-permute-done.57.refs_2_), channel_id=1, source_target_pairs={{0,4},{4,0},{1,5},{5,1},{2,6},{6,2},{3,7},{7,3},{8,12},{12,8},{9,1... | collective-permute-start | bytes 786440 | tf_op jit(solution)/shard_map/ppermute | solution.py:371
  539.8 62.3 %collective-permute-start.60 = (bf16[512,256]{1,0:T(8,128)(2,1)}, bf16[512,256]{1,0:T(8,128)(2,1)}, u32[]{:S(2)}, u32[]{:S(2)}) collective-permute-start(bf16[512,256]{1,0:T(8,128)(2,1)} %collective-permute-done.56.refs_1_), channel_id=1, source_target_pairs={{0,4},{4,0},{1,5},{5,1},{2,6},{6,2},{3,7},{7,3},{8,12},{12,8},{9,1... | collective-permute-start | bytes 786440 | tf_op jit(solution)/shard_map/ppermute | solution.py:371
  540.9 61.3 %collective-permute-start.62 = (bf16[512,256]{1,0:T(8,128)(2,1)}, bf16[512,256]{1,0:T(8,128)(2,1)}, u32[]{:S(2)}, u32[]{:S(2)}) collective-permute-start(bf16[512,256]{1,0:T(8,128)(2,1)} %collective-permute-done.58.refs_3_), channel_id=1, source_target_pairs={{0,4},{4,0},{1,5},{5,1},{2,6},{6,2},{3,7},{7,3},{8,12},{12,8},{9,1... | collective-permute-start | bytes 786440 | tf_op jit(solution)/shard_map/ppermute | solution.py:371
  (89 other events, 1327.3 us)

commit v2 on v1

v2 whole, which is shorter than its diff:
```python
import functools

import jax
import jax.numpy as jnp
from jax import lax
from jax.experimental import pallas as pl
from jax.experimental.pallas import tpu as pltpu
from jax.sharding import Mesh
from jax.sharding import PartitionSpec as P

HEADS = 8
HD = 128
MICRO = 2
BLK = 256
TOPK = 128
CACHE = 256
D = 1024
NQ = 4
DP = D // NQ
HALF = 512
LEN = 1024
HID = 352
RA = 4 * HD
RB = 3 * HID

EPS = 1e-06
NEG = -1e30
BF = jnp.bfloat16
F32 = jnp.float32


def nn(a, b):
    return lax.dot_general(a, b, (((1,), (0,)), ((), ())), preferred_element_type=F32)


def nt(a, b):
    return lax.dot_general(a, b, (((1,), (1,)), ((), ())), preferred_element_type=F32)


def tn(a, b):
    return lax.dot_general(a, b, (((0,), (0,)), ((), ())), preferred_element_type=F32)


VM = pl.BlockSpec(memory_space=pltpu.VMEM)
SM = pl.BlockSpec(memory_space=pltpu.SMEM)


def call(body, outs, args, flops=0, trans=0, scratch=(), name=None, vmem=None):
    nbytes = sum(a.size * a.dtype.itemsize for a in args) + sum(
        jnp.dtype(t).itemsize * functools.reduce(lambda x, y: x * y, s, 1) for s, t in outs
    )
    return pl.pallas_call(
        body,
        out_shape=[jax.ShapeDtypeStruct(s, t) for s, t in outs],
        in_specs=[SM if i == 0 else VM for i in range(len(args))],
        out_specs=[VM for _ in outs],
        scratch_shapes=list(scratch),
        name=name,
        compiler_params=pltpu.CompilerParams(vmem_limit_bytes=vmem),
        cost_estimate=pl.CostEstimate(flops=int(flops), bytes_accessed=int(nbytes), transcendentals=int(trans)),
    )(*args)


def block(index, size):
    return pl.ds(pl.multiple_of(index * size, size), size)


def lanes(k):
    return slice(k * DP, (k + 1) * DP)


def unprep_rows_body(ids, b0, b1, out):
    q, t = ids[0], ids[2]
    for k in range(NQ):
        cols = block(q ^ k, DP)
        for r, src in ((0, b0), (1, b1)):
            out[(r + t) & 1, :, cols] = src[:, lanes(k)]


def scale_of(x):
    return lax.rsqrt(jnp.mean(x * x, axis=-1, keepdims=True) + EPS)


def own_b_body(ids, gate_t, up_t, down, out):
    q, c = ids[0], ids[1]
    for k in range(NQ):
        for i, w in enumerate((gate_t, up_t, down)):
            out[i * HID : (i + 1) * HID, lanes(k)] = w[pl.ds(pl.multiple_of(c * HID, 32), HID), block(q ^ k, DP)]


def rel_gain(ids, gain):
    return jnp.concatenate([gain[:, block(ids[0] ^ k, DP)] for k in range(NQ)], axis=1)


def output_body(ids, hidden, y_own, y_got, s0, s1):
    t = ids[2]
    for r, out in ((0, s0), (1, s1)):
        rows = block((t & 1) ^ r, 256)
        out[...] = (hidden[rows, :] + (y_own[rows, :] + y_got[rows, :].astype(F32))).astype(BF)


def norm_back(grad, x, gain):
    scale = scale_of(x)
    scaled = grad * gain
    gain_part = jnp.sum(grad * x * scale, axis=0, keepdims=True)
    back = scale * scaled - x * (scale * scale * scale) * jnp.mean(scaled * x, axis=-1, keepdims=True)
    return back, gain_part


def put_gain(ids, out, total):
    q = ids[0]
    for k in range(NQ):
        out[:, block(q ^ k, DP)] = total[:, lanes(k)]


def norm_two_back_body(ids, d_own, d_got, cot, hidden, gain, grad_hidden, low, gain_out):
    gain = rel_gain(ids, gain)
    total = jnp.zeros((1, D), F32)
    for i in range(2):
        rows = slice(i * 256, (i + 1) * 256)
        grad = d_own[rows, :] + d_got[rows, :].astype(F32)
        back, part = norm_back(grad, hidden[rows, :], gain)
        total = total + part
        g = cot[rows, :].astype(F32) + back
        grad_hidden[rows, :] = g
        low[rows, :] = g.astype(BF)
    put_gain(ids, gain_out, total)


def norm_one_back_body(ids, d_own, d_got, grad_hidden, x, gain, s0, s1, gain_out):
    gain = rel_gain(ids, gain)
    t = ids[2]
    total = jnp.zeros((1, D), F32)
    for r, out in ((0, s0), (1, s1)):
        rows = block((t & 1) ^ r, 256)
        grad = d_own[rows, :] + d_got[rows, :].astype(F32)
        back, part = norm_back(grad, x[rows, :].astype(F32), gain)
        total = total + part
        out[...] = (grad_hidden[rows, :] + back).astype(BF)
    put_gain(ids, gain_out, total)


def causal():
    return lax.broadcasted_iota(jnp.int32, (BLK, BLK), 1) <= lax.broadcasted_iota(jnp.int32, (BLK, BLK), 0)


def attention_back_body(j, pieces, ids, g_own, g_oth, n_own, n_oth, wa, qkv_all, att_all, lse_all, mem_all,
                        keep_out, send_out, dq_own, dq_oth, da, dk, dv, dall):
    c = ids[1]
    wo = wa[j, 3 * HD : 4 * HD, :]
    qkv, att, lse, mem = qkv_all.at[j], att_all.at[:, j * HD : (j + 1) * HD], lse_all.at[j], mem_all.at[j]
    grad_o = jnp.zeros((HD, D), F32)
    for who, g in ((c, g_own), (1 - c, g_oth)):
        rows = block(who, HALF)
        grads = g[...]
        da[rows, :] = nt(grads, wo).astype(BF)
        grad_o = grad_o + tn(att[rows, :], grads)
    keep = causal()
    for b in range(LEN // BLK):
        rows = slice(b * BLK, (b + 1) * BLK)
        query = qkv[rows, 0:HD]
        grad = da[rows, :]
        level = lse[rows, 0:1]
        mem_k = mem[b * TOPK : (b + 1) * TOPK, :]
        mem_v = mem[512 + b * TOPK : 512 + (b + 1) * TOPK, :]
        p_d = jnp.exp(jnp.where(keep, nt(query, qkv[rows, HD : 2 * HD]), NEG) - level)
        p_f = jnp.exp(nt(query, mem_k) - level)
        g_d = nt(grad, qkv[rows, 2 * HD : 3 * HD])
        g_f = nt(grad, mem_v)
        delta = jnp.sum(p_d * g_d, axis=1, keepdims=True) + jnp.sum(p_f * g_f, axis=1, keepdims=True)
        if b:
            past = slice(0, b * BLK)
            p_p = jnp.exp(nt(query, qkv[past, HD : 2 * HD]) - level)
            g_p = nt(grad, qkv[past, 2 * HD : 3 * HD])
            delta = delta + jnp.sum(p_p * g_p, axis=1, keepdims=True)
        s_d = (p_d * (g_d - delta)).astype(BF)
        s_f = (p_f * (g_f - delta)).astype(BF)
        dq = nn(s_d, qkv[rows, HD : 2 * HD]) + nn(s_f, mem_k)
        if b:
            s_p = (p_p * (g_p - delta)).astype(BF)
            dq = dq + nn(s_p, qkv[past, HD : 2 * HD])
            dk[past, :] = dk[past, :] + tn(s_p, query)
            dv[past, :] = dv[past, :] + tn(p_p.astype(BF), grad)
        dk[rows, :] = tn(s_d, query)
        dv[rows, :] = tn(p_d.astype(BF), grad)
        dall[rows, 0:HD] = (dq * (HD**-0.5)).astype(BF)
    dall[:, HD : 2 * HD] = dk[...].astype(BF)
    dall[:, 2 * HD : 3 * HD] = dv[...].astype(BF)
    grad_w = jnp.zeros((3 * HD, D), F32)
    for who, n, out in ((c, n_own, dq_own), (1 - c, n_oth, dq_oth)):
        part = dall[block(who, HALF), :]
        out[...] = part
        grad_w = grad_w + tn(part, n[...])
    for out, which in ((keep_out, pieces[:2]), (send_out, pieces[2:])):
        for slot, k in enumerate(which):
            out[slot, 0 : 3 * HD, :] = grad_w[:, lanes(k)].astype(BF)
            out[slot, 3 * HD : 4 * HD, :] = grad_o[:, lanes(k)].astype(BF)


def in_proj_back_body(ids, *refs):
    parts, (wa, d_own, d_oth) = refs[:8], refs[8:]
    weights = jnp.concatenate([wa[j, 0 : 3 * HD, :] for j in range(4)], axis=0)
    for side, out in ((1, d_oth), (0, d_own)):
        d = jnp.concatenate([parts[2 * j + side][...] for j in range(4)], axis=1)
        out[...] = nn(d, weights).astype(out.dtype)


def ffn_body(pieces, ids, n_own, n_oth, c_own, c_oth, w, keep_out, send_out, act, dgu):
    for side, n, cot in ((0, n_own, c_own), (1, n_oth, c_oth)):
        for i in range(2):
            rows = slice(i * 256, (i + 1) * 256)
            cols = slice(side * HALF + i * 256, side * HALF + (i + 1) * 256)
            normed = n[rows, :]
            gate = nt(w[0:HID, :], normed)
            up = nt(w[HID : 2 * HID, :], normed)
            grad = nt(w[2 * HID : 3 * HID, :], cot[rows, :])
            sig = 1.0 / (1.0 + jnp.exp(-gate))
            silu = gate * sig
            act[:, cols] = (silu * up).astype(BF)
            dgu[0:HID, cols] = (grad * up * sig * (1.0 + gate * (1.0 - sig))).astype(BF)
            dgu[HID : 2 * HID, cols] = (grad * silu).astype(BF)
    for out, which in ((keep_out, pieces[:2]), (send_out, pieces[2:])):
        for slot, k in enumerate(which):
            g = nn(dgu[:, 0:HALF], n_own[:, lanes(k)]) + nn(dgu[:, HALF:LEN], n_oth[:, lanes(k)])
            out[slot, 0 : 2 * HID, :] = g.astype(BF)
            g = nn(act[:, 0:HALF], c_own[:, lanes(k)]) + nn(act[:, HALF:LEN], c_oth[:, lanes(k)])
            out[slot, 2 * HID : 3 * HID, :] = g.astype(BF)


def ffn_sum_body(lo, hi, ids, *refs):
    parts, w, (own, oth, acc) = refs[:4], refs[4:6], refs[6:]
    for side, out in ((1, oth), (0, own)):
        cols = slice(side * HALF, (side + 1) * HALF)
        for j in range(4):
            weights = w[1][j - 1, lo:hi, :] if j else w[0][lo:hi, :]
            got = tn(parts[j][:, cols], weights)
            if j == 0:
                acc[...] = got
            elif j < 3:
                acc[...] = acc[...] + got
            else:
                out[...] = (acc[...] + got).astype(out.dtype)


def place_a_body(ids, *refs):
    q, c = ids[0], ids[1]
    own, oth, (gq, gk, gv, go) = refs[:4], refs[4:8], refs[8:]
    for k in range(NQ):
        rows = block(q ^ k, DP)
        for half, src in ((c, own[k]), (1 - c, oth[k])):
            for i, out in enumerate((gq, gk, gv)):
                out[rows, block(half, HD)] = src[i * HD : (i + 1) * HD, :].astype(F32).T
            go[block(half, HD), rows] = src[3 * HD : 4 * HD, :].astype(F32)


def place_b_body(ids, *refs):
    q, c = ids[0], ids[1]
    own, oth, outs = refs[:4], refs[4:8], refs[8:]
    for k in range(NQ):
        cols = block(q ^ k, DP)
        for half, src in ((c, own[k]), (1 - c, oth[k])):
            rows = pl.ds(pl.multiple_of(half * HID, 32), HID)
            for i, out in enumerate(outs):
                out[rows, cols] = src[i * HID : (i + 1) * HID, :].astype(F32)


def where_am_i():
    return lax.axis_index("r"), lax.axis_index("q"), lax.axis_index("c"), lax.axis_index("t")


def at(q, c, t):
    return {"q": q, "c": c, "t": t}


def dp_at(index):
    return {"r": index // (2 * NQ), "q": lax.rem(index // 2, NQ), "c": lax.rem(index, 2)}


def remote(src, dst, send_sem, recv_sem, device):
    return pltpu.make_async_remote_copy(
        src_ref=src, dst_ref=dst, send_sem=send_sem, recv_sem=recv_sem, device_id=device,
        device_id_type=pl.DeviceIdType.MESH,
    )


def arrived(dst, recv_sem, spare):
    pltpu.make_async_copy(dst, dst, recv_sem).wait()


def greet(devices):
    barrier = pltpu.get_barrier_semaphore()
    for device in devices:
        pl.semaphore_signal(barrier, inc=1, device_id=device, device_id_type=pl.DeviceIdType.MESH)
    pl.semaphore_wait(barrier, len(devices))


class Sends:
    def __init__(self):
        self.open = []

    def go(self, src, dst, send_sem, recv_sem, device, when=None):
        copy = remote(src, dst, send_sem, recv_sem, device)
        self.open.append((copy, when))
        if when is None:
            copy.start()
        else:
            pl.when(when)(copy.start)

    def drain(self):
        for copy, when in self.open:
            if when is None:
                copy.wait_send()
            else:
                pl.when(when)(copy.wait_send)
        self.open = []


def front_body(tok, cot, gain_a, gain_f, ck, cv, knn, wq, wk, wv, wo, gate_t, up_t, down,
               wa, wb, x_own, n_own, n_oth, cot_own, cot_oth, mem, qkv, att, lse, hidden, n2_own, n2_oth,
               prev_k, prev_v, picked, o_send, o_got,
               row_send, row_recv, cot_send, cot_recv, cache_send, cache_recv, mem_send, mem_recv,
               za_send, za_recv, xa_send, xa_recv, zb_send, zb_recv, xb_send, xb_recv, pair_send, pair_recv):
    r, q, c, t = where_am_i()
    count = lax.axis_size("r") * 2 * NQ
    me = (r * NQ + q) * 2 + c
    after = dp_at(lax.rem(me + 1, count))
    across = dp_at(lax.rem(me + jnp.where(c == 0, count - 1, 1), count))
    mid = (t == 1) | (t == 2)
    second, third = jnp.where(mid, 3, 2), jnp.where(mid, 2, 3)
    partner = at(q, 1 - c, t)
    sends = Sends()
    greet(
        [at(q, c, t ^ j) for j in range(1, 4)] + [at(q, 1 - c, t ^ j) for j in range(4)]
        + [at(q ^ 1, c, t), at(q ^ 2, c, t), at(q ^ 3, c, t), across]
    )

    def rows_out(src, dst, send_sem, recv_sem):
        slot = t & 1
        for m in range(MICRO):
            here = (c == (t >> 1)) & (m == slot)
            for k in range(NQ):
                one = src.at[m, :, block(q ^ k, DP)]
                two = dst.at[block(slot, 256), lanes(k)]
                sends.go(one, two, send_sem.at[m, k], recv_sem.at[slot, k], at(q, t >> 1, 2 * c + m),
                         when=jnp.logical_not(here))
                pl.when(here)(pltpu.make_async_copy(one, two, recv_sem.at[slot, k]).start)

    def rows_in(dst, recv_sem):
        for slot in range(2):
            for k in range(NQ):
                arrived(dst.at[slot * 256 : (slot + 1) * 256, lanes(k)], recv_sem.at[slot, k], None)

    rows_out(tok, x_own, row_send, row_recv)
    for i, (one, two) in enumerate(((ck, prev_k), (cv, prev_v))):
        sends.go(one, two, cache_send.at[i], cache_recv.at[i], after)

    for k in range(NQ):
        rows = block(q ^ k, DP)
        for i, w in enumerate((wq, wk, wv)):
            wa[0, i * HD : (i + 1) * HD, lanes(k)] = w[rows, block(c, HD)].T
        wa[0, 3 * HD : 4 * HD, lanes(k)] = wo[block(c, HD), rows]

    for i, two in enumerate((prev_k, prev_v)):
        arrived(two, cache_recv.at[i], None)
    for m in range(MICRO):
        for h in range(2):
            cols = slice(h * HD, (h + 1) * HD)
            for b in range(LEN // BLK):
                picks = knn[m, b, h : h + 1, :]
                rows = lax.broadcasted_iota(jnp.int32, (CACHE, TOPK), 0)
                hot_own = jnp.where(rows == picks, 1.0, 0.0).astype(BF)
                hot_prev = jnp.where(rows + CACHE == picks, 1.0, 0.0).astype(BF)
                for kv, own, prev in ((0, ck, prev_k), (1, cv, prev_v)):
                    got = tn(hot_own, own[m, :, cols]) + tn(hot_prev, prev[m, :, cols])
                    picked[m, h, kv * 512 + b * TOPK : kv * 512 + (b + 1) * TOPK, :] = got.astype(BF)
    for m in range(MICRO):
        for h in range(2):
            kind = t ^ (2 * c + m)
            here = (c == h) & (kind == 0)
            sends.go(picked.at[m, h], mem.at[kind], mem_send.at[m, h], mem_recv.at[kind], at(q, h, 2 * c + m),
                     when=jnp.logical_not(here))
            pl.when(here)(pltpu.make_async_copy(picked.at[m, h], mem.at[kind], mem_recv.at[kind]).start)

    near, far_mid = at(q, c, t ^ 1), at(q, c, t ^ 3)
    a_piece = [wa.at[0, :, lanes(0)]]
    b_piece = [w.at[pl.ds(pl.multiple_of(c * HID, 32), HID), block(q, DP)] for w in (gate_t, up_t, down)]

    def a_slot(s):
        return [wa.at[s, :, lanes(0)]]

    def b_slot(s):
        return [wb.at[s - 1, i * HID : (i + 1) * HID, lanes(0)] for i in range(3)]

    def z_first(piece, slot, send_sem, recv_sem):
        for i, (one, two) in enumerate(zip(piece, slot(1))):
            sends.go(one, two, send_sem.at[0, i], recv_sem.at[1, i], near)
        for i, (one, two) in enumerate(zip(piece, slot(3))):
            sends.go(one, two, send_sem.at[1, i], recv_sem.at[3, i], far_mid, when=mid)

    def relay(order, slot, whole, z_send, z_recv, x_send, x_recv):
        s = (None, 1, second, third)[order]
        for i, two in enumerate(slot(s)):
            arrived(two, z_recv.at[s, i], None)
        if order == 1:
            for i, (one, two) in enumerate(zip(slot(1), slot(2))):
                sends.go(one, two, z_send.at[2, i], z_recv.at[2, i], far_mid, when=mid)
        elif order == 2:
            for i, (one, two) in enumerate(zip(slot(3), slot(2))):
                sends.go(one, two, z_send.at[3, i], z_recv.at[2, i], near, when=mid)
        else:
            for i, (one, two) in enumerate(zip(slot(2), slot(3))):
                sends.go(one, two, z_send.at[4, i], z_recv.at[3, i], near, when=mid)
        sends.go(whole(s, 0), whole(s, 1), x_send.at[s, 1], x_recv.at[s, 1], at(q ^ 1, c, t))
        sends.go(whole(s, 0), whole(s, 2), x_send.at[s, 2], x_recv.at[s, 2], at(q ^ 2, c, t))
        if order == 3:
            sends.go(whole(s, 0), whole(s, 3), x_send.at[s, 3], x_recv.at[s, 3], at(q ^ 3, c, t))

    def relay_far(order, whole, x_send, x_recv):
        s = (None, 1, second)[order]
        arrived(whole(s, order), x_recv.at[s, order], None)
        sends.go(whole(s, order), whole(s, 3), x_send.at[s, 3], x_recv.at[s, 3], at(q ^ (3 - order), c, t))

    def in_place(order, whole, x_recv):
        s = (None, 1, second, third)[order]
        for k in range(1, NQ):
            if k != order or order == 3:
                arrived(whole(s, k), x_recv.at[s, k], None)

    def a_whole(s, k):
        return wa.at[s, :, lanes(k)]

    def b_whole(s, k):
        return wb.at[s - 1, :, lanes(k)]

    relay_a = functools.partial(relay, slot=a_slot, whole=a_whole, z_send=za_send, z_recv=za_recv, x_send=xa_send, x_recv=xa_recv)
    relay_b = functools.partial(relay, slot=b_slot, whole=b_whole, z_send=zb_send, z_recv=zb_recv, x_send=xb_send, x_recv=xb_recv)

    z_first(a_piece, a_slot, za_send, za_recv)
    rows_out(cot, cot_own, cot_send, cot_recv)
    z_first(b_piece, b_slot, zb_send, zb_recv)

    rows_in(x_own, row_recv)
    gain = jnp.concatenate([gain_a[:, block(q ^ k, DP)] for k in range(NQ)], axis=1)
    for i in range(2):
        rows = slice(i * 256, (i + 1) * 256)
        x = x_own[rows, :].astype(F32)
        n_own[rows, :] = (x * scale_of(x) * gain).astype(BF)
    sends.go(n_own, n_oth, pair_send.at[0], pair_recv.at[0], partner)

    def project(j, who, n):
        acc = nt(n[...], wa[j, 0 : 3 * HD, :])
        rows = block(who, HALF)
        qkv[j, rows, 0:HD] = (acc[:, 0:HD] * (HD**-0.5)).astype(BF)
        qkv[j, rows, HD : 3 * HD] = acc[:, HD : 3 * HD].astype(BF)

    def attend(j):
        keep = causal()
        for b in range(LEN // BLK):
            rows = slice(b * BLK, (b + 1) * BLK)
            query = qkv[j, rows, 0:HD]
            diag = jnp.where(keep, nt(query, qkv[j, rows, HD : 2 * HD]), NEG)
            far = nt(query, mem[j, b * TOPK : (b + 1) * TOPK, :])
            top = jnp.maximum(jnp.max(diag, axis=1, keepdims=True), jnp.max(far, axis=1, keepdims=True))
            if b:
                past = nt(query, qkv[j, 0 : b * BLK, HD : 2 * HD])
                top = jnp.maximum(top, jnp.max(past, axis=1, keepdims=True))
            diag = jnp.exp(diag - top)
            far = jnp.exp(far - top)
            total = jnp.sum(diag, axis=1, keepdims=True) + jnp.sum(far, axis=1, keepdims=True)
            if b:
                past = jnp.exp(past - top)
                total = total + jnp.sum(past, axis=1, keepdims=True)
            inverse = 1.0 / total
            out = nn((diag * inverse).astype(BF), qkv[j, rows, 2 * HD : 3 * HD])
            out = out + nn((far * inverse).astype(BF), mem[j, 512 + b * TOPK : 512 + (b + 1) * TOPK, :])
            if b:
                out = out + nn((past * inverse).astype(BF), qkv[j, 0 : b * BLK, 2 * HD : 3 * HD])
            att[rows, j * HD : (j + 1) * HD] = out.astype(BF)
            lse[j, rows, :] = jnp.broadcast_to(top + jnp.log(total), (BLK, HD))

    def got_mem(j):
        arrived(mem.at[j], mem_recv.at[j], None)

    project(0, c, n_own)
    arrived(n_oth, pair_recv.at[0], None)
    project(0, 1 - c, n_oth)
    got_mem(0)
    relay_a(1)
    attend(0)
    relay_a(2)
    relay_far(1, a_whole, xa_send, xa_recv)
    relay_a(3)
    relay_far(2, a_whole, xa_send, xa_recv)
    in_place(1, a_whole, xa_recv)
    got_mem(1)
    project(1, c, n_own)
    project(1, 1 - c, n_oth)
    attend(1)
    in_place(2, a_whole, xa_recv)
    in_place(3, a_whole, xa_recv)
    relay_b(1)
    for j in (2, 3):
        got_mem(j)
        project(j, c, n_own)
        project(j, 1 - c, n_oth)
        attend(j)
        if j == 2:
            relay_b(2)
            relay_far(1, b_whole, xb_send, xb_recv)

    weights = jnp.concatenate([wa[j, 3 * HD : 4 * HD, :] for j in range(4)], axis=0)
    o_send[...] = nn(att[block(1 - c, HALF), :], weights).astype(BF)
    sends.go(o_send, o_got, pair_send.at[1], pair_recv.at[1], partner)
    hidden[...] = nn(att[block(c, HALF), :], weights)
    rows_in(cot_own, cot_recv)
    sends.go(cot_own, cot_oth, pair_send.at[2], pair_recv.at[2], partner)
    arrived(o_got, pair_recv.at[1], None)
    gain = jnp.concatenate([gain_f[:, block(q ^ k, DP)] for k in range(NQ)], axis=1)
    for i in range(2):
        rows = slice(i * 256, (i + 1) * 256)
        h = x_own[rows, :].astype(F32) + (hidden[rows, :] + o_got[rows, :].astype(F32))
        hidden[rows, :] = h
        n2_own[rows, :] = (h * scale_of(h) * gain).astype(BF)
    sends.go(n2_own, n2_oth, pair_send.at[3], pair_recv.at[3], partner)
    relay_b(3)
    relay_far(2, b_whole, xb_send, xb_recv)
    for order in range(1, 4):
        in_place(order, b_whole, xb_recv)
    arrived(n2_oth, pair_recv.at[3], None)
    arrived(cot_oth, pair_recv.at[2], None)
    sends.drain()


def front(*args):
    hbm = pl.BlockSpec(memory_space=pl.ANY)
    outs = [
        ((4, RA, D), BF, VM), ((3, RB, D), BF, hbm), ((HALF, D), BF, VM), ((HALF, D), BF, VM), ((HALF, D), BF, VM),
        ((HALF, D), BF, hbm), ((HALF, D), BF, hbm), ((4, 1024, HD), BF, VM), ((4, LEN, 3 * HD), BF, VM),
        ((LEN, 4 * HD), BF, VM), ((4, LEN, HD), F32, VM), ((HALF, D), F32, VM), ((HALF, D), BF, VM), ((HALF, D), BF, VM),
    ]
    dma = pltpu.SemaphoreType.DMA
    return pl.pallas_call(
        front_body,
        out_shape=[jax.ShapeDtypeStruct(s, d) for s, d, _ in outs],
        in_specs=[hbm, hbm] + [VM] * 9 + [hbm] * 3,
        out_specs=[m for _, _, m in outs],
        scratch_shapes=[
            pltpu.VMEM((MICRO, CACHE, 256), BF), pltpu.VMEM((MICRO, CACHE, 256), BF),
            pltpu.VMEM((MICRO, 2, 1024, HD), BF), pltpu.VMEM((HALF, D), BF), pltpu.VMEM((HALF, D), BF),
            dma((2, 4)), dma((2, 4)), dma((2, 4)), dma((2, 4)), dma((2,)), dma((2,)), dma((2, 2)), dma((4,)),
            dma((5, 1)), dma((4, 1)), dma((4, 4)), dma((4, 4)), dma((5, 3)), dma((4, 3)), dma((4, 4)), dma((4, 4)),
            dma((4,)), dma((4,)),
        ],
        compiler_params=pltpu.CompilerParams(collective_id=0, has_side_effects=True, vmem_limit_bytes=60 << 20),
        name="front",
        cost_estimate=pl.CostEstimate(flops=int(2e10), bytes_accessed=int(5e7), transcendentals=0),
    )(*args)


def send(value, axis, pairs):
    return lax.ppermute(value, axis, pairs)


def flip(value, axis, bits):
    count = lax.axis_size(axis)
    return send(value, axis, [(i, i ^ bits) for i in range(count)])


def row_pairs(r):
    return [
        (c * 4 + t, (t // 2) * 4 + 2 * c + (r + t) % 2)
        for c in range(2)
        for t in range(4)
    ]


def rows_to_sequences(s0, s1):
    return [send(s, ("c", "t"), row_pairs(r)) for r, s in ((0, s0), (1, s1))]


def rows_back(s0, s1):
    return [send(s, ("c", "t"), [(b, a) for a, b in row_pairs(r)]) for r, s in ((0, s0), (1, s1))]


PIECES = ((0, 2, 1, 3), (0, 1, 2, 3), (0, 2, 1, 3), (0, 1, 2, 3))


def plane_sum(j, keep, out):
    first, second = (1, 2) if j % 2 == 0 else (2, 1)
    kept = (keep.astype(F32) + flip(out, "q", first).astype(F32)).astype(BF)
    return (kept[0].astype(F32) + flip(kept[1], "q", second).astype(F32)).astype(BF)


def column_sum(sums):
    total = sums[0].astype(F32)
    for j in range(1, 4):
        total = total + flip(sums[j], "t", j).astype(F32)
    if lax.axis_size("r") > 1:
        total = lax.psum(total, "r")
    return total.astype(BF)


def spread(total, odd):
    by_x = flip(total, "q", 1)
    by_y = flip(total, "q", 2)
    far = flip(by_x, "q", 2) if odd else flip(by_y, "q", 1)
    own = [total, by_x, by_y, far]
    return own, [flip(p, "c", 1) for p in own]


def per_device(tokens, attn_gain, ffn_gain, query_weight, key_weight, value_weight, out_weight, gate_weight,
               up_weight, down_weight, cache_keys, cache_values, knn_index, cotangent):
    q, c, t = lax.axis_index("q"), lax.axis_index("c"), lax.axis_index("t")
    ids = jnp.stack([q, c, t]).astype(jnp.int32)
    gain_a, gain_f = attn_gain.reshape(1, D), ffn_gain.reshape(1, D)
    gate_t, up_t = gate_weight.T, up_weight.T
    rows16 = ((256, D), BF)
    half16, half32 = ((HALF, D), BF), ((HALF, D), F32)

    wa, wb, x_own, n1_own, n1_oth, cot_own, cot_oth, mem, qkv, att, lse, hidden, n2_own, n2_oth = front(
        tokens, cotangent, gain_a, gain_f, cache_keys, cache_values, knn_index, query_weight, key_weight, value_weight,
        out_weight, gate_t, up_t, down_weight,
    )
    (wb0,) = call(own_b_body, [((RB, D), BF)], (ids, gate_t, up_t, down_weight), name="own_b")
    chunks = [
        call(
            functools.partial(ffn_body, PIECES[j]),
            [((2, RB, DP), BF), ((2, RB, DP), BF), ((HID, LEN), BF), ((2 * HID, LEN), BF)],
            (ids, n2_own, n2_oth, cot_own, cot_oth, wb[j - 1] if j else wb0),
            flops=6 * 2 * 1024 * 1024 * HID, trans=1024 * HID, name="ffn",
        )
        for j in range(4)
    ]
    d2_own, d2_oth = call(
        functools.partial(ffn_sum_body, 0, 2 * HID), [half32, half16], (ids, *[ch[3] for ch in chunks], wb0, wb),
        flops=2 * 1024 * 1024 * 8 * HID, scratch=[pltpu.VMEM((HALF, D), F32)], name="ffn_back",
    )
    d2_got = flip(d2_oth, "c", 1)
    y_own, y_oth = call(
        functools.partial(ffn_sum_body, 2 * HID, 3 * HID), [half32, half16], (ids, *[ch[2] for ch in chunks], wb0, wb),
        flops=2 * 1024 * 1024 * 4 * HID, scratch=[pltpu.VMEM((HALF, D), F32)], name="ffn_out",
    )
    y_got = flip(y_oth, "c", 1)
    grad_hidden, low_own, gain_two = call(
        norm_two_back_body, [half32, half16, ((1, D), F32)], (ids, d2_own, d2_got, cot_own, hidden, gain_f),
        name="norm_two_back",
    )
    low_oth = flip(low_own, "c", 1)
    os0, os1 = call(output_body, [rows16, rows16], (ids, hidden, y_own, y_got), name="output")
    ob0, ob1 = rows_back(os0, os1)
    (output,) = call(unprep_rows_body, [((MICRO, 256, D), BF)], (ids, ob0, ob1), name="unprep_output")

    sums_b = [plane_sum(j, ch[0], ch[1]) for j, ch in enumerate(chunks)]
    backs = [
        call(
            functools.partial(attention_back_body, j, PIECES[j]),
            [((2, RA, DP), BF), ((2, RA, DP), BF), ((HALF, 3 * HD), BF), ((HALF, 3 * HD), BF)],
            (ids, low_own, low_oth, n1_own, n1_oth, wa, qkv, att, lse, mem),
            flops=2 * 1024 * 1024 * 640 + 10 * 128 * 786432, trans=786432,
            scratch=[
                pltpu.VMEM((LEN, HD), BF), pltpu.VMEM((LEN, HD), F32), pltpu.VMEM((LEN, HD), F32),
                pltpu.VMEM((LEN, 3 * HD), BF),
            ],
            name="attention_back",
        )
        for j in range(4)
    ]
    total_b = column_sum(sums_b)
    b_own, b_oth = spread(total_b, True)
    sums_a = [plane_sum(j, bk[0], bk[1]) for j, bk in enumerate(backs)]
    d1_own, d1_oth = call(
        in_proj_back_body, [half32, half16], (ids, *[p for bk in backs for p in bk[2:]], wa),
        flops=2 * 1024 * 1024 * 1536, name="in_proj_back",
    )
    d1_got = flip(d1_oth, "c", 1)
    gs0, gs1, gain_one = call(
        norm_one_back_body, [rows16, rows16, ((1, D), F32)], (ids, d1_own, d1_got, grad_hidden, x_own, gain_a),
        name="norm_one_back",
    )
    gb0, gb1 = rows_back(gs0, gs1)
    (grad_tokens,) = call(unprep_rows_body, [((MICRO, 256, D), BF)], (ids, gb0, gb1), name="unprep_grad")
    total_a = column_sum(sums_a)
    a_own, a_oth = spread(total_a, False)

    tall = ((2 * HID, D), F32)
    gg, gu, gd = call(place_b_body, [tall, tall, tall], (ids, *b_own, *b_oth), name="place_b")
    col, row = ((D, 2 * HD), F32), ((2 * HD, D), F32)
    gq, gk, gv, go = call(place_a_body, [col, col, col, row], (ids, *a_own, *a_oth), name="place_a")
    gain_sums = lax.psum(jnp.concatenate((gain_one, gain_two)), ("r", "q", "c", "t"))
    return output, grad_tokens, gq, gk, gv, go, gg.T, gu.T, gd, gain_sums[0], gain_sums[1]


def solution(mesh):
    n_dp, n_t = mesh.shape["dp"], mesh.shape["tensor"]
    fine = Mesh(mesh.devices.reshape(n_dp // 8, NQ, 2, n_t), ("r", "q", "c", "t"))
    dp = ("r", "q", "c")
    rows = P(None, dp + ("t",), None)
    placed = (
        rows, P(), P(), P(None, "t"), P(None, "t"), P(None, "t"), P("t", None), P(None, "t"), P(None, "t"),
        P("t", None), P(None, dp, "t"), P(None, dp, "t"), P(None, dp, "t", None), rows,
    )
    return jax.shard_map(
        per_device,
        mesh=fine,
        in_specs=placed,
        out_specs=(
            rows, rows, P(None, "t"), P(None, "t"), P(None, "t"), P("t", None), P(None, "t"), P(None, "t"),
            P("t", None), P(), P(),
        ),
        check_vma=False,
    )
```

time: 612 us -> 552 us (0.902)
  Pallas kernels: 190 us -> 330 us
  waiting for transfers between devices: 202 us -> 96.7 us
  starting transfers between devices: 135 us -> 52.9 us
  local copies, waits for them, and re-layouts: 20.1 us -> 11 us
    pallas_call x0 -> x1, Pallas kernels: none -> 183 us  [front(): pl.pallas_call(front_body, out_shape=[jax.ShapeDtypeStruct(s, d) for s, d...]
    ppermute x81 -> x44, waiting for transfers between devices: 202 us -> 96.7 us  [send(): return lax.ppermute(value, axis, pairs)]
    ppermute x81 -> x44, starting transfers between devices: 135 us -> 52.9 us  [send(): return lax.ppermute(value, axis, pairs)]
    pallas_call x31 -> x19, Pallas kernels: 190 us -> 147 us  [call(): pl.pallas_call(body, out_shape=[jax.ShapeDtypeStruct(s, t) for s, t in ou...]
    unnamed x116 -> x58, local copies, waits for them, and re-layouts: 14.2 us -> 3.57 us
  transfers between devices with their start and end apart: 81 -> 44, of which waited for: 29 -> 13; matrix products, arithmetic and copies ran while one was open for 4% -> 4% of each run, Pallas kernels for 27% -> 24%
where the time goes in v2:
time: 552 us; the launch traced here: 549 us
  Pallas kernels  330 us (60%)
  waiting for transfers between devices  96.7 us (18%)
  starting transfers between devices  52.9 us (10%)
  blocking collectives  43.7 us (8%)
  other arithmetic  13.2 us (2%)
  local copies, waits for them, and re-layouts  11 us (2%)
    pallas_call x1, Pallas kernels, front(): pl.pallas_call(front_body, out_shape=[jax.ShapeDtypeStruct(s, d) for s, d...  183 us
    pallas_call x19, Pallas kernels, call(): pl.pallas_call(body, out_shape=[jax.ShapeDtypeStruct(s, t) for s, t in ou...  147 us
    ppermute x44, waiting for transfers between devices, send(): return lax.ppermute(value, axis, pairs)  96.7 us
    ppermute x44, starting transfers between devices, send(): return lax.ppermute(value, axis, pairs)  52.9 us
    psum x1, blocking collectives, per_device(): lax.psum(jnp.concatenate((gain_one, gain_two)), ('r', 'q', 'c', 't'))  43.7 us
  transfers between devices with their start and end apart: 44, of which 13 were waited for; matrix products, arithmetic and copies ran while one was open for 4% of the time, Pallas kernels for 24%

profile of v2, /device:TPU:0, one launch (start us, length us, event | category | flops | bytes accessed | tf_op | source)
XLA Modules:
  0.0 549.1 jit_solution(5654541793879576334)
XLA Ops:
  1.3 3.9 own_b.1.w.refs_4_
  5.2 183.3 %front.1 = (bf16[4,512,1024]{2,1,0:T(8,128)(2,1)}, bf16[3,1056,1024]{2,1,0:T(8,128)(2,1)}, bf16[512,1024]{1,0:T(8,128)(2,1)}, bf16[512,1024]{1,0:T(8,128)(2,1)},...) custom-call(bf16[2,256,1024]{2,1,0:T(8,128)(2,1)} %tok.1, ...), custom_call_target="tpu_custom_call" | custom-call | flops 20000000000 | bytes 50000000 | tf_op jit(solution)/shard_map/front/pallas_call | solution.py:542
  188.5 9.1 %ffn.4 = (bf16[2,1056,256]{2,1,0:T(8,128)(2,1)}, bf16[2,1056,256]{2,1,0:T(8,128)(2,1)}, bf16[352,1024]{1,0:T(8,128)(2,1)}, bf16[704,1024]{1,0:T(8,128)(2,1)}) custom-call(s32[3]{0:T(128)} %pad_add_fusion.ids, bf16[512,1024]{1,0:T(8,128)(2,1)} %get-tuple-element.79.n_own, bf16[512,1024]{1,0:T(8,128)(2,1)} %get-tuple-element.80.n_oth, ...), custom_call_target="tpu_custom_call" | custom-call | flops 4429185024 | bytes 10682380 | tf_op jit(solution)/shard_map/ffn/pallas_call | solution.py:52
  199.0 5.8 %slice_bitcast_fusion = (bf16[1056,1024]{1,0:T(8,128)(2,1)}, bf16[1056,1024]{1,0:T(8,128)(2,1)}, bf16[1056,1024]{1,0:T(8,128)(2,1)}) fusion(bf16[3,1056,1024]{2,1,0:T(8,128)(2,1)} %get-tuple-element.84.refs_5_), kind=kLoop, calls=%fused_computation.4 | loop fusion | bytes 12976128 | tf_op jit(solution)/shard_map/squeeze | solution.py:629
  204.8 9.2 %ffn.7 = (bf16[2,1056,256]{2,1,0:T(8,128)(2,1)}, bf16[2,1056,256]{2,1,0:T(8,128)(2,1)}, bf16[352,1024]{1,0:T(8,128)(2,1)}, bf16[704,1024]{1,0:T(8,128)(2,1)}) custom-call(s32[3]{0:T(128)} %pad_add_fusion.ids, bf16[512,1024]{1,0:T(8,128)(2,1)} %get-tuple-element.79.n_own, bf16[512,1024]{1,0:T(8,128)(2,1)} %get-tuple-element.80.n_oth, ...), custom_call_target="tpu_custom_call" | custom-call | flops 4429185024 | bytes 10682380 | tf_op jit(solution)/shard_map/ffn/pallas_call | solution.py:52
  214.0 9.1 %ffn.6 = (bf16[2,1056,256]{2,1,0:T(8,128)(2,1)}, bf16[2,1056,256]{2,1,0:T(8,128)(2,1)}, bf16[352,1024]{1,0:T(8,128)(2,1)}, bf16[704,1024]{1,0:T(8,128)(2,1)}) custom-call(s32[3]{0:T(128)} %pad_add_fusion.ids, bf16[512,1024]{1,0:T(8,128)(2,1)} %get-tuple-element.79.n_own, bf16[512,1024]{1,0:T(8,128)(2,1)} %get-tuple-element.80.n_oth, ...), custom_call_target="tpu_custom_call" | custom-call | flops 4429185024 | bytes 10682380 | tf_op jit(solution)/shard_map/ffn/pallas_call | solution.py:52
  223.1 9.0 %ffn.5 = (bf16[2,1056,256]{2,1,0:T(8,128)(2,1)}, bf16[2,1056,256]{2,1,0:T(8,128)(2,1)}, bf16[352,1024]{1,0:T(8,128)(2,1)}, bf16[704,1024]{1,0:T(8,128)(2,1)}) custom-call(s32[3]{0:T(128)} %pad_add_fusion.ids, bf16[512,1024]{1,0:T(8,128)(2,1)} %get-tuple-element.79.n_own, bf16[512,1024]{1,0:T(8,128)(2,1)} %get-tuple-element.80.n_oth, ...), custom_call_target="tpu_custom_call" | custom-call | flops 4429185024 | bytes 10682380 | tf_op jit(solution)/shard_map/ffn/pallas_call | solution.py:52
  232.1 13.6 %ffn_back.1 = (f32[512,1024]{1,0:T(8,128)}, bf16[512,1024]{1,0:T(8,128)(2,1)}) custom-call(s32[3]{0:T(128)} %pad_add_fusion.ids, bf16[704,1024]{1,0:T(8,128)(2,1)} %get-tuple-element.92.refs_0_, bf16[704,1024]{1,0:T(8,128)(2,1)} %get-tuple-element.93.refs_1_, bf16[704,1024]{1,0:T(8,128)(2,1)} %get-tuple-element.94.refs_2_, ...), custom_call_target="tpu_custom_call" | custom-call | flops 5905580032 | bytes 17563660 | tf_op jit(solution)/shard_map/ffn_back/pallas_call | solution.py:52
  245.8 10.2 %ffn_out.1 = (f32[512,1024]{1,0:T(8,128)}, bf16[512,1024]{1,0:T(8,128)(2,1)}) custom-call(s32[3]{0:T(128)} %pad_add_fusion.ids, bf16[352,1024]{1,0:T(8,128)(2,1)} %get-tuple-element.83.refs_0_, bf16[352,1024]{1,0:T(8,128)(2,1)} %get-tuple-element.85.refs_1_, bf16[352,1024]{1,0:T(8,128)(2,1)} %get-tuple-element.86.refs_2_, ...), custom_call_target="tpu_custom_call" | custom-call | flops 2952790016 | bytes 14680076 | tf_op jit(solution)/shard_map/ffn_out/pallas_call | solution.py:52
  259.6 5.6 %norm_two_back.1 = (f32[512,1024]{1,0:T(8,128)}, bf16[512,1024]{1,0:T(8,128)(2,1)}, f32[1,1024]{1,0:T(1,128)}) custom-call(s32[3]{0:T(128)} %pad_add_fusion.ids, f32[512,1024]{1,0:T(8,128)} %get-tuple-element.96.d_own, bf16[512,1024]{1,0:T(8,128)(2,1)} %copy-done.9, bf16[512,1024]{1,0:T(8,128)(2,1)} %get-tuple-element.81.c_own.cot, ...), custom_call_target="tpu_custom_call" | custom-call | bytes 9445388 | tf_op jit(solution)/shard_map/norm_two_back/pallas_call | solution.py:52
  266.1 3.8 output.1
  269.9 5.3 collective-permute-start.1
  275.3 1.5 add_convert_fusion.3
  277.6 6.0 %collective-permute-done.34 = bf16[2,1056,256]{2,1,0:T(8,128)(2,1)} collective-permute-done((bf16[2,1056,256]{2,1,0:T(8,128)(2,1)}, bf16[2,1056,256]{2,1,0:T(8,128)(2,1)}, u32[]{:S(2)}, u32[]{:S(2)}) %collective-permute-start.34) | collective-permute-done | bytes 1081376 | tf_op jit(solution)/shard_map/ppermute | solution.py:561
  284.3 1.5 add_convert_fusion
  285.9 1.5 collective-permute-start.35
  287.4 1.5 add_convert_fusion.1
  288.9 17.8 %collective-permute-done.28 = bf16[2,1056,256]{2,1,0:T(8,128)(2,1)} collective-permute-done((bf16[2,1056,256]{2,1,0:T(8,128)(2,1)}, bf16[2,1056,256]{2,1,0:T(8,128)(2,1)}, u32[]{:S(2)}, u32[]{:S(2)}) %collective-permute-start.28) | collective-permute-done | bytes 1081376 | tf_op jit(solution)/shard_map/ppermute | solution.py:561
  307.4 1.5 add_convert_fusion.2
  309.0 1.5 collective-permute-start.29
  311.4 17.4 %collective-permute-done.32 = bf16[1056,256]{1,0:T(8,128)(2,1)S(1)} collective-permute-done((bf16[1056,256]{1,0:T(8,128)(2,1)S(1)}, bf16[1056,256]{1,0:T(8,128)(2,1)S(1)}, u32[]{:S(2)}, u32[]{:S(2)}) %collective-permute-start.32) | collective-permute-done | bytes 540704 | tf_op jit(solution)/shard_map/ppermute | solution.py:561
  330.7 4.4 collective-permute-start.30
  335.1 11.3 %attention_back.7 = (bf16[2,512,256]{2,1,0:T(8,128)(2,1)}, bf16[2,512,256]{2,1,0:T(8,128)(2,1)}, bf16[512,384]{1,0:T(8,128)(2,1)}, bf16[512,384]{1,0:T(8,128)(2,1)}) custom-call(s32[3]{0:T(128)} %pad_add_fusion.ids, bf16[512,1024]{1,0:T(8,128)(2,1)} %get-tuple-element.98.g_own, bf16[512,1024]{1,0:T(8,128)(2,1)} %copy-done, ...), custom_call_target="tpu_custom_call" | custom-call | flops 2348810240 | bytes 17563660 | tf_op jit(solution)/shard_map/attention_back/pallas_call | solution.py:52
  346.4 11.4 %attention_back.6 = (bf16[2,512,256]{2,1,0:T(8,128)(2,1)}, bf16[2,512,256]{2,1,0:T(8,128)(2,1)}, bf16[512,384]{1,0:T(8,128)(2,1)}, bf16[512,384]{1,0:T(8,128)(2,1)}) custom-call(s32[3]{0:T(128)} %pad_add_fusion.ids, bf16[512,1024]{1,0:T(8,128)(2,1)} %get-tuple-element.98.g_own, bf16[512,1024]{1,0:T(8,128)(2,1)} %copy-done, ...), custom_call_target="tpu_custom_call" | custom-call | flops 2348810240 | bytes 17563660 | tf_op jit(solution)/shard_map/attention_back/pallas_call | solution.py:52
  357.8 11.5 %attention_back.5 = (bf16[2,512,256]{2,1,0:T(8,128)(2,1)}, bf16[2,512,256]{2,1,0:T(8,128)(2,1)}, bf16[512,384]{1,0:T(8,128)(2,1)}, bf16[512,384]{1,0:T(8,128)(2,1)}) custom-call(s32[3]{0:T(128)} %pad_add_fusion.ids, bf16[512,1024]{1,0:T(8,128)(2,1)} %get-tuple-element.98.g_own, bf16[512,1024]{1,0:T(8,128)(2,1)} %copy-done, ...), custom_call_target="tpu_custom_call" | custom-call | flops 2348810240 | bytes 17563660 | tf_op jit(solution)/shard_map/attention_back/pallas_call | solution.py:52
  369.3 11.5 %attention_back.4 = (bf16[2,512,256]{2,1,0:T(8,128)(2,1)}, bf16[2,512,256]{2,1,0:T(8,128)(2,1)}, bf16[512,384]{1,0:T(8,128)(2,1)}, bf16[512,384]{1,0:T(8,128)(2,1)}) custom-call(s32[3]{0:T(128)} %pad_add_fusion.ids, bf16[512,1024]{1,0:T(8,128)(2,1)} %get-tuple-element.98.g_own, bf16[512,1024]{1,0:T(8,128)(2,1)} %copy-done, ...), custom_call_target="tpu_custom_call" | custom-call | flops 2348810240 | bytes 17563660 | tf_op jit(solution)/shard_map/attention_back/pallas_call | solution.py:52
  380.8 7.9 %in_proj_back.1 = (f32[512,1024]{1,0:T(8,128)}, bf16[512,1024]{1,0:T(8,128)(2,1)}) custom-call(s32[3]{0:T(128)} %pad_add_fusion.ids, bf16[512,384]{1,0:T(8,128)(2,1)} %get-tuple-element.106.refs_0_, bf16[512,384]{1,0:T(8,128)(2,1)} %get-tuple-element.107.refs_1_, bf16[512,384]{1,0:T(8,128)(2,1)} %get-tuple-element.108.refs_2_, ...), custom_call_target="tpu_custom_call" | custom-call | flops 3221225472 | bytes 10485772 | tf_op jit(solution)/shard_map/in_proj_back/pallas_call | solution.py:52
  392.9 1.5 add_convert_fusion.4.refs_0_
  394.4 9.4 %collective-permute-done.16 = bf16[2,512,256]{2,1,0:T(8,128)(2,1)S(1)} collective-permute-done((bf16[2,512,256]{2,1,0:T(8,128)(2,1)}, bf16[2,512,256]{2,1,0:T(8,128)(2,1)S(1)}, u32[]{:S(2)}, u32[]{:S(2)}) %collective-permute-start.16) | collective-permute-done | bytes 524320 | tf_op jit(solution)/shard_map/ppermute | solution.py:561
  406.0 9.1 %collective-permute-done.10 = bf16[2,512,256]{2,1,0:T(8,128)(2,1)S(1)} collective-permute-done((bf16[2,512,256]{2,1,0:T(8,128)(2,1)}, bf16[2,512,256]{2,1,0:T(8,128)(2,1)S(1)}, u32[]{:S(2)}, u32[]{:S(2)}) %collective-permute-start.10) | collective-permute-done | bytes 524320 | tf_op jit(solution)/shard_map/ppermute | solution.py:561
  415.8 1.5 collective-permute-start.17
  418.3 8.3 %collective-permute-done.38.refs_2_ = bf16[1056,256]{1,0:T(8,128)(2,1)S(1)} collective-permute-done((bf16[1056,256]{1,0:T(8,128)(2,1)S(1)}, bf16[1056,256]{1,0:T(8,128)(2,1)S(1)}, u32[]{:S(2)}, u32[]{:S(2)}) %collective-permute-start.38) | collective-permute-done | bytes 540704 | tf_op jit(solution)/shard_map/ppermute | solution.py:561
  427.3 5.6 %collective-permute-done.17 = bf16[512,256]{1,0:T(8,128)(2,1)S(1)} collective-permute-done((bf16[512,256]{1,0:T(8,128)(2,1)S(1)}, bf16[512,256]{1,0:T(8,128)(2,1)S(1)}, u32[]{:S(2)}, u32[]{:S(2)}) %collective-permute-start.17) | collective-permute-done | bytes 262176 | tf_op jit(solution)/shard_map/ppermute | solution.py:561
  435.4 1.8 collective-permute-start.15
  437.2 2.1 collective-permute-done.9
  439.4 3.3 collective-permute-done.18
  442.7 7.8 %collective-permute-start.12 = (bf16[512,256]{1,0:T(8,128)(2,1)S(1)}, bf16[512,256]{1,0:T(8,128)(2,1)}, u32[]{:S(2)}, u32[]{:S(2)}) collective-permute-start(bf16[512,256]{1,0:T(8,128)(2,1)S(1)} %fusion.6), channel_id=1, source_target_pairs={{0,1},{1,0},{2,3},{3,2},{4,5},{5,4},{6,7},{7,6},{8,9},{9,8},{10,11... | collective-permute-start | bytes 786440 | tf_op jit(solution)/shard_map/ppermute | solution.py:561
  450.4 2.7 collective-permute-done.15
  454.8 5.0 norm_one_back.1
  462.0 6.5 %collective-permute-done.2.b1 = bf16[256,1024]{1,0:T(8,128)(2,1)} collective-permute-done((bf16[256,1024]{1,0:T(8,128)(2,1)}, bf16[256,1024]{1,0:T(8,128)(2,1)}, u32[]{:S(2)}, u32[]{:S(2)}) %collective-permute-start.2) | collective-permute-done | bytes 524320 | tf_op jit(solution)/shard_map/ppermute | solution.py:561
  468.5 1.7 collective-permute-start.6
  472.4 8.0 %collective-permute-done.20.refs_2_ = bf16[512,256]{1,0:T(8,128)(2,1)S(1)} collective-permute-done((bf16[512,256]{1,0:T(8,128)(2,1)S(1)}, bf16[512,256]{1,0:T(8,128)(2,1)S(1)}, u32[]{:S(2)}, u32[]{:S(2)}) %collective-permute-start.20) | collective-permute-done | bytes 262176 | tf_op jit(solution)/shard_map/ppermute | solution.py:561
  481.1 2.5 unprep_output.1
  483.9 5.9 %collective-permute-start.24 = (bf16[512,256]{1,0:T(8,128)(2,1)S(1)}, bf16[512,256]{1,0:T(8,128)(2,1)S(1)}, u32[]{:S(2)}, u32[]{:S(2)}) collective-permute-start(bf16[512,256]{1,0:T(8,128)(2,1)S(1)} %collective-permute-done.20.refs_2_), channel_id=1, source_target_pairs={{0,4},{4,0},{1,5},{5,1},{2,6},{6,2},{3,7},{7,3},{8,12},{12,8},{9,1... | collective-permute-start | bytes 786440 | tf_op jit(solution)/shard_map/ppermute | solution.py:561
  490.3 43.7 %psum.7 = f32[2,1024]{1,0:T(2,128)S(1)} all-reduce(f32[2,1024]{1,0:T(2,128)S(1)} %pad_maximum_fusion), channel_id=1, replica_groups=mesh['r'=1,'q'=4,'c'=2,'t'=4] {'r','q','c','t'}, use_global_device_ids=true, to_apply=%region_0.0 | all-reduce | flops 2048 | bytes 16384 | tf_op jit(solution)/shard_map/psum | solution.py:689
  534.6 2.3 unprep_grad.1
  537.8 6.2 %place_b.1 = (f32[704,1024]{1,0:T(8,128)}, f32[704,1024]{1,0:T(8,128)}, f32[704,1024]{1,0:T(8,128)}) custom-call(s32[3]{0:T(128)} %pad_add_fusion.ids, bf16[1056,256]{1,0:T(8,128)(2,1)} %copy-done.1, bf16[1056,256]{1,0:T(8,128)(2,1)} %copy-done.11, bf16[1056,256]{1,0:T(8,128)(2,1)} %copy-done.10, bf16[1056,256]{1,0:T(8,128)(2,1)} %copy-done.12, ...), custom_call_target="tpu_custom_call" | custom-call | bytes 12976140 | tf_op jit(solution)/shard_map/place_b/pallas_call | solution.py:52
  544.9 4.0 place_a.1
  (147 shorter events, 32.9 us)
Async XLA Ops:
  197.6 72.4 %collective-permute-start.26 = (bf16[2,1056,256]{2,1,0:T(8,128)(2,1)}, bf16[2,1056,256]{2,1,0:T(8,128)(2,1)}, u32[]{:S(2)}, u32[]{:S(2)}) collective-permute-start(bf16[2,1056,256]{2,1,0:T(8,128)(2,1)} %get-tuple-element.133), channel_id=1, source_target_pairs={{0,8},{8,0},{16,24},{24,16},{1,9},{9,1},{17,25},{25,17},{2,10},{10... | collective-permute-start | bytes 3244040 | tf_op jit(solution)/shard_map/ppermute | solution.py:561
  245.8 12.9 %collective-permute-start.3 = (bf16[512,1024]{1,0:T(8,128)(2,1)}, bf16[512,1024]{1,0:T(8,128)(2,1)S(1)}, u32[]{:S(2)}, u32[]{:S(2)}) collective-permute-start(bf16[512,1024]{1,0:T(8,128)(2,1)} %get-tuple-element.97), channel_id=1, source_target_pairs={{0,4},{4,0},{1,5},{5,1},{2,6},{6,2},{3,7},{7,3},{8,12},{12,8},{9,1... | collective-permute-start | bytes 3145736 | tf_op jit(solution)/shard_map/ppermute | solution.py:561
  256.0 9.2 %collective-permute-start = (bf16[512,1024]{1,0:T(8,128)(2,1)}, bf16[512,1024]{1,0:T(8,128)(2,1)S(1)}, u32[]{:S(2)}, u32[]{:S(2)}) collective-permute-start(bf16[512,1024]{1,0:T(8,128)(2,1)} %get-tuple-element.89), channel_id=1, source_target_pairs={{0,4},{4,0},{1,5},{5,1},{2,6},{6,2},{3,7},{7,3},{8,12},{12,8},{9,1... | collective-permute-start | bytes 3145736 | tf_op jit(solution)/shard_map/ppermute | solution.py:561
  256.5 27.1 %collective-permute-start.34 = (bf16[2,1056,256]{2,1,0:T(8,128)(2,1)}, bf16[2,1056,256]{2,1,0:T(8,128)(2,1)}, u32[]{:S(2)}, u32[]{:S(2)}) collective-permute-start(bf16[2,1056,256]{2,1,0:T(8,128)(2,1)} %get-tuple-element.139), channel_id=1, source_target_pairs={{0,16},{8,24},{16,0},{24,8},{1,17},{9,25},{17,1},{25,9},{2,18},{10... | collective-permute-start | bytes 3244040 | tf_op jit(solution)/shard_map/ppermute | solution.py:561
  257.2 28.6 %collective-permute-start.31 = (bf16[2,1056,256]{2,1,0:T(8,128)(2,1)}, bf16[2,1056,256]{2,1,0:T(8,128)(2,1)}, u32[]{:S(2)}, u32[]{:S(2)}) collective-permute-start(bf16[2,1056,256]{2,1,0:T(8,128)(2,1)} %get-tuple-element.137), channel_id=1, source_target_pairs={{0,8},{8,0},{16,24},{24,16},{1,9},{9,1},{17,25},{25,17},{2,10},{10... | collective-permute-start | bytes 3244040 | tf_op jit(solution)/shard_map/ppermute | solution.py:561
  258.6 48.1 %collective-permute-start.28 = (bf16[2,1056,256]{2,1,0:T(8,128)(2,1)}, bf16[2,1056,256]{2,1,0:T(8,128)(2,1)}, u32[]{:S(2)}, u32[]{:S(2)}) collective-permute-start(bf16[2,1056,256]{2,1,0:T(8,128)(2,1)} %get-tuple-element.135), channel_id=1, source_target_pairs={{0,16},{8,24},{16,0},{24,8},{1,17},{9,25},{17,1},{25,9},{2,18},{10... | collective-permute-start | bytes 3244040 | tf_op jit(solution)/shard_map/ppermute | solution.py:561
  265.2 65.5 %collective-permute-start.4 = (bf16[512,1024]{1,0:T(8,128)(2,1)}, bf16[512,1024]{1,0:T(8,128)(2,1)S(1)}, u32[]{:S(2)}, u32[]{:S(2)}) collective-permute-start(bf16[512,1024]{1,0:T(8,128)(2,1)} %get-tuple-element.98.g_own), channel_id=1, source_target_pairs={{0,4},{4,0},{1,5},{5,1},{2,6},{6,2},{3,7},{7,3},{8,12},{12,8},{9,1... | collective-permute-start | bytes 3145736 | tf_op jit(solution)/shard_map/ppermute | solution.py:561
  269.9 147.6 %collective-permute-start.1 = (bf16[256,1024]{1,0:T(8,128)(2,1)}, bf16[256,1024]{1,0:T(8,128)(2,1)}, u32[]{:S(2)}, u32[]{:S(2)}) collective-permute-start(bf16[256,1024]{1,0:T(8,128)(2,1)} %get-tuple-element.90), channel_id=1, source_target_pairs={{0,0},{1,1},{4,2},{5,3},{2,4},{3,5},{6,6},{7,7},{8,8},{9,9},{12,10... | collective-permute-start | bytes 1572872 | tf_op jit(solution)/shard_map/ppermute | solution.py:561
  283.6 105.2 %collective-permute-start.27 = (bf16[1056,256]{1,0:T(8,128)(2,1)}, bf16[1056,256]{1,0:T(8,128)(2,1)S(1)}, u32[]{:S(2)}, u32[]{:S(2)}) collective-permute-start(bf16[1056,256]{1,0:T(8,128)(2,1)} %slice_bitcast_fusion.9), channel_id=1, source_target_pairs={{0,16},{8,24},{16,0},{24,8},{1,17},{9,25},{17,1},{25,9},{2,18},{10... | collective-permute-start | bytes 1622024 | tf_op jit(solution)/shard_map/ppermute | solution.py:561
  285.9 23.2 %collective-permute-start.35 = (bf16[1056,256]{1,0:T(8,128)(2,1)S(1)}, bf16[1056,256]{1,0:T(8,128)(2,1)S(1)}, u32[]{:S(2)}, u32[]{:S(2)}) collective-permute-start(bf16[1056,256]{1,0:T(8,128)(2,1)S(1)} %slice_bitcast_fusion.3), channel_id=1, source_target_pairs={{0,8},{8,0},{16,24},{24,16},{1,9},{9,1},{17,25},{25,17},{2,10},{10... | collective-permute-start | bytes 1622024 | tf_op jit(solution)/shard_map/ppermute | solution.py:561
  306.7 22.1 %collective-permute-start.32 = (bf16[1056,256]{1,0:T(8,128)(2,1)S(1)}, bf16[1056,256]{1,0:T(8,128)(2,1)S(1)}, u32[]{:S(2)}, u32[]{:S(2)}) collective-permute-start(bf16[1056,256]{1,0:T(8,128)(2,1)S(1)} %slice_bitcast_fusion.5), channel_id=1, source_target_pairs={{0,16},{8,24},{16,0},{24,8},{1,17},{9,25},{17,1},{25,9},{2,18},{10... | collective-permute-start | bytes 1622024 | tf_op jit(solution)/shard_map/ppermute | solution.py:561
  309.0 20.8 %collective-permute-start.29 = (bf16[1056,256]{1,0:T(8,128)(2,1)S(1)}, bf16[1056,256]{1,0:T(8,128)(2,1)S(1)}, u32[]{:S(2)}, u32[]{:S(2)}) collective-permute-start(bf16[1056,256]{1,0:T(8,128)(2,1)S(1)} %slice_bitcast_fusion.7), channel_id=1, source_target_pairs={{0,8},{8,0},{16,24},{24,16},{1,9},{9,1},{17,25},{25,17},{2,10},{10... | collective-permute-start | bytes 1622024 | tf_op jit(solution)/shard_map/ppermute | solution.py:561
  328.8 60.7 %collective-permute-start.36 = (bf16[1056,256]{1,0:T(8,128)(2,1)}, bf16[1056,256]{1,0:T(8,128)(2,1)S(1)}, u32[]{:S(2)}, u32[]{:S(2)}) collective-permute-start(bf16[1056,256]{1,0:T(8,128)(2,1)} %fusion), channel_id=1, source_target_pairs={{0,3},{1,2},{2,1},{3,0},{4,7},{5,6},{6,5},{7,4},{8,11},{9,10},{10,... | collective-permute-start | bytes 1622024 | tf_op jit(solution)/shard_map/ppermute | solution.py:561
  329.8 61.2 %collective-permute-start.33 = (bf16[1056,256]{1,0:T(8,128)(2,1)}, bf16[1056,256]{1,0:T(8,128)(2,1)}, u32[]{:S(2)}, u32[]{:S(2)}) collective-permute-start(bf16[1056,256]{1,0:T(8,128)(2,1)} %fusion.1), channel_id=1, source_target_pairs={{0,2},{1,3},{2,0},{3,1},{4,6},{5,7},{6,4},{7,5},{8,10},{9,11},{10,... | collective-permute-start | bytes 1622024 | tf_op jit(solution)/shard_map/ppermute | solution.py:561
  330.7 60.7 %collective-permute-start.30 = (bf16[1056,256]{1,0:T(8,128)(2,1)}, bf16[1056,256]{1,0:T(8,128)(2,1)}, u32[]{:S(2)}, u32[]{:S(2)}) collective-permute-start(bf16[1056,256]{1,0:T(8,128)(2,1)} %fusion.2), channel_id=1, source_target_pairs={{0,1},{1,0},{2,3},{3,2},{4,5},{5,4},{6,7},{7,6},{8,9},{9,8},{10,11... | collective-permute-start | bytes 1622024 | tf_op jit(solution)/shard_map/ppermute | solution.py:561
  388.8 15.1 %collective-permute-start.16 = (bf16[2,512,256]{2,1,0:T(8,128)(2,1)}, bf16[2,512,256]{2,1,0:T(8,128)(2,1)S(1)}, u32[]{:S(2)}, u32[]{:S(2)}) collective-permute-start(bf16[2,512,256]{2,1,0:T(8,128)(2,1)} %get-tuple-element.127), channel_id=1, source_target_pairs={{0,16},{8,24},{16,0},{24,8},{1,17},{9,25},{17,1},{25,9},{2,18},{10... | collective-permute-start | bytes 1572872 | tf_op jit(solution)/shard_map/ppermute | solution.py:561
  389.5 15.0 %collective-permute-start.13 = (bf16[2,512,256]{2,1,0:T(8,128)(2,1)}, bf16[2,512,256]{2,1,0:T(8,128)(2,1)S(1)}, u32[]{:S(2)}, u32[]{:S(2)}) collective-permute-start(bf16[2,512,256]{2,1,0:T(8,128)(2,1)} %get-tuple-element.125), channel_id=1, source_target_pairs={{0,8},{8,0},{16,24},{24,16},{1,9},{9,1},{17,25},{25,17},{2,10},{10... | collective-permute-start | bytes 1572872 | tf_op jit(solution)/shard_map/ppermute | solution.py:561
  391.0 24.1 %collective-permute-start.10 = (bf16[2,512,256]{2,1,0:T(8,128)(2,1)}, bf16[2,512,256]{2,1,0:T(8,128)(2,1)S(1)}, u32[]{:S(2)}, u32[]{:S(2)}) collective-permute-start(bf16[2,512,256]{2,1,0:T(8,128)(2,1)} %get-tuple-element.123), channel_id=1, source_target_pairs={{0,16},{8,24},{16,0},{24,8},{1,17},{9,25},{17,1},{25,9},{2,18},{10... | collective-permute-start | bytes 1572872 | tf_op jit(solution)/shard_map/ppermute | solution.py:561
  391.5 24.4 %collective-permute-start.8 = (bf16[2,512,256]{2,1,0:T(8,128)(2,1)}, bf16[2,512,256]{2,1,0:T(8,128)(2,1)S(1)}, u32[]{:S(2)}, u32[]{:S(2)}) collective-permute-start(bf16[2,512,256]{2,1,0:T(8,128)(2,1)} %get-tuple-element.121), channel_id=1, source_target_pairs={{0,8},{8,0},{16,24},{24,16},{1,9},{9,1},{17,25},{25,17},{2,10},{10... | collective-permute-start | bytes 1572872 | tf_op jit(solution)/shard_map/ppermute | solution.py:561
  403.8 49.6 %collective-permute-start.5 = (bf16[512,1024]{1,0:T(8,128)(2,1)S(1)}, bf16[512,1024]{1,0:T(8,128)(2,1)S(1)}, u32[]{:S(2)}, u32[]{:S(2)}) collective-permute-start(bf16[512,1024]{1,0:T(8,128)(2,1)S(1)} %copy-done.28), channel_id=1, source_target_pairs={{0,4},{4,0},{1,5},{5,1},{2,6},{6,2},{3,7},{7,3},{8,12},{12,8},{9,1... | collective-permute-start | bytes 3145736 | tf_op jit(solution)/shard_map/ppermute | solution.py:561
  404.5 22.1 %collective-permute-start.38 = (bf16[1056,256]{1,0:T(8,128)(2,1)S(1)}, bf16[1056,256]{1,0:T(8,128)(2,1)S(1)}, u32[]{:S(2)}, u32[]{:S(2)}) collective-permute-start(bf16[1056,256]{1,0:T(8,128)(2,1)S(1)} %add_convert_fusion.4.refs_0_), channel_id=1, source_target_pairs={{0,16},{8,24},{16,0},{24,8},{1,17},{9,25},{17,1},{25,9},{2,18},{10... | collective-permute-start | bytes 1622024 | tf_op jit(solution)/shard_map/ppermute | solution.py:561
  415.1 20.3 %collective-permute-start.37 = (bf16[1056,256]{1,0:T(8,128)(2,1)S(1)}, bf16[1056,256]{1,0:T(8,128)(2,1)S(1)}, u32[]{:S(2)}, u32[]{:S(2)}) collective-permute-start(bf16[1056,256]{1,0:T(8,128)(2,1)S(1)} %add_convert_fusion.4.refs_0_), channel_id=1, source_target_pairs={{0,8},{8,0},{16,24},{24,16},{1,9},{9,1},{17,25},{25,17},{2,10},{10... | collective-permute-start | bytes 1622024 | tf_op jit(solution)/shard_map/ppermute | solution.py:561
  415.8 17.0 %collective-permute-start.17 = (bf16[512,256]{1,0:T(8,128)(2,1)S(1)}, bf16[512,256]{1,0:T(8,128)(2,1)S(1)}, u32[]{:S(2)}, u32[]{:S(2)}) collective-permute-start(bf16[512,256]{1,0:T(8,128)(2,1)S(1)} %slice_bitcast_fusion.11), channel_id=1, source_target_pairs={{0,8},{8,0},{16,24},{24,16},{1,9},{9,1},{17,25},{25,17},{2,10},{10... | collective-permute-start | bytes 786440 | tf_op jit(solution)/shard_map/ppermute | solution.py:561
  417.5 16.7 %collective-permute-start.14 = (bf16[512,256]{1,0:T(8,128)(2,1)S(1)}, bf16[512,256]{1,0:T(8,128)(2,1)S(1)}, u32[]{:S(2)}, u32[]{:S(2)}) collective-permute-start(bf16[512,256]{1,0:T(8,128)(2,1)S(1)} %slice_bitcast_fusion.13), channel_id=1, source_target_pairs={{0,16},{8,24},{16,0},{24,8},{1,17},{9,25},{17,1},{25,9},{2,18},{10... | collective-permute-start | bytes 786440 | tf_op jit(solution)/shard_map/ppermute | solution.py:561
  426.6 10.5 %collective-permute-start.11 = (bf16[512,256]{1,0:T(8,128)(2,1)S(1)}, bf16[512,256]{1,0:T(8,128)(2,1)S(1)}, u32[]{:S(2)}, u32[]{:S(2)}) collective-permute-start(bf16[512,256]{1,0:T(8,128)(2,1)S(1)} %slice_bitcast_fusion.15), channel_id=1, source_target_pairs={{0,8},{8,0},{16,24},{24,16},{1,9},{9,1},{17,25},{25,17},{2,10},{10... | collective-permute-start | bytes 786440 | tf_op jit(solution)/shard_map/ppermute | solution.py:561
  432.8 6.5 %collective-permute-start.9 = (bf16[512,256]{1,0:T(8,128)(2,1)S(1)}, bf16[512,256]{1,0:T(8,128)(2,1)}, u32[]{:S(2)}, u32[]{:S(2)}) collective-permute-start(bf16[512,256]{1,0:T(8,128)(2,1)S(1)} %slice_bitcast_fusion.17), channel_id=1, source_target_pairs={{0,16},{8,24},{16,0},{24,8},{1,17},{9,25},{17,1},{25,9},{2,18},{10... | collective-permute-start | bytes 786440 | tf_op jit(solution)/shard_map/ppermute | solution.py:561
  434.2 8.4 %collective-permute-start.18 = (bf16[512,256]{1,0:T(8,128)(2,1)S(1)}, bf16[512,256]{1,0:T(8,128)(2,1)}, u32[]{:S(2)}, u32[]{:S(2)}) collective-permute-start(bf16[512,256]{1,0:T(8,128)(2,1)S(1)} %fusion.4), channel_id=1, source_target_pairs={{0,3},{1,2},{2,1},{3,0},{4,7},{5,6},{6,5},{7,4},{8,11},{9,10},{10,... | collective-permute-start | bytes 786440 | tf_op jit(solution)/shard_map/ppermute | solution.py:561
  435.4 17.8 %collective-permute-start.15 = (bf16[512,256]{1,0:T(8,128)(2,1)S(1)}, bf16[512,256]{1,0:T(8,128)(2,1)S(1)}, u32[]{:S(2)}, u32[]{:S(2)}) collective-permute-start(bf16[512,256]{1,0:T(8,128)(2,1)S(1)} %fusion.5), channel_id=1, source_target_pairs={{0,2},{1,3},{2,0},{3,1},{4,6},{5,7},{6,4},{7,5},{8,10},{9,11},{10,... | collective-permute-start | bytes 786440 | tf_op jit(solution)/shard_map/ppermute | solution.py:561
  437.2 33.0 %collective-permute-start.40 = (bf16[1056,256]{1,0:T(8,128)(2,1)S(1)}, bf16[1056,256]{1,0:T(8,128)(2,1)}, u32[]{:S(2)}, u32[]{:S(2)}) collective-permute-start(bf16[1056,256]{1,0:T(8,128)(2,1)S(1)} %add_convert_fusion.4.refs_0_), channel_id=1, source_target_pairs={{0,4},{4,0},{1,5},{5,1},{2,6},{6,2},{3,7},{7,3},{8,12},{12,8},{9,1... | collective-permute-start | bytes 1622024 | tf_op jit(solution)/shard_map/ppermute | solution.py:561
  439.3 30.9 %collective-permute-start.42 = (bf16[1056,256]{1,0:T(8,128)(2,1)S(1)}, bf16[1056,256]{1,0:T(8,128)(2,1)}, u32[]{:S(2)}, u32[]{:S(2)}) collective-permute-start(bf16[1056,256]{1,0:T(8,128)(2,1)S(1)} %collective-permute-done.38.refs_2_), channel_id=1, source_target_pairs={{0,4},{4,0},{1,5},{5,1},{2,6},{6,2},{3,7},{7,3},{8,12},{12,8},{9,1... | collective-permute-start | bytes 1622024 | tf_op jit(solution)/shard_map/ppermute | solution.py:561
  442.7 17.1 %collective-permute-start.12 = (bf16[512,256]{1,0:T(8,128)(2,1)S(1)}, bf16[512,256]{1,0:T(8,128)(2,1)}, u32[]{:S(2)}, u32[]{:S(2)}) collective-permute-start(bf16[512,256]{1,0:T(8,128)(2,1)S(1)} %fusion.6), channel_id=1, source_target_pairs={{0,1},{1,0},{2,3},{3,2},{4,5},{5,4},{6,7},{7,6},{8,9},{9,8},{10,11... | collective-permute-start | bytes 786440 | tf_op jit(solution)/shard_map/ppermute | solution.py:561
  453.2 15.4 %collective-permute-start.2 = (bf16[256,1024]{1,0:T(8,128)(2,1)}, bf16[256,1024]{1,0:T(8,128)(2,1)}, u32[]{:S(2)}, u32[]{:S(2)}) collective-permute-start(bf16[256,1024]{1,0:T(8,128)(2,1)} %get-tuple-element.91), channel_id=1, source_target_pairs={{1,0},{0,1},{5,2},{4,3},{3,4},{2,5},{7,6},{6,7},{9,8},{8,9},{13,10... | collective-permute-start | bytes 1572872 | tf_op jit(solution)/shard_map/ppermute | solution.py:561
  453.9 17.1 %collective-permute-start.41 = (bf16[1056,256]{1,0:T(8,128)(2,1)S(1)}, bf16[1056,256]{1,0:T(8,128)(2,1)}, u32[]{:S(2)}, u32[]{:S(2)}) collective-permute-start(bf16[1056,256]{1,0:T(8,128)(2,1)S(1)} %collective-permute-done.37.refs_1_), channel_id=1, source_target_pairs={{0,4},{4,0},{1,5},{5,1},{2,6},{6,2},{3,7},{7,3},{8,12},{12,8},{9,1... | collective-permute-start | bytes 1622024 | tf_op jit(solution)/shard_map/ppermute | solution.py:561
  459.8 21.2 %collective-permute-start.39 = (bf16[1056,256]{1,0:T(8,128)(2,1)S(1)}, bf16[1056,256]{1,0:T(8,128)(2,1)S(1)}, u32[]{:S(2)}, u32[]{:S(2)}) collective-permute-start(bf16[1056,256]{1,0:T(8,128)(2,1)S(1)} %collective-permute-done.37.refs_1_), channel_id=1, source_target_pairs={{0,16},{8,24},{16,0},{24,8},{1,17},{9,25},{17,1},{25,9},{2,18},{10... | collective-permute-start | bytes 1622024 | tf_op jit(solution)/shard_map/ppermute | solution.py:561
  461.9 75.0 %copy-start.6 = (bf16[512,256]{1,0:T(8,128)(2,1)}, bf16[512,256]{1,0:T(8,128)(2,1)S(1)}, u32[]{:S(2)}) copy-start(bf16[512,256]{1,0:T(8,128)(2,1)S(1)} %add_convert_fusion.9.refs_0_) | copy-start | bytes 786436
  468.5 15.4 %collective-permute-start.6 = (bf16[256,1024]{1,0:T(8,128)(2,1)}, bf16[256,1024]{1,0:T(8,128)(2,1)S(1)}, u32[]{:S(2)}, u32[]{:S(2)}) collective-permute-start(bf16[256,1024]{1,0:T(8,128)(2,1)} %get-tuple-element.118), channel_id=1, source_target_pairs={{0,0},{1,1},{4,2},{5,3},{2,4},{3,5},{6,6},{7,7},{8,8},{9,9},{12,10... | collective-permute-start | bytes 1572872 | tf_op jit(solution)/shard_map/ppermute | solution.py:561
  470.2 19.6 %collective-permute-start.7 = (bf16[256,1024]{1,0:T(8,128)(2,1)}, bf16[256,1024]{1,0:T(8,128)(2,1)}, u32[]{:S(2)}, u32[]{:S(2)}) collective-permute-start(bf16[256,1024]{1,0:T(8,128)(2,1)} %get-tuple-element.119), channel_id=1, source_target_pairs={{1,0},{0,1},{5,2},{4,3},{3,4},{2,5},{7,6},{6,7},{9,8},{8,9},{13,10... | collective-permute-start | bytes 1572872 | tf_op jit(solution)/shard_map/ppermute | solution.py:561
  470.2 10.2 %collective-permute-start.20 = (bf16[512,256]{1,0:T(8,128)(2,1)S(1)}, bf16[512,256]{1,0:T(8,128)(2,1)S(1)}, u32[]{:S(2)}, u32[]{:S(2)}) collective-permute-start(bf16[512,256]{1,0:T(8,128)(2,1)S(1)} %add_convert_fusion.9.refs_0_), channel_id=1, source_target_pairs={{0,16},{8,24},{16,0},{24,8},{1,17},{9,25},{17,1},{25,9},{2,18},{10... | collective-permute-start | bytes 786440 | tf_op jit(solution)/shard_map/ppermute | solution.py:561
  471.0 12.6 %collective-permute-start.19 = (bf16[512,256]{1,0:T(8,128)(2,1)S(1)}, bf16[512,256]{1,0:T(8,128)(2,1)S(1)}, u32[]{:S(2)}, u32[]{:S(2)}) collective-permute-start(bf16[512,256]{1,0:T(8,128)(2,1)S(1)} %add_convert_fusion.9.refs_0_), channel_id=1, source_target_pairs={{0,8},{8,0},{16,24},{24,16},{1,9},{9,1},{17,25},{25,17},{2,10},{10... | collective-permute-start | bytes 786440 | tf_op jit(solution)/shard_map/ppermute | solution.py:561
  480.4 56.6 %copy-start.19 = (bf16[512,256]{1,0:T(8,128)(2,1)}, bf16[512,256]{1,0:T(8,128)(2,1)S(1)}, u32[]{:S(2)}) copy-start(bf16[512,256]{1,0:T(8,128)(2,1)S(1)} %collective-permute-done.20.refs_2_) | copy-start | bytes 786436
  480.4 9.5 %collective-permute-start.21 = (bf16[512,256]{1,0:T(8,128)(2,1)S(1)}, bf16[512,256]{1,0:T(8,128)(2,1)S(1)}, u32[]{:S(2)}, u32[]{:S(2)}) collective-permute-start(bf16[512,256]{1,0:T(8,128)(2,1)S(1)} %collective-permute-done.20.refs_2_), channel_id=1, source_target_pairs={{0,8},{8,0},{16,24},{24,16},{1,9},{9,1},{17,25},{25,17},{2,10},{10... | collective-permute-start | bytes 786440 | tf_op jit(solution)/shard_map/ppermute | solution.py:561
  481.0 55.9 %copy-start.12 = (bf16[1056,256]{1,0:T(8,128)(2,1)}, bf16[1056,256]{1,0:T(8,128)(2,1)S(1)}, u32[]{:S(2)}) copy-start(bf16[1056,256]{1,0:T(8,128)(2,1)S(1)} %collective-permute-done.39.refs_3_) | copy-start | bytes 1622020
  481.0 55.9 %collective-permute-start.43 = (bf16[1056,256]{1,0:T(8,128)(2,1)S(1)}, bf16[1056,256]{1,0:T(8,128)(2,1)S(1)}, u32[]{:S(2)}, u32[]{:S(2)}) collective-permute-start(bf16[1056,256]{1,0:T(8,128)(2,1)S(1)} %collective-permute-done.39.refs_3_), channel_id=1, source_target_pairs={{0,4},{4,0},{1,5},{5,1},{2,6},{6,2},{3,7},{7,3},{8,12},{12,8},{9,1... | collective-permute-start | bytes 1622024 | tf_op jit(solution)/shard_map/ppermute | solution.py:561
  483.6 60.5 %copy-start.20 = (bf16[512,256]{1,0:T(8,128)(2,1)}, bf16[512,256]{1,0:T(8,128)(2,1)S(1)}, u32[]{:S(2)}) copy-start(bf16[512,256]{1,0:T(8,128)(2,1)S(1)} %collective-permute-done.19.refs_1_) | copy-start | bytes 786436
  483.6 60.5 %collective-permute-start.22 = (bf16[512,256]{1,0:T(8,128)(2,1)S(1)}, bf16[512,256]{1,0:T(8,128)(2,1)S(1)}, u32[]{:S(2)}, u32[]{:S(2)}) collective-permute-start(bf16[512,256]{1,0:T(8,128)(2,1)S(1)} %add_convert_fusion.9.refs_0_), channel_id=1, source_target_pairs={{0,4},{4,0},{1,5},{5,1},{2,6},{6,2},{3,7},{7,3},{8,12},{12,8},{9,1... | collective-permute-start | bytes 786440 | tf_op jit(solution)/shard_map/ppermute | solution.py:561
  483.9 60.2 %collective-permute-start.24 = (bf16[512,256]{1,0:T(8,128)(2,1)S(1)}, bf16[512,256]{1,0:T(8,128)(2,1)S(1)}, u32[]{:S(2)}, u32[]{:S(2)}) collective-permute-start(bf16[512,256]{1,0:T(8,128)(2,1)S(1)} %collective-permute-done.20.refs_2_), channel_id=1, source_target_pairs={{0,4},{4,0},{1,5},{5,1},{2,6},{6,2},{3,7},{7,3},{8,12},{12,8},{9,1... | collective-permute-start | bytes 786440 | tf_op jit(solution)/shard_map/ppermute | solution.py:561
  489.8 54.3 %collective-permute-start.23 = (bf16[512,256]{1,0:T(8,128)(2,1)S(1)}, bf16[512,256]{1,0:T(8,128)(2,1)S(1)}, u32[]{:S(2)}, u32[]{:S(2)}) collective-permute-start(bf16[512,256]{1,0:T(8,128)(2,1)S(1)} %collective-permute-done.19.refs_1_), channel_id=1, source_target_pairs={{0,4},{4,0},{1,5},{5,1},{2,6},{6,2},{3,7},{7,3},{8,12},{12,8},{9,1... | collective-permute-start | bytes 786440 | tf_op jit(solution)/shard_map/ppermute | solution.py:561
  489.9 54.2 %collective-permute-start.25 = (bf16[512,256]{1,0:T(8,128)(2,1)S(1)}, bf16[512,256]{1,0:T(8,128)(2,1)}, u32[]{:S(2)}, u32[]{:S(2)}) collective-permute-start(bf16[512,256]{1,0:T(8,128)(2,1)S(1)} %collective-permute-done.21.refs_3_), channel_id=1, source_target_pairs={{0,4},{4,0},{1,5},{5,1},{2,6},{6,2},{3,7},{7,3},{8,12},{12,8},{9,1... | collective-permute-start | bytes 786440 | tf_op jit(solution)/shard_map/ppermute | solution.py:561
  (25 other events, 348.7 us)
